TPU v7x, 256 devices: a whole 4x4x8 slice. The times are simulated.
256 devices in a mesh: dom: 64 (over z, x_lo, y), dir: 4 (over x_hi, core).
Axes of the slice: x: 4 (x_hi: 2, x_lo: 2; x = x_hi * 2 + x_lo), y: 4, z: 8, core: 2. Of those that a mesh axis runs over, the one named last changes fastest.
Arguments:
- action: float32 [64, 32, 32768], P('dir', None, 'dom'), may hold values from -6 to 6
- edge_angle: float32 [6, 32768], P(None, 'dom'), may hold values from -3.140625 to 3.140625
- edge_speed: float32 [6, 32768], P(None, 'dom'), may hold values from 0.3 to 3
- neighbours: int32 [6, 32768], P(None, 'dom'), may hold values from 0 to 575, as said below
- send_rows: int32 [2, 2048], P(None, 'dom'), may hold values from 0 to 511, as said below
- refract_rate: float32 [32, 32768], P(None, 'dom'), may hold values from -0.45 to 0.45
- refract_angle: float32 [32768], P('dom'), may hold values from -3.140625 to 3.140625
- shift_rate: float32 [32, 32768], P(None, 'dom'), may hold values from -0.45 to 0.45
Outputs:
- wave_action: float32 [64, 32, 32768], P('dir', None, 'dom')
Inputs may be any that keep to these rules, and one draw needn't show every extreme that they name: `neighbours`: slots below 512 are the partition's own nodes, then 32 slots from the lower and 32 from the upper neighbouring partition. `send_rows`: local node numbers within the sending partition.
All inputs are finite; a program needn't handle non-finite values.
Results may differ from a plain program's by a relative error of at most 0.00002.
Values sent between devices are 32-bit elements; how exact they have to be, the bound alone decides.
No kernel may reach another device: no remote copies, remote signals or barrier semaphores. Data moves between devices by JAX's collectives and lax.ppermute only.
A program may use at most 64 MiB of HBM per device.

v0:
```python
import math

import jax
import jax.numpy as jnp
from jax import lax
from jax.sharding import PartitionSpec as P

NDIR = 64
NEIGH = 6
SWEEPS = 3


def passed_along(array, axis, by):
    count = lax.axis_size(axis)
    pairs = [(i, i + by) for i in range(count) if 0 <= i + by < count]
    return lax.ppermute(array, axis, pairs)


def extended_2(array, sides, width):
    for axis, dim in sides:
        count, length = (lax.axis_size(axis), array.shape[dim])
        up = [(i, (i + 1) % count) for i in range(count)]
        down = [(j, i) for i, j in up]
        last = lax.slice_in_dim(array, length - width, length, axis=dim)
        first = lax.slice_in_dim(array, 0, width, axis=dim)
        before = lax.ppermute(last, axis, up)
        after = lax.ppermute(first, axis, down)
        array = jnp.concatenate([before, array, after], axis=dim)
    return array


def upwind_freq(refracted, shift_rate):
    padded = jnp.pad(refracted, ((0, 0), (1, 1), (0, 0)))
    rate = shift_rate[None, :, :]
    return refracted - (
        jax.nn.relu(rate) * (refracted - padded[:, :-2, :])
        + jnp.minimum(rate, 0.0) * (padded[:, 2:, :] - refracted)
    )


def shards(
    action, edge_angle, edge_speed, neighbours, send_rows, refract_rate, refract_angle, shift_rate
):
    sector = action.shape[0]
    freq_count = action.shape[1]
    node_count = action.shape[2]
    columns = sector * freq_count
    first_dir = lax.axis_index("dir") * sector
    angles = (
        2.0 * math.pi * (first_dir + jnp.arange(sector, dtype=jnp.int32)).astype(jnp.float32) / NDIR
    )
    weight_nodes = edge_speed[:, :, None] * jax.nn.relu(
        jnp.cos(angles[None, None, :] - edge_angle[:, :, None])
    )
    denom_nodes = 1.0 + jnp.sum(weight_nodes, axis=0)
    weight_wide = jnp.repeat(weight_nodes, freq_count, axis=2)
    denom_wide = jnp.repeat(denom_nodes, freq_count, axis=1)
    start_rows = action.reshape(columns, node_count).T
    field = start_rows
    for sweep in range(SWEEPS):
        down_part = jnp.take(field, send_rows[0], axis=0)
        up_part = jnp.take(field, send_rows[1], axis=0)
        lower_rows = passed_along(up_part, "dom", 1)
        upper_rows = passed_along(down_part, "dom", -1)
        extended = jnp.concatenate([field, lower_rows, upper_rows], axis=0)
        total = start_rows
        for slot in range(NEIGH):
            total = total + weight_wide[slot] * jnp.take(extended, neighbours[slot], axis=0)
        field = total / denom_wide
    swept = field.T.reshape(sector, freq_count, node_count)
    speed = refract_rate[None, :, :] * jnp.sin(angles[:, None, None] - refract_angle[None, None, :])
    padded = extended_2(swept, (("dir", 0),), 1)
    refracted = swept - (
        jax.nn.relu(speed) * (swept - padded[:-2]) + jnp.minimum(speed, 0.0) * (padded[2:] - swept)
    )
    return upwind_freq(refracted, shift_rate)


def solution(mesh):
    return jax.shard_map(
        shards,
        mesh=mesh,
        in_specs=(
            P("dir", None, "dom"),
            P(None, "dom"),
            P(None, "dom"),
            P(None, "dom"),
            P(None, "dom"),
            P(None, "dom"),
            P("dom"),
            P(None, "dom"),
        ),
        out_specs=P("dir", None, "dom"),
        check_vma=False,
    )
```

profile of v0, /device:TPU:127, one launch (start us, length us, event | category | flops | bytes accessed | tf_op | source)
XLA Modules:
  0.0 131.1 jit_solution(14308016864176415732)
XLA Ops:
  2.4 4.7 %collective-permute-start = (f32[32,512]{1,0:T(8,128)S(1)}, f32[32,512]{1,0:T(8,128)S(1)}, u32[]{:S(2)}, u32[]{:S(2)}) collective-permute-start(f32[32,512]{1,0:T(8,128)S(1)} %broadcast_select_fusion.5), channel_id=1, source_target_pairs={{0,4},{4,8},{8,12},{12,16},{16,20},{20,24},{24,28},{28,32},{32,36}... | collective-permute-start | bytes 196616 | tf_op jit(solution)/shard_map/ppermute | solution.py:16
  8.4 1.9 %collective-permute-start.1 = (f32[32,512]{1,0:T(8,128)}, f32[32,512]{1,0:T(8,128)S(1)}, u32[]{:S(2)}, u32[]{:S(2)}) collective-permute-start(f32[32,512]{1,0:T(8,128)} %broadcast_select_fusion.4), channel_id=1, source_target_pairs={{4,0},{8,4},{12,8},{16,12},{20,16},{24,20},{28,24},{32,28},{36,32}... | collective-permute-start | bytes 196616 | tf_op jit(solution)/shard_map/ppermute | solution.py:16
  23.4 2.3 %gather_fusion.2 = f32[512,512]{1,0:T(8,128)} fusion(f32[576,512]{1,0:T(8,128)S(1)} %pad_maximum_fusion, s32[1024]{0:T(1024)S(1)} %pad_clamp_fusion.5), kind=kCustom, calls=%fused_computation.1.clone | custom fusion | bytes 2099200 | tf_op jit(solution)/shard_map/jit(_take)/gather | solution.py:68
  25.7 2.4 %gather_fusion.3 = f32[512,512]{1,0:T(8,128)} fusion(f32[576,512]{1,0:T(8,128)S(1)} %pad_maximum_fusion, s32[1024]{0:T(1024)S(1)} %pad_clamp_fusion.4), kind=kCustom, calls=%fused_computation.7.clone | custom fusion | bytes 2099200 | tf_op jit(solution)/shard_map/jit(_take)/gather | solution.py:68
  28.1 2.3 %gather_fusion.4 = f32[512,512]{1,0:T(8,128)} fusion(f32[576,512]{1,0:T(8,128)S(1)} %pad_maximum_fusion, s32[1024]{0:T(1024)S(1)} %pad_clamp_fusion.3), kind=kCustom, calls=%fused_computation.8.clone | custom fusion | bytes 2099200 | tf_op jit(solution)/shard_map/jit(_take)/gather | solution.py:68
  30.4 2.3 %gather_fusion.5 = f32[512,512]{1,0:T(8,128)} fusion(f32[576,512]{1,0:T(8,128)S(1)} %pad_maximum_fusion, s32[1024]{0:T(1024)S(1)} %pad_clamp_fusion.2), kind=kCustom, calls=%fused_computation.9.clone | custom fusion | bytes 2099200 | tf_op jit(solution)/shard_map/jit(_take)/gather | solution.py:68
  32.7 2.3 %gather_fusion.6 = f32[512,512]{1,0:T(8,128)} fusion(f32[576,512]{1,0:T(8,128)S(1)} %pad_maximum_fusion, s32[1024]{0:T(1024)S(1)} %copy-done.4), kind=kCustom, calls=%fused_computation.10.clone | custom fusion | bytes 2099200 | tf_op jit(solution)/shard_map/jit(_take)/gather | solution.py:68
  35.1 2.3 %gather_fusion.7 = f32[512,512]{1,0:T(8,128)} fusion(f32[576,512]{1,0:T(8,128)S(1)} %pad_maximum_fusion, s32[1024]{0:T(1024)S(1)} %pad_clamp_fusion), kind=kCustom, calls=%fused_computation.11.clone | custom fusion | bytes 2099200 | tf_op jit(solution)/shard_map/jit(_take)/gather | solution.py:68
  37.5 5.2 %fusion.28 = f32[512,512]{1,0:T(8,128)S(1)} fusion(f32[512,512]{1,0:T(8,128)} %copy.24, f32[512,512]{1,0:T(8,128)} %copy.23, f32[512,512]{1,0:T(8,128)} %gather_fusion.7, f32[512,512]{1,0:T(8,128)} %copy.22, f32[512,512]{1,0:T(8,128)} %gather_fusion.6, f32[512,512]{1,0:T(8,128)} %copy.21, f32[512,512]{1,0:T(8,128)} %gather_fusion.5, f32[512,512]{1,0:T(8,128)} %copy.20, ...), kind=kLoop, calls=%fused_computation.74 | loop fusion | flops 4980736 | bytes 15731712 | tf_op jit(solution)/shard_map/div | solution.py:69
  44.4 7.6 %collective-permute-start.2 = (f32[32,512]{1,0:T(8,128)S(1)}, f32[32,512]{1,0:T(8,128)S(1)}, u32[]{:S(2)}, u32[]{:S(2)}) collective-permute-start(f32[32,512]{1,0:T(8,128)S(1)} %broadcast_select_fusion.3), channel_id=1, source_target_pairs={{0,4},{4,8},{8,12},{12,16},{16,20},{20,24},{24,28},{28,32},{32,36}... | collective-permute-start | bytes 196616 | tf_op jit(solution)/shard_map/ppermute | solution.py:16
  52.0 2.1 %collective-permute-start.3 = (f32[32,512]{1,0:T(8,128)S(1)}, f32[32,512]{1,0:T(8,128)S(1)}, u32[]{:S(2)}, u32[]{:S(2)}) collective-permute-start(f32[32,512]{1,0:T(8,128)S(1)} %broadcast_select_fusion.2), channel_id=1, source_target_pairs={{4,0},{8,4},{12,8},{16,12},{20,16},{24,20},{28,24},{32,28},{36,32}... | collective-permute-start | bytes 196616 | tf_op jit(solution)/shard_map/ppermute | solution.py:16
  54.1 7.1 %collective-permute-done.3 = f32[32,512]{1,0:T(8,128)S(1)} collective-permute-done((f32[32,512]{1,0:T(8,128)S(1)}, f32[32,512]{1,0:T(8,128)S(1)}, u32[]{:S(2)}, u32[]{:S(2)}) %collective-permute-start.3) | collective-permute-done | bytes 65568 | tf_op jit(solution)/shard_map/ppermute | solution.py:16
  62.5 2.3 %gather_fusion.10 = f32[512,512]{1,0:T(8,128)} fusion(f32[576,512]{1,0:T(8,128)S(1)} %pad_maximum_fusion.1, s32[1024]{0:T(1024)S(1)} %pad_clamp_fusion.5), kind=kCustom, calls=%fused_computation.12.clone | custom fusion | bytes 2099200 | tf_op jit(solution)/shard_map/jit(_take)/gather | solution.py:68
  64.9 2.3 %gather_fusion.11 = f32[512,512]{1,0:T(8,128)} fusion(f32[576,512]{1,0:T(8,128)S(1)} %pad_maximum_fusion.1, s32[1024]{0:T(1024)S(1)} %pad_clamp_fusion.4), kind=kCustom, calls=%fused_computation.13.clone | custom fusion | bytes 2099200 | tf_op jit(solution)/shard_map/jit(_take)/gather | solution.py:68
  67.2 2.3 %gather_fusion.12 = f32[512,512]{1,0:T(8,128)} fusion(f32[576,512]{1,0:T(8,128)S(1)} %pad_maximum_fusion.1, s32[1024]{0:T(1024)S(1)} %pad_clamp_fusion.3), kind=kCustom, calls=%fused_computation.14.clone | custom fusion | bytes 2099200 | tf_op jit(solution)/shard_map/jit(_take)/gather | solution.py:68
  69.5 2.4 %gather_fusion.13 = f32[512,512]{1,0:T(8,128)} fusion(f32[576,512]{1,0:T(8,128)S(1)} %pad_maximum_fusion.1, s32[1024]{0:T(1024)S(1)} %pad_clamp_fusion.2), kind=kCustom, calls=%fused_computation.15.clone | custom fusion | bytes 2099200 | tf_op jit(solution)/shard_map/jit(_take)/gather | solution.py:68
  71.9 2.3 %gather_fusion.14 = f32[512,512]{1,0:T(8,128)} fusion(f32[576,512]{1,0:T(8,128)S(1)} %pad_maximum_fusion.1, s32[1024]{0:T(1024)S(1)} %copy-done.4), kind=kCustom, calls=%fused_computation.16.clone | custom fusion | bytes 2099200 | tf_op jit(solution)/shard_map/jit(_take)/gather | solution.py:68
  74.2 2.3 %gather_fusion.15 = f32[512,512]{1,0:T(8,128)} fusion(f32[576,512]{1,0:T(8,128)S(1)} %pad_maximum_fusion.1, s32[1024]{0:T(1024)S(1)} %pad_clamp_fusion), kind=kCustom, calls=%fused_computation.17.clone | custom fusion | bytes 2099200 | tf_op jit(solution)/shard_map/jit(_take)/gather | solution.py:68
  76.6 5.1 %fusion.21 = f32[512,512]{1,0:T(8,128)S(1)} fusion(f32[512,512]{1,0:T(8,128)} %copy.24, f32[512,512]{1,0:T(8,128)} %copy.23, f32[512,512]{1,0:T(8,128)} %gather_fusion.15, f32[512,512]{1,0:T(8,128)} %copy.22, f32[512,512]{1,0:T(8,128)} %gather_fusion.14, f32[512,512]{1,0:T(8,128)} %copy.21, f32[512,512]{1,0:T(8,128)} %gather_fusion.13, f32[512,512]{1,0:T(8,128)} %copy.20, ...), kind=kLoop, calls=%fused_computation.61 | loop fusion | flops 4980736 | bytes 15731712 | tf_op jit(solution)/shard_map/div | solution.py:69
  83.4 1.9 %collective-permute-start.4 = (f32[32,512]{1,0:T(8,128)S(1)}, f32[32,512]{1,0:T(8,128)S(1)}, u32[]{:S(2)}, u32[]{:S(2)}) collective-permute-start(f32[32,512]{1,0:T(8,128)S(1)} %broadcast_select_fusion.1), channel_id=1, source_target_pairs={{0,4},{4,8},{8,12},{12,16},{16,20},{20,24},{24,28},{28,32},{32,36}... | collective-permute-start | bytes 196616 | tf_op jit(solution)/shard_map/ppermute | solution.py:16
  85.4 3.4 %collective-permute-start.5 = (f32[32,512]{1,0:T(8,128)S(1)}, f32[32,512]{1,0:T(8,128)S(1)}, u32[]{:S(2)}, u32[]{:S(2)}) collective-permute-start(f32[32,512]{1,0:T(8,128)S(1)} %broadcast_select_fusion), channel_id=1, source_target_pairs={{4,0},{8,4},{12,8},{16,12},{20,16},{24,20},{28,24},{32,28},{36,32}... | collective-permute-start | bytes 196616 | tf_op jit(solution)/shard_map/ppermute | solution.py:16
  88.8 5.8 %collective-permute-done.5 = f32[32,512]{1,0:T(8,128)S(1)} collective-permute-done((f32[32,512]{1,0:T(8,128)S(1)}, f32[32,512]{1,0:T(8,128)S(1)}, u32[]{:S(2)}, u32[]{:S(2)}) %collective-permute-start.5) | collective-permute-done | bytes 65568 | tf_op jit(solution)/shard_map/ppermute | solution.py:16
  95.9 2.3 %gather_fusion.18 = f32[512,512]{1,0:T(8,128)} fusion(f32[576,512]{1,0:T(8,128)S(1)} %pad_maximum_fusion.2, s32[1024]{0:T(1024)S(1)} %pad_clamp_fusion.5), kind=kCustom, calls=%fused_computation.18.clone | custom fusion | bytes 2099200 | tf_op jit(solution)/shard_map/jit(_take)/gather | solution.py:68
  98.3 2.3 %gather_fusion.19 = f32[512,512]{1,0:T(8,128)} fusion(f32[576,512]{1,0:T(8,128)S(1)} %pad_maximum_fusion.2, s32[1024]{0:T(1024)S(1)} %pad_clamp_fusion.4), kind=kCustom, calls=%fused_computation.19.clone | custom fusion | bytes 2099200 | tf_op jit(solution)/shard_map/jit(_take)/gather | solution.py:68
  100.6 2.4 %gather_fusion.20 = f32[512,512]{1,0:T(8,128)} fusion(f32[576,512]{1,0:T(8,128)S(1)} %pad_maximum_fusion.2, s32[1024]{0:T(1024)S(1)} %pad_clamp_fusion.3), kind=kCustom, calls=%fused_computation.20.clone | custom fusion | bytes 2099200 | tf_op jit(solution)/shard_map/jit(_take)/gather | solution.py:68
  103.0 2.3 %gather_fusion.21 = f32[512,512]{1,0:T(8,128)} fusion(f32[576,512]{1,0:T(8,128)S(1)} %pad_maximum_fusion.2, s32[1024]{0:T(1024)S(1)} %pad_clamp_fusion.2), kind=kCustom, calls=%fused_computation.21.clone | custom fusion | bytes 2099200 | tf_op jit(solution)/shard_map/jit(_take)/gather | solution.py:68
  105.3 2.3 %gather_fusion.22 = f32[512,512]{1,0:T(8,128)} fusion(f32[576,512]{1,0:T(8,128)S(1)} %pad_maximum_fusion.2, s32[1024]{0:T(1024)S(1)} %copy-done.4), kind=kCustom, calls=%fused_computation.22.clone | custom fusion | bytes 2099200 | tf_op jit(solution)/shard_map/jit(_take)/gather | solution.py:68
  107.6 2.3 %gather_fusion.23 = f32[512,512]{1,0:T(8,128)} fusion(f32[576,512]{1,0:T(8,128)S(1)} %pad_maximum_fusion.2, s32[1024]{0:T(1024)S(1)} %copy-done.6), kind=kCustom, calls=%fused_computation.23.clone | custom fusion | bytes 2099200 | tf_op jit(solution)/shard_map/jit(_take)/gather | solution.py:68
  110.0 5.1 %fusion.14 = f32[512,512]{0,1:T(8,128)S(1)} fusion(f32[512,512]{1,0:T(8,128)} %copy.24, f32[512,512]{1,0:T(8,128)} %copy.23, f32[512,512]{1,0:T(8,128)} %gather_fusion.23, f32[512,512]{1,0:T(8,128)} %copy.22, f32[512,512]{1,0:T(8,128)} %gather_fusion.22, f32[512,512]{1,0:T(8,128)} %copy.21, f32[512,512]{1,0:T(8,128)} %gather_fusion.21, f32[512,512]{1,0:T(8,128)} %copy.20, ...), kind=kLoop, calls=%fused_computation.48 | loop fusion | flops 4980736 | bytes 15731712 | tf_op jit(solution)/shard_map/transpose | solution.py:70
  115.9 4.5 %collective-permute-start.6 = (f32[1,32,512]{1,2,0:T(8,128)}, f32[1,32,512]{1,2,0:T(8,128)S(1)}, u32[]{:S(2)}, u32[]{:S(2)}) collective-permute-start(f32[1,32,512]{1,2,0:T(8,128)} %get-tuple-element.11), channel_id=1, source_target_pairs={{0,1},{1,2},{2,3},{3,0},{4,5},{5,6},{6,7},{7,4},{8,9},{9,10},{10,1... | collective-permute-start | bytes 196616 | tf_op jit(solution)/shard_map/ppermute | solution.py:26
  121.0 3.3 %collective-permute-done.6 = f32[1,32,512]{1,2,0:T(8,128)S(1)} collective-permute-done((f32[1,32,512]{1,2,0:T(8,128)}, f32[1,32,512]{1,2,0:T(8,128)S(1)}, u32[]{:S(2)}, u32[]{:S(2)}) %collective-permute-start.6) | collective-permute-done | bytes 65568 | tf_op jit(solution)/shard_map/ppermute | solution.py:26
  124.4 4.9 %collective-permute-done.7 = f32[1,32,512]{1,2,0:T(8,128)S(1)} collective-permute-done((f32[1,32,512]{1,2,0:T(8,128)S(1)}, f32[1,32,512]{1,2,0:T(8,128)S(1)}, u32[]{:S(2)}, u32[]{:S(2)}) %collective-permute-start.7) | collective-permute-done | bytes 65568 | tf_op jit(solution)/shard_map/ppermute | solution.py:27
  (120 shorter events, 25.8 us)
Async XLA Ops:
  0.0 1.6 %copy-start.26 = (s32[2,32]{1,0:T(2,128)S(1)}, s32[2,32]{1,0:T(2,128)}, u32[]{:S(2)}) copy-start(s32[2,32]{1,0:T(2,128)} %param.16) | copy-start | bytes 772
  1.6 8.7 %copy-start.9 = (s32[6,512]{1,0:T(8,128)S(1)}, s32[6,512]{1,0:T(8,128)}, u32[]{:S(2)}) copy-start(s32[6,512]{1,0:T(8,128)} %param.15) | copy-start | bytes 36868
  1.6 11.7 %copy-start.7 = (f32[6,512]{1,0:T(8,128)S(1)}, f32[6,512]{1,0:T(8,128)}, u32[]{:S(2)}) copy-start(f32[6,512]{1,0:T(8,128)} %param.13) | copy-start | bytes 36868
  1.6 11.7 %copy-start.8 = (f32[6,512]{1,0:T(8,128)S(1)}, f32[6,512]{1,0:T(8,128)}, u32[]{:S(2)}) copy-start(f32[6,512]{1,0:T(8,128)} %param.14) | copy-start | bytes 36868
  1.6 6.0 %copy-start.16 = (pred[32]{0:T(512)(128)(4,1)}, pred[32]{0:T(512)(128)(4,1)S(1)}, u32[]{:S(2)}) copy-start(pred[32]{0:T(512)(128)(4,1)S(1)} %get-tuple-element.29) | copy-start | bytes 100
  1.7 6.0 %copy-start.18 = (pred[32]{0:T(512)(128)(4,1)}, pred[32]{0:T(512)(128)(4,1)S(1)}, u32[]{:S(2)}) copy-start(pred[32]{0:T(512)(128)(4,1)S(1)} %get-tuple-element.6) | copy-start | bytes 100
  1.7 10.4 %copy-start.21 = (s32[1024]{0:T(1024)}, s32[1024]{0:T(1024)S(1)}, u32[]{:S(2)}) copy-start(s32[1024]{0:T(1024)S(1)} %pad_clamp_fusion.7) | copy-start | bytes 12292
  2.4 20.9 %collective-permute-start = (f32[32,512]{1,0:T(8,128)S(1)}, f32[32,512]{1,0:T(8,128)S(1)}, u32[]{:S(2)}, u32[]{:S(2)}) collective-permute-start(f32[32,512]{1,0:T(8,128)S(1)} %broadcast_select_fusion.5), channel_id=1, source_target_pairs={{0,4},{4,8},{8,12},{12,16},{16,20},{20,24},{24,28},{28,32},{32,36}... | collective-permute-start | bytes 196616 | tf_op jit(solution)/shard_map/ppermute | solution.py:16
  8.4 14.9 %collective-permute-start.1 = (f32[32,512]{1,0:T(8,128)}, f32[32,512]{1,0:T(8,128)S(1)}, u32[]{:S(2)}, u32[]{:S(2)}) collective-permute-start(f32[32,512]{1,0:T(8,128)} %broadcast_select_fusion.4), channel_id=1, source_target_pairs={{4,0},{8,4},{12,8},{16,12},{20,16},{24,20},{28,24},{32,28},{36,32}... | collective-permute-start | bytes 196616 | tf_op jit(solution)/shard_map/ppermute | solution.py:16
  23.3 51.0 %copy-start.5 = (s32[1024]{0:T(1024)}, s32[1024]{0:T(1024)S(1)}, u32[]{:S(2)}) copy-start(s32[1024]{0:T(1024)S(1)} %pad_clamp_fusion) | copy-start | bytes 12292
  30.4 2.4 %copy-start.4 = (s32[1024]{0:T(1024)S(1)}, s32[1024]{0:T(1024)}, u32[]{:S(2)}) copy-start(s32[1024]{0:T(1024)} %pad_clamp_fusion.1) | copy-start | bytes 12292
  35.1 2.4 %copy-start.10 = (pred[512]{0:T(512)(128)(4,1)S(1)}, pred[512]{0:T(512)(128)(4,1)}, u32[]{:S(2)}) copy-start(pred[512]{0:T(512)(128)(4,1)} %get-tuple-element.31) | copy-start | bytes 1540
  35.1 2.4 %copy-start.11 = (pred[512]{0:T(512)(128)(4,1)S(1)}, pred[512]{0:T(512)(128)(4,1)}, u32[]{:S(2)}) copy-start(pred[512]{0:T(512)(128)(4,1)} %get-tuple-element.32) | copy-start | bytes 1540
  35.1 2.4 %copy-start.12 = (pred[512]{0:T(512)(128)(4,1)S(1)}, pred[512]{0:T(512)(128)(4,1)}, u32[]{:S(2)}) copy-start(pred[512]{0:T(512)(128)(4,1)} %get-tuple-element.33) | copy-start | bytes 1540
  35.1 2.4 %copy-start.13 = (pred[512]{0:T(512)(128)(4,1)S(1)}, pred[512]{0:T(512)(128)(4,1)}, u32[]{:S(2)}) copy-start(pred[512]{0:T(512)(128)(4,1)} %get-tuple-element.34) | copy-start | bytes 1540
  35.1 2.4 %copy-start.14 = (pred[512]{0:T(512)(128)(4,1)S(1)}, pred[512]{0:T(512)(128)(4,1)}, u32[]{:S(2)}) copy-start(pred[512]{0:T(512)(128)(4,1)} %get-tuple-element.35) | copy-start | bytes 1540
  35.1 2.4 %copy-start.15 = (pred[512]{0:T(512)(128)(4,1)S(1)}, pred[512]{0:T(512)(128)(4,1)}, u32[]{:S(2)}) copy-start(pred[512]{0:T(512)(128)(4,1)} %get-tuple-element.36) | copy-start | bytes 1540
  42.7 11.5 %copy-start.1 = (f32[512,512]{1,0:T(8,128)}, f32[512,512]{1,0:T(8,128)S(1)}, u32[]{:S(2)}) copy-start(f32[512,512]{1,0:T(8,128)S(1)} %fusion.28) | copy-start | bytes 3145732
  42.7 1.6 %copy-start.19 = (pred[32]{0:T(512)(128)(4,1)S(1)}, pred[32]{0:T(512)(128)(4,1)}, u32[]{:S(2)}) copy-start(pred[32]{0:T(512)(128)(4,1)} %copy-done.18) | copy-start | bytes 100
  42.7 9.3 %copy-start.17 = (pred[32]{0:T(512)(128)(4,1)S(1)}, pred[32]{0:T(512)(128)(4,1)}, u32[]{:S(2)}) copy-start(pred[32]{0:T(512)(128)(4,1)} %copy-done.16) | copy-start | bytes 100
  44.4 9.8 %collective-permute-start.2 = (f32[32,512]{1,0:T(8,128)S(1)}, f32[32,512]{1,0:T(8,128)S(1)}, u32[]{:S(2)}, u32[]{:S(2)}) collective-permute-start(f32[32,512]{1,0:T(8,128)S(1)} %broadcast_select_fusion.3), channel_id=1, source_target_pairs={{0,4},{4,8},{8,12},{12,16},{16,20},{20,24},{24,28},{28,32},{32,36}... | collective-permute-start | bytes 196616 | tf_op jit(solution)/shard_map/ppermute | solution.py:16
  52.0 9.2 %collective-permute-start.3 = (f32[32,512]{1,0:T(8,128)S(1)}, f32[32,512]{1,0:T(8,128)S(1)}, u32[]{:S(2)}, u32[]{:S(2)}) collective-permute-start(f32[32,512]{1,0:T(8,128)S(1)} %broadcast_select_fusion.2), channel_id=1, source_target_pairs={{4,0},{8,4},{12,8},{16,12},{20,16},{24,20},{28,24},{32,28},{36,32}... | collective-permute-start | bytes 196616 | tf_op jit(solution)/shard_map/ppermute | solution.py:16
  81.7 7.1 %copy-start = (f32[512,512]{1,0:T(8,128)}, f32[512,512]{1,0:T(8,128)S(1)}, u32[]{:S(2)}) copy-start(f32[512,512]{1,0:T(8,128)S(1)} %fusion.21) | copy-start | bytes 3145732
  81.7 7.0 %copy-start.2 = (f32[32,512]{1,0:T(8,128)S(1)}, f32[32,512]{1,0:T(8,128)}, u32[]{:S(2)}) copy-start(f32[32,512]{1,0:T(8,128)} %param.19) | copy-start | bytes 196612
  83.4 5.4 %collective-permute-start.4 = (f32[32,512]{1,0:T(8,128)S(1)}, f32[32,512]{1,0:T(8,128)S(1)}, u32[]{:S(2)}, u32[]{:S(2)}) collective-permute-start(f32[32,512]{1,0:T(8,128)S(1)} %broadcast_select_fusion.1), channel_id=1, source_target_pairs={{0,4},{4,8},{8,12},{12,16},{16,20},{20,24},{24,28},{28,32},{32,36}... | collective-permute-start | bytes 196616 | tf_op jit(solution)/shard_map/ppermute | solution.py:16
  85.4 9.2 %collective-permute-start.5 = (f32[32,512]{1,0:T(8,128)S(1)}, f32[32,512]{1,0:T(8,128)S(1)}, u32[]{:S(2)}, u32[]{:S(2)}) collective-permute-start(f32[32,512]{1,0:T(8,128)S(1)} %broadcast_select_fusion), channel_id=1, source_target_pairs={{4,0},{8,4},{12,8},{16,12},{20,16},{24,20},{28,24},{32,28},{36,32}... | collective-permute-start | bytes 196616 | tf_op jit(solution)/shard_map/ppermute | solution.py:16
  105.3 2.4 %copy-start.6 = (s32[1024]{0:T(1024)S(1)}, s32[1024]{0:T(1024)}, u32[]{:S(2)}) copy-start(s32[1024]{0:T(1024)} %copy-done.5) | copy-start | bytes 12292
  109.9 10.5 %copy-start.24 = (f32[16]{0:T(128)S(1)}, f32[16]{0:T(128)}, u32[]{:S(2)}) copy-start(f32[16]{0:T(128)} %copy-done.23) | copy-start | bytes 196
  110.0 10.5 %copy-start.25 = (f32[512]{0:T(512)S(1)}, f32[512]{0:T(512)}, u32[]{:S(2)}) copy-start(f32[512]{0:T(512)} %param.18) | copy-start | bytes 6148
  115.9 8.4 %collective-permute-start.6 = (f32[1,32,512]{1,2,0:T(8,128)}, f32[1,32,512]{1,2,0:T(8,128)S(1)}, u32[]{:S(2)}, u32[]{:S(2)}) collective-permute-start(f32[1,32,512]{1,2,0:T(8,128)} %get-tuple-element.11), channel_id=1, source_target_pairs={{0,1},{1,2},{2,3},{3,0},{4,5},{5,6},{6,7},{7,4},{8,9},{9,10},{10,1... | collective-permute-start | bytes 196616 | tf_op jit(solution)/shard_map/ppermute | solution.py:26
  120.5 8.9 %collective-permute-start.7 = (f32[1,32,512]{1,2,0:T(8,128)S(1)}, f32[1,32,512]{1,2,0:T(8,128)S(1)}, u32[]{:S(2)}, u32[]{:S(2)}) collective-permute-start(f32[1,32,512]{1,2,0:T(8,128)S(1)} %get-tuple-element.12), channel_id=1, source_target_pairs={{1,0},{2,1},{3,2},{0,3},{5,4},{6,5},{7,6},{4,7},{9,8},{10,9},{11,1... | collective-permute-start | bytes 196616 | tf_op jit(solution)/shard_map/ppermute | solution.py:27
  120.7 8.8 %copy-start.3 = (f32[32,512]{1,0:T(8,128)S(1)}, f32[32,512]{1,0:T(8,128)}, u32[]{:S(2)}) copy-start(f32[32,512]{1,0:T(8,128)} %param.17) | copy-start | bytes 196612
  (3 other events, 2.8 us)
where the time goes:
time: 132 us; the launch traced here: 131 us
  local copies, waits for them, and re-layouts  58.6 us (44%)
  starting transfers between devices  26 us (20%)
  other arithmetic  24.7 us (19%)
  waiting for transfers between devices  21.2 us (16%)
    gather x18, local copies, waits for them, and re-layouts, shards(): jnp.take(extended, neighbours[slot], axis=0)  42.1 us
    ppermute x6, starting transfers between devices, passed_along(): return lax.ppermute(array, axis, pairs)  21.5 us
    ppermute x6, waiting for transfers between devices, passed_along(): return lax.ppermute(array, axis, pairs)  12.9 us
    div x2, other arithmetic, shards(): field = total / denom_wide  10.3 us
    broadcast_in_dim x12, local copies, waits for them, and re-layouts, shards(): weight_wide = jnp.repeat(weight_nodes, freq_count, axis=2)  7.69 us
    transpose x1, other arithmetic, shards(): swept = field.T.reshape(sector, freq_count, node_count)  5.15 us
    ppermute x1, waiting for transfers between devices, extended_2(): after = lax.ppermute(first, axis, down)  4.94 us
    ppermute x1, starting transfers between devices, extended_2(): before = lax.ppermute(last, axis, up)  4.53 us
  transfers between devices with their start and end apart: 8, of which 4 were waited for; matrix products, arithmetic and copies ran while one was open for 11% of the time, Pallas kernels for 0%

commit v1 on v0

v1 whole, which is shorter than its diff:
```python
import math

import jax
import jax.numpy as jnp
from jax import lax
from jax.experimental import pallas as pl
from jax.experimental.pallas import tpu as pltpu
from jax.sharding import PartitionSpec as P

NDIR = 64
NEIGH = 6
LANES = 128
PAD = 8

F32 = jnp.float32
VMEM = pl.BlockSpec(memory_space=pltpu.VMEM)
SMEM = pl.BlockSpec(memory_space=pltpu.SMEM)
ANY = pl.BlockSpec(memory_space=pl.ANY)


def params():
    return pltpu.CompilerParams(vmem_limit_bytes=8 << 20)


def cost(flops, nbytes):
    return pl.CostEstimate(flops=flops, bytes_accessed=nbytes, transcendentals=0)


def low_half():
    return lax.broadcasted_iota(jnp.int32, (8, LANES), 0) < 4


def two_rows(ref, first, second, low):
    return jnp.where(low, ref[pl.ds(first + PAD, 8), :], ref[pl.ds(second + (PAD - 4), 8), :])


def rows_body(send, action, field, to_upper, to_lower, stage, sems):
    chunks = action.shape[0] // LANES
    nodes = action.shape[1]
    copies = []
    for c in range(chunks):
        copy = pltpu.make_async_copy(action.at[pl.ds(c * LANES, LANES), :], stage.at[c], sems.at[c])
        copy.start()
        copies.append(copy)
    for c in range(chunks):
        copies[c].wait()
        field[pl.ds(PAD + c, nodes, stride=4), :] = stage[c].T
    low = low_half()
    ghost = to_upper.shape[0] // 4
    for i in range(0, ghost, 2):
        to_upper[pl.ds(4 * i, 8), :] = two_rows(field, send[1, i] * 4, send[1, i + 1] * 4, low)
        to_lower[pl.ds(4 * i, 8), :] = two_rows(field, send[0, i] * 4, send[0, i + 1] * 4, low)


def weights_body(edge_angle, edge_speed, field, weight, base):
    sector = 16
    nodes = edge_angle.shape[1]
    freq = 4 * LANES // sector
    first = lax.axis_index("dir") * sector
    number = lax.broadcasted_iota(jnp.int32, (sector, nodes), 0) + first
    angle = (2.0 * math.pi) * number.astype(F32) / NDIR
    parts = []
    total = jnp.ones((sector, nodes), F32)
    for j in range(NEIGH):
        part = edge_speed[pl.ds(j, 1), :] * jnp.maximum(jnp.cos(angle - edge_angle[pl.ds(j, 1), :]), 0.0)
        parts.append(part)
        total = total + part
    inverse = 1.0 / total
    spread = (
        lax.broadcasted_iota(jnp.int32, (3 * sector, 4 * LANES), 0) % sector
        == lax.broadcasted_iota(jnp.int32, (3 * sector, 4 * LANES), 1) // freq
    ).astype(F32).astype(jnp.bfloat16)

    def widened(value):
        high = value.astype(jnp.bfloat16)
        rest = value - high.astype(F32)
        middle = rest.astype(jnp.bfloat16)
        last = (rest - middle.astype(F32)).astype(jnp.bfloat16)
        pieces = jnp.concatenate([high, middle, last], axis=0)
        return lax.dot_general(pieces, spread, (((0,), (0,)), ((), ())), preferred_element_type=F32)

    for j in range(NEIGH):
        wide = widened(parts[j] * inverse)
        for c in range(4):
            weight[pl.ds(PAD + j * 4 * nodes + c, nodes, stride=4), :] = wide[:, c * LANES : (c + 1) * LANES]
    wide = widened(inverse)
    for c in range(4):
        rows = pl.ds(PAD + c, nodes, stride=4)
        base[rows, :] = field[rows, :] * wide[:, c * LANES : (c + 1) * LANES]


def place_ghosts(field, lower, upper, nodes):
    part = lax.axis_index("dom")
    last = lax.axis_size("dom") - 1
    rows = lower.shape[0]
    field[pl.ds(PAD + 4 * nodes, rows), :] = jnp.where(part > 0, lower[...], 0.0)
    field[pl.ds(PAD + 4 * nodes + rows, rows), :] = jnp.where(part < last, upper[...], 0.0)


def shared_body(send, slots, field_in, lower, upper, weight, base, field, to_upper, to_lower):
    del field_in
    nodes = slots.shape[0] // NEIGH
    place_ghosts(field, lower, upper, nodes)
    low = low_half()
    ghost = to_upper.shape[0] // 4
    for row, out in ((1, to_upper), (0, to_lower)):
        for i in range(0, ghost, 2):
            n = send[row, i]
            m = send[row, i + 1]
            total = two_rows(base, n * 4, m * 4, low)
            for j in range(NEIGH):
                w = two_rows(weight, n * 4 + j * 4 * nodes, m * 4 + j * 4 * nodes, low)
                total = total + w * two_rows(field, slots[j * nodes + n], slots[j * nodes + m], low)
            out[pl.ds(4 * i, 8), :] = total


def sweep_rows(slots, field, weight, base, out, nodes, offset):
    low = low_half()

    def step(i, carry):
        n = i * 2
        row = pl.multiple_of(i * 8, 8)
        total = base[pl.ds(PAD + row, 8), :]
        for j in range(NEIGH):
            value = two_rows(field, slots[j * nodes + n], slots[j * nodes + n + 1], low)
            total = total + weight[pl.ds(PAD + j * 4 * nodes + row, 8), :] * value
        out[pl.ds(offset + row, 8), :] = total
        return carry

    lax.fori_loop(0, nodes // 2, step, 0, unroll=8)


def sweep_body(slots, field, weight, base, out):
    sweep_rows(slots, field, weight, base, out, slots.shape[0] // NEIGH, PAD)


def last_body(slots, field_in, lower, upper, weight, base, field, swept, first, last, rows):
    del field_in
    nodes = slots.shape[0] // NEIGH
    place_ghosts(field, lower, upper, nodes)
    sweep_rows(slots, field, weight, base, rows, nodes, 0)
    freq = first.shape[0]
    for c in range(4):
        planes = rows[pl.ds(c, nodes, stride=4), :].T
        swept[pl.ds(c * LANES, LANES), :] = planes
        if c == 0:
            first[...] = planes[:freq, :]
        if c == 3:
            last[...] = planes[LANES - freq :, :]


def finished(plane, before, after, direction, rate, bearing, shift):
    angle = (2.0 * math.pi) * direction.astype(F32) / NDIR
    speed = rate * jnp.sin(angle - bearing)
    value = plane - (jnp.maximum(speed, 0.0) * (plane - before) + jnp.minimum(speed, 0.0) * (after - plane))
    freq = plane.shape[0]
    row = lax.broadcasted_iota(jnp.int32, plane.shape, 0)
    under = jnp.where(row == 0, 0.0, pltpu.roll(value, 1, 0))
    over = jnp.where(row == freq - 1, 0.0, pltpu.roll(value, freq - 1, 0))
    return value - (jnp.maximum(shift, 0.0) * (value - under) + jnp.minimum(shift, 0.0) * (over - value))


def inner_body(swept, rate, bearing, shift, out, stage, sem):
    freq, nodes = rate.shape
    sector = swept.shape[0] // freq
    first = jnp.full((1, nodes), lax.axis_index("dir") * sector, jnp.int32)
    for d in range(1, sector - 1):
        plane = swept[pl.ds(d * freq, freq), :]
        stage[pl.ds((d - 1) * freq, freq), :] = finished(
            plane,
            swept[pl.ds((d - 1) * freq, freq), :],
            swept[pl.ds((d + 1) * freq, freq), :],
            first + d,
            rate[...],
            bearing[...],
            shift[...],
        )
    copy = pltpu.make_async_copy(stage, out.at[pl.ds(freq, (sector - 2) * freq), :], sem)
    copy.start()
    copy.wait()


def edge_body(swept, before, after, rate, bearing, shift, out_in, out, stage, sem):
    del out_in
    freq, nodes = rate.shape
    sector = swept.shape[0] // freq
    first = jnp.full((1, nodes), lax.axis_index("dir") * sector, jnp.int32)
    copies = []
    for k, d in enumerate((0, sector - 1)):
        plane = swept[pl.ds(d * freq, freq), :]
        low = before[...] if d == 0 else swept[pl.ds((d - 1) * freq, freq), :]
        high = after[...] if d == sector - 1 else swept[pl.ds((d + 1) * freq, freq), :]
        stage[k] = finished(plane, low, high, first + d, rate[...], bearing[...], shift[...])
        copy = pltpu.make_async_copy(stage.at[k], out.at[pl.ds(d * freq, freq), :], sem.at[k])
        copy.start()
        copies.append(copy)
    for copy in copies:
        copy.wait()


def around(array, axis, by):
    count = lax.axis_size(axis)
    return lax.ppermute(array, axis, [(i, (i + by) % count) for i in range(count)])


def shards(
    action, edge_angle, edge_speed, neighbours, send_rows, refract_rate, refract_angle, shift_rate
):
    sector, freq, nodes = action.shape
    ghost = send_rows.shape[1]
    field_rows = 4 * (nodes + 2 * ghost) + 2 * PAD
    fields = jax.ShapeDtypeStruct((field_rows, LANES), F32)
    shares = jax.ShapeDtypeStruct((4 * ghost, LANES), F32)
    weights = jax.ShapeDtypeStruct((NEIGH * 4 * nodes + 2 * PAD, LANES), F32)
    bases = jax.ShapeDtypeStruct((4 * nodes + 2 * PAD, LANES), F32)
    columns = sector * freq
    slots = (neighbours * 4).reshape(-1)
    bearing = refract_angle.reshape(1, nodes)

    field, up, down = pl.pallas_call(
        rows_body,
        out_shape=(fields, shares, shares),
        in_specs=[SMEM, ANY],
        out_specs=(VMEM, VMEM, VMEM),
        scratch_shapes=[pltpu.VMEM((4, LANES, nodes), F32), pltpu.SemaphoreType.DMA((4,))],
        compiler_params=params(),
        name="rows",
    )(send_rows, action.reshape(columns, nodes))
    lower = around(up, "dom", 1)
    upper = around(down, "dom", -1)
    weight, base = pl.pallas_call(
        weights_body,
        out_shape=(weights, bases),
        in_specs=[VMEM] * 3,
        out_specs=(VMEM, VMEM),
        compiler_params=params(),
        cost_estimate=cost(1 << 30, 8 << 20),
        name="weights",
    )(edge_angle, edge_speed, field)

    for _ in range(2):
        field, up, down = pl.pallas_call(
            shared_body,
            out_shape=(fields, shares, shares),
            in_specs=[SMEM, SMEM] + [VMEM] * 5,
            out_specs=(VMEM, VMEM, VMEM),
            input_output_aliases={2: 0},
            compiler_params=params(),
            name="shared",
        )(send_rows, slots, field, lower, upper, weight, base)
        lower = around(up, "dom", 1)
        upper = around(down, "dom", -1)
        field = pl.pallas_call(
            sweep_body,
            out_shape=fields,
            in_specs=[SMEM] + [VMEM] * 3,
            out_specs=VMEM,
            compiler_params=params(),
            cost_estimate=cost(1 << 30, 8 << 20),
            name="sweep",
        )(slots, field, weight, base)

    edge = jax.ShapeDtypeStruct((freq, nodes), F32)
    plane_shape = jax.ShapeDtypeStruct((columns, nodes), F32)
    _, swept, first, last = pl.pallas_call(
        last_body,
        out_shape=(fields, plane_shape, edge, edge),
        in_specs=[SMEM] + [VMEM] * 5,
        out_specs=(VMEM,) * 4,
        input_output_aliases={1: 0},
        scratch_shapes=[pltpu.VMEM((4 * nodes, LANES), F32)],
        compiler_params=params(),
        name="last_sweep",
    )(slots, field, lower, upper, weight, base)
    before = around(last, "dir", 1)
    after = around(first, "dir", -1)
    out = pl.pallas_call(
        inner_body,
        out_shape=plane_shape,
        in_specs=[VMEM] * 4,
        out_specs=ANY,
        scratch_shapes=[pltpu.VMEM((columns - 2 * freq, nodes), F32), pltpu.SemaphoreType.DMA],
        compiler_params=params(),
        cost_estimate=cost(1 << 28, 2 << 20),
        name="inner_planes",
    )(swept, refract_rate, bearing, shift_rate)
    out = pl.pallas_call(
        edge_body,
        out_shape=plane_shape,
        in_specs=[VMEM] * 6 + [ANY],
        out_specs=ANY,
        input_output_aliases={6: 0},
        scratch_shapes=[pltpu.VMEM((2, freq, nodes), F32), pltpu.SemaphoreType.DMA((2,))],
        compiler_params=params(),
        name="edge_planes",
    )(swept, before, after, refract_rate, bearing, shift_rate, out)
    return out.reshape(sector, freq, nodes)


def solution(mesh):
    return jax.shard_map(
        shards,
        mesh=mesh,
        in_specs=(
            P("dir", None, "dom"),
            P(None, "dom"),
            P(None, "dom"),
            P(None, "dom"),
            P(None, "dom"),
            P(None, "dom"),
            P("dom"),
            P(None, "dom"),
        ),
        out_specs=P("dir", None, "dom"),
        check_vma=False,
    )
```

time: 132 us -> 52.8 us (0.40)
  the two profiles are of different devices: /device:TPU:127 before, /device:TPU:1 now
where the time goes in v1:
time: 52.8 us; the launch traced here: 52.4 us
  starting transfers between devices  25.9 us (49%)
  Pallas kernels  19 us (36%)
  local copies, waits for them, and re-layouts  3.36 us (6%)
  waiting for transfers between devices  3.21 us (6%)
  other arithmetic  0.72 us (1%)
    ppermute x8, starting transfers between devices, around(): lax.ppermute(array, axis, [(i, (i + by) % count) for i in range(count)])  25.9 us
    pallas_call x2, Pallas kernels, shards(): pl.pallas_call(sweep_body, out_shape=fields, in_specs=[SMEM] + [VMEM] * 3...  6.94 us
    pallas_call x1, Pallas kernels, shards(): pl.pallas_call(last_body, out_shape=(fields, plane_shape, edge, edge), in...  3.83 us
    unnamed x16, local copies, waits for them, and re-layouts  3.36 us
    ppermute x8, waiting for transfers between devices, around(): lax.ppermute(array, axis, [(i, (i + by) % count) for i in range(count)])  3.21 us
    pallas_call x2, Pallas kernels, shards(): pl.pallas_call(shared_body, out_shape=(fields, shares, shares), in_specs=...  2.43 us
    pallas_call x1, Pallas kernels, shards(): pl.pallas_call(inner_body, out_shape=plane_shape, in_specs=[VMEM] * 4, ou...  1.96 us
    pallas_call x1, Pallas kernels, shards(): pl.pallas_call(weights_body, out_shape=(weights, bases), in_specs=[VMEM]...  1.79 us
  transfers between devices with their start and end apart: 8, of which 1 were waited for; matrix products, arithmetic and copies ran while one was open for 1% of the time, Pallas kernels for 20%

profile of v1, /device:TPU:1, one launch (start us, length us, event | category | flops | bytes accessed | tf_op | source)
XLA Modules:
  0.0 52.4 jit_solution(14056617898651560885)
XLA Ops:
  0.0 1.2 %copy-done = f32[16,32,512]{2,1,0:T(8,128)S(1)} copy-done((f32[16,32,512]{2,1,0:T(8,128)S(1)}, f32[16,32,512]{2,1,0:T(8,128)}, u32[]{:S(2)}) %copy-start) | copy-done | bytes 1048600
  1.2 0.7 %copy-done.3 = s32[2,32]{1,0:T(2,128)S(1)} copy-done((s32[2,32]{1,0:T(2,128)S(1)}, s32[2,32]{1,0:T(2,128)}, u32[]{:S(2)}) %copy-start.3) | copy-done | bytes 280
  1.9 1.2 %rows.1 = (f32[2320,128]{1,0:T(8,128)S(1)}, f32[128,128]{1,0:T(8,128)S(1)}, f32[128,128]{1,0:T(8,128)S(1)}) custom-call(s32[2,32]{1,0:T(2,128)S(1)} %copy-done.3, f32[512,512]{1,0:T(8,128)S(1)} %bitcast.3), custom_call_target="tpu_custom_call" | custom-call | tf_op jit(solution)/shard_map/rows/pallas_call | solution.py:220
  3.1 2.2 %collective-permute-start = (f32[128,128]{1,0:T(8,128)S(1)}, f32[128,128]{1,0:T(8,128)S(1)}, u32[]{:S(2)}, u32[]{:S(2)}) collective-permute-start(f32[128,128]{1,0:T(8,128)S(1)} %get-tuple-element.20), channel_id=1, source_target_pairs={{0,4},{4,8},{8,12},{12,16},{16,20},{20,24},{24,28},{28,32},{32,36}... | collective-permute-start | bytes 196616 | tf_op jit(solution)/shard_map/ppermute | solution.py:203
  5.3 7.7 %collective-permute-start.1 = (f32[128,128]{1,0:T(8,128)S(1)}, f32[128,128]{1,0:T(8,128)S(1)}, u32[]{:S(2)}, u32[]{:S(2)}) collective-permute-start(f32[128,128]{1,0:T(8,128)S(1)} %get-tuple-element.21), channel_id=1, source_target_pairs={{0,252},{4,0},{8,4},{12,8},{16,12},{20,16},{24,20},{28,24},{32,28}... | collective-permute-start | bytes 196616 | tf_op jit(solution)/shard_map/ppermute | solution.py:203
  13.1 0.7 %broadcast_multiply_fusion = s32[6,512]{1,0:T(8,128)S(1)} fusion(s32[6,512]{1,0:T(8,128)} %param.11), kind=kLoop, calls=%fused_computation | loop fusion | flops 3072 | bytes 24576 | tf_op jit(solution)/shard_map/mul | solution.py:217
  13.8 0.7 %copy-done.6 = f32[6,512]{1,0:T(8,128)S(1)} copy-done((f32[6,512]{1,0:T(8,128)S(1)}, f32[6,512]{1,0:T(8,128)}, u32[]{:S(2)}) %copy-start.6) | copy-done | bytes 12312
  14.5 0.7 %copy-done.7 = f32[6,512]{1,0:T(8,128)S(1)} copy-done((f32[6,512]{1,0:T(8,128)S(1)}, f32[6,512]{1,0:T(8,128)}, u32[]{:S(2)}) %copy-start.7) | copy-done | bytes 12312
  15.3 1.8 %weights.1 = (f32[12304,128]{1,0:T(8,128)S(1)}, f32[2064,128]{1,0:T(8,128)S(1)}) custom-call(f32[6,512]{1,0:T(8,128)S(1)} %copy-done.6, f32[6,512]{1,0:T(8,128)S(1)} %copy-done.7, f32[2320,128]{1,0:T(8,128)S(1)} %get-tuple-element.19.field.field_in), custom_call_target="tpu_custom_call" | custom-call | flops 1073741824 | bytes 8388608 | tf_op jit(solution)/shard_map/weights/pallas_call | solution.py:231
  17.1 0.0 collective-permute-done.lower
  17.1 0.0 collective-permute-done.1.upper
  17.1 1.2 %shared.2 = (f32[2320,128]{1,0:T(8,128)S(1)}, f32[128,128]{1,0:T(8,128)S(1)}, f32[128,128]{1,0:T(8,128)S(1)}) custom-call(s32[2,32]{1,0:T(2,128)S(1)} %copy-done.4, s32[3072]{0:T(1024)S(1)} %reshape.12.slots, f32[2320,128]{1,0:T(8,128)S(1)} %get-tuple-element.19.field.field_in, ...), custom_call_target="tpu_custom_call", output_to_operand_aliasing={{0}: (2, {})} | custom-call | tf_op jit(solution)/shard_map/shared/pallas_call | solution.py:242
  18.3 0.1 collective-permute-start.2
  18.4 5.7 %collective-permute-start.3 = (f32[128,128]{1,0:T(8,128)S(1)}, f32[128,128]{1,0:T(8,128)S(1)}, u32[]{:S(2)}, u32[]{:S(2)}) collective-permute-start(f32[128,128]{1,0:T(8,128)S(1)} %get-tuple-element.26), channel_id=1, source_target_pairs={{0,252},{4,0},{8,4},{12,8},{16,12},{20,16},{24,20},{28,24},{32,28}... | collective-permute-start | bytes 196616 | tf_op jit(solution)/shard_map/ppermute | solution.py:203
  24.1 3.5 %sweep.2.field_in = f32[2320,128]{1,0:T(8,128)S(1)} custom-call(s32[3072]{0:T(1024)S(1)} %reshape.12.slots, f32[2320,128]{1,0:T(8,128)S(1)} %get-tuple-element.24.field, f32[12304,128]{1,0:T(8,128)S(1)} %get-tuple-element.22.weight, f32[2064,128]{1,0:T(8,128)S(1)} %get-tuple-element.23.base), custom_call_target="tpu_custom_call" | custom-call | flops 1073741824 | bytes 8388608 | tf_op jit(solution)/shard_map/sweep/pallas_call | solution.py:253
  27.5 0.0 collective-permute-done.2.lower
  27.6 0.0 collective-permute-done.3.upper
  27.6 1.2 %shared.3 = (f32[2320,128]{1,0:T(8,128)S(1)}, f32[128,128]{1,0:T(8,128)S(1)}, f32[128,128]{1,0:T(8,128)S(1)}) custom-call(s32[2,32]{1,0:T(2,128)S(1)} %copy-done.4, s32[3072]{0:T(1024)S(1)} %reshape.12.slots, f32[2320,128]{1,0:T(8,128)S(1)} %sweep.2.field_in, f32[128,128]{1,0:T(8,128)S(1)} %collective-permute-done.2.lower, ...), custom_call_target="tpu_custom_call", output_to_operand_aliasing={{0}: (2, {})} | custom-call | tf_op jit(solution)/shard_map/shared/pallas_call | solution.py:242
  28.8 0.1 collective-permute-start.4
  28.9 5.7 %collective-permute-start.5 = (f32[128,128]{1,0:T(8,128)S(1)}, f32[128,128]{1,0:T(8,128)S(1)}, u32[]{:S(2)}, u32[]{:S(2)}) collective-permute-start(f32[128,128]{1,0:T(8,128)S(1)} %get-tuple-element.29), channel_id=1, source_target_pairs={{0,252},{4,0},{8,4},{12,8},{16,12},{20,16},{24,20},{28,24},{32,28}... | collective-permute-start | bytes 196616 | tf_op jit(solution)/shard_map/ppermute | solution.py:203
  34.6 3.5 %sweep.3.field_in = f32[2320,128]{1,0:T(8,128)S(1)} custom-call(s32[3072]{0:T(1024)S(1)} %reshape.12.slots, f32[2320,128]{1,0:T(8,128)S(1)} %get-tuple-element.27.field, f32[12304,128]{1,0:T(8,128)S(1)} %get-tuple-element.22.weight, f32[2064,128]{1,0:T(8,128)S(1)} %get-tuple-element.23.base), custom_call_target="tpu_custom_call" | custom-call | flops 1073741824 | bytes 8388608 | tf_op jit(solution)/shard_map/sweep/pallas_call | solution.py:253
  38.0 0.0 copy-start.1
  38.0 0.0 copy-start.2
  38.0 0.0 copy-start.5
  38.1 0.0 collective-permute-done.5.upper
  38.1 3.8 %last_sweep.1 = (f32[2320,128]{1,0:T(8,128)S(1)}, f32[512,512]{1,0:T(8,128)S(1)}, f32[32,512]{1,0:T(8,128)S(1)}, f32[32,512]{1,0:T(8,128)S(1)}) custom-call(s32[3072]{0:T(1024)S(1)} %reshape.12.slots, f32[2320,128]{1,0:T(8,128)S(1)} %sweep.3.field_in, f32[128,128]{1,0:T(8,128)S(1)} %collective-permute-done.4.lower, ...), custom_call_target="tpu_custom_call", output_to_operand_aliasing={{0}: (1, {})} | custom-call | tf_op jit(solution)/shard_map/last_sweep/pallas_call | solution.py:265
  41.9 4.5 %collective-permute-start.6 = (f32[32,512]{1,0:T(8,128)S(1)}, f32[32,512]{1,0:T(8,128)S(1)}, u32[]{:S(2)}, u32[]{:S(2)}) collective-permute-start(f32[32,512]{1,0:T(8,128)S(1)} %get-tuple-element.31), channel_id=1, source_target_pairs={{0,1},{1,2},{2,3},{3,0},{4,5},{5,6},{6,7},{7,4},{8,9},{9,10},{10,1... | collective-permute-start | bytes 196616 | tf_op jit(solution)/shard_map/ppermute | solution.py:203
  46.4 0.0 collective-permute-start.7
  46.4 2.0 %inner_planes.1.out_in = f32[512,512]{1,0:T(8,128)} custom-call(f32[512,512]{1,0:T(8,128)S(1)} %get-tuple-element.30.swept, f32[32,512]{1,0:T(8,128)S(1)} %copy-done.1, f32[1,512]{1,0:T(1,128)S(1)} %bitcast.4, f32[32,512]{1,0:T(8,128)S(1)} %copy-done.2), custom_call_target="tpu_custom_call" | custom-call | flops 268435456 | bytes 2097152 | tf_op jit(solution)/shard_map/inner_planes/pallas_call | solution.py:277
  48.4 0.0 collective-permute-done.6.before
  48.4 3.2 %collective-permute-done.7.after = f32[32,512]{1,0:T(8,128)S(1)} collective-permute-done((f32[32,512]{1,0:T(8,128)S(1)}, f32[32,512]{1,0:T(8,128)S(1)}, u32[]{:S(2)}, u32[]{:S(2)}) %collective-permute-start.7) | collective-permute-done | bytes 65568 | tf_op jit(solution)/shard_map/ppermute | solution.py:203
  51.6 0.8 %edge_planes.1 = f32[512,512]{1,0:T(8,128)} custom-call(f32[512,512]{1,0:T(8,128)S(1)} %get-tuple-element.30.swept, f32[32,512]{1,0:T(8,128)S(1)} %collective-permute-done.6.before, f32[32,512]{1,0:T(8,128)S(1)} %collective-permute-done.7.after, f32[32,512]{1,0:T(8,128)S(1)} %copy-done.1, f32[1,512]{1,0:T(1,128)S(1)} %bitcast.5, ...), custom_call_target="tpu_custom_call", output_to_operand_aliasing={{}: (6, {})} | custom-call | tf_op jit(solution)/shard_map/edge_planes/pallas_call | solution.py:287
  (11 shorter events, 0.0 us)
Async XLA Ops:
  0.0 1.2 %copy-start = (f32[16,32,512]{2,1,0:T(8,128)S(1)}, f32[16,32,512]{2,1,0:T(8,128)}, u32[]{:S(2)}) copy-start(f32[16,32,512]{2,1,0:T(8,128)} %param.8) | copy-start | bytes 3145732
  1.2 0.7 %copy-start.3 = (s32[2,32]{1,0:T(2,128)S(1)}, s32[2,32]{1,0:T(2,128)}, u32[]{:S(2)}) copy-start(s32[2,32]{1,0:T(2,128)} %send.5) | copy-start | bytes 772
  3.1 13.9 %collective-permute-start = (f32[128,128]{1,0:T(8,128)S(1)}, f32[128,128]{1,0:T(8,128)S(1)}, u32[]{:S(2)}, u32[]{:S(2)}) collective-permute-start(f32[128,128]{1,0:T(8,128)S(1)} %get-tuple-element.20), channel_id=1, source_target_pairs={{0,4},{4,8},{8,12},{12,16},{16,20},{20,24},{24,28},{28,32},{32,36}... | collective-permute-start | bytes 196616 | tf_op jit(solution)/shard_map/ppermute | solution.py:203
  5.3 11.7 %collective-permute-start.1 = (f32[128,128]{1,0:T(8,128)S(1)}, f32[128,128]{1,0:T(8,128)S(1)}, u32[]{:S(2)}, u32[]{:S(2)}) collective-permute-start(f32[128,128]{1,0:T(8,128)S(1)} %get-tuple-element.21), channel_id=1, source_target_pairs={{0,252},{4,0},{8,4},{12,8},{16,12},{20,16},{24,20},{28,24},{32,28}... | collective-permute-start | bytes 196616 | tf_op jit(solution)/shard_map/ppermute | solution.py:203
  13.8 0.7 %copy-start.6 = (f32[6,512]{1,0:T(8,128)S(1)}, f32[6,512]{1,0:T(8,128)}, u32[]{:S(2)}) copy-start(f32[6,512]{1,0:T(8,128)} %edge_angle.1) | copy-start | bytes 36868
  14.5 0.7 %copy-start.7 = (f32[6,512]{1,0:T(8,128)S(1)}, f32[6,512]{1,0:T(8,128)}, u32[]{:S(2)}) copy-start(f32[6,512]{1,0:T(8,128)} %edge_speed.1) | copy-start | bytes 36868
  15.3 1.8 %copy-start.4 = (s32[2,32]{1,0:T(2,128)S(1)}, s32[2,32]{1,0:T(2,128)}, u32[]{:S(2)}) copy-start(s32[2,32]{1,0:T(2,128)} %send.5) | copy-start | bytes 772
  18.3 9.2 %collective-permute-start.2 = (f32[128,128]{1,0:T(8,128)S(1)}, f32[128,128]{1,0:T(8,128)S(1)}, u32[]{:S(2)}, u32[]{:S(2)}) collective-permute-start(f32[128,128]{1,0:T(8,128)S(1)} %get-tuple-element.25), channel_id=1, source_target_pairs={{0,4},{4,8},{8,12},{12,16},{16,20},{20,24},{24,28},{28,32},{32,36}... | collective-permute-start | bytes 196616 | tf_op jit(solution)/shard_map/ppermute | solution.py:203
  18.4 9.2 %collective-permute-start.3 = (f32[128,128]{1,0:T(8,128)S(1)}, f32[128,128]{1,0:T(8,128)S(1)}, u32[]{:S(2)}, u32[]{:S(2)}) collective-permute-start(f32[128,128]{1,0:T(8,128)S(1)} %get-tuple-element.26), channel_id=1, source_target_pairs={{0,252},{4,0},{8,4},{12,8},{16,12},{20,16},{24,20},{28,24},{32,28}... | collective-permute-start | bytes 196616 | tf_op jit(solution)/shard_map/ppermute | solution.py:203
  28.8 9.3 %collective-permute-start.4 = (f32[128,128]{1,0:T(8,128)S(1)}, f32[128,128]{1,0:T(8,128)S(1)}, u32[]{:S(2)}, u32[]{:S(2)}) collective-permute-start(f32[128,128]{1,0:T(8,128)S(1)} %get-tuple-element.28), channel_id=1, source_target_pairs={{0,4},{4,8},{8,12},{12,16},{16,20},{20,24},{24,28},{28,32},{32,36}... | collective-permute-start | bytes 196616 | tf_op jit(solution)/shard_map/ppermute | solution.py:203
  28.9 9.2 %collective-permute-start.5 = (f32[128,128]{1,0:T(8,128)S(1)}, f32[128,128]{1,0:T(8,128)S(1)}, u32[]{:S(2)}, u32[]{:S(2)}) collective-permute-start(f32[128,128]{1,0:T(8,128)S(1)} %get-tuple-element.29), channel_id=1, source_target_pairs={{0,252},{4,0},{8,4},{12,8},{16,12},{20,16},{24,20},{28,24},{32,28}... | collective-permute-start | bytes 196616 | tf_op jit(solution)/shard_map/ppermute | solution.py:203
  38.0 8.4 %copy-start.1 = (f32[32,512]{1,0:T(8,128)S(1)}, f32[32,512]{1,0:T(8,128)}, u32[]{:S(2)}) copy-start(f32[32,512]{1,0:T(8,128)} %rate.3) | copy-start | bytes 196612
  38.0 8.4 %copy-start.2 = (f32[32,512]{1,0:T(8,128)S(1)}, f32[32,512]{1,0:T(8,128)}, u32[]{:S(2)}) copy-start(f32[32,512]{1,0:T(8,128)} %shift.3) | copy-start | bytes 196612
  38.0 8.4 %copy-start.5 = (f32[512]{0:T(512)S(1)}, f32[512]{0:T(512)}, u32[]{:S(2)}) copy-start(f32[512]{0:T(512)} %param.14) | copy-start | bytes 6148
  41.9 6.5 %collective-permute-start.6 = (f32[32,512]{1,0:T(8,128)S(1)}, f32[32,512]{1,0:T(8,128)S(1)}, u32[]{:S(2)}, u32[]{:S(2)}) collective-permute-start(f32[32,512]{1,0:T(8,128)S(1)} %get-tuple-element.31), channel_id=1, source_target_pairs={{0,1},{1,2},{2,3},{3,0},{4,5},{5,6},{6,7},{7,4},{8,9},{9,10},{10,1... | collective-permute-start | bytes 196616 | tf_op jit(solution)/shard_map/ppermute | solution.py:203
  46.4 5.2 %collective-permute-start.7 = (f32[32,512]{1,0:T(8,128)S(1)}, f32[32,512]{1,0:T(8,128)S(1)}, u32[]{:S(2)}, u32[]{:S(2)}) collective-permute-start(f32[32,512]{1,0:T(8,128)S(1)} %get-tuple-element.32), channel_id=1, source_target_pairs={{0,3},{1,0},{2,1},{3,2},{4,7},{5,4},{6,5},{7,6},{8,11},{9,8},{10,9... | collective-permute-start | bytes 196616 | tf_op jit(solution)/shard_map/ppermute | solution.py:203

commit v2 on v1

--- a/solution.py
+++ b/solution.py
@@ -16,6 +16,11 @@
 VMEM = pl.BlockSpec(memory_space=pltpu.VMEM)
 SMEM = pl.BlockSpec(memory_space=pltpu.SMEM)
 ANY = pl.BlockSpec(memory_space=pl.ANY)
+HBM = pl.BlockSpec(memory_space=pltpu.HBM)
+
+
+def in_hbm(array):
+    return pltpu.with_memory_space_constraint(array, pltpu.HBM)
 
 
 def params():
@@ -34,7 +39,11 @@
     return jnp.where(low, ref[pl.ds(first + PAD, 8), :], ref[pl.ds(second + (PAD - 4), 8), :])
 
 
-def rows_body(send, action, field, to_upper, to_lower, stage, sems):
+def odd(axis):
+    return lax.axis_index(axis) % 2
+
+
+def rows_body(send_hbm, action, field, to_far, to_near, stage, send, sems, send_sem):
     chunks = action.shape[0] // LANES
     nodes = action.shape[1]
     copies = []
@@ -42,17 +51,32 @@
         copy = pltpu.make_async_copy(action.at[pl.ds(c * LANES, LANES), :], stage.at[c], sems.at[c])
         copy.start()
         copies.append(copy)
+    listed = pltpu.make_async_copy(send_hbm, send, send_sem)
+    listed.start()
     for c in range(chunks):
         copies[c].wait()
         field[pl.ds(PAD + c, nodes, stride=4), :] = stage[c].T
+    listed.wait()
     low = low_half()
-    ghost = to_upper.shape[0] // 4
+    far = odd("dom")
+    ghost = to_far.shape[0] // 4
     for i in range(0, ghost, 2):
-        to_upper[pl.ds(4 * i, 8), :] = two_rows(field, send[1, i] * 4, send[1, i + 1] * 4, low)
-        to_lower[pl.ds(4 * i, 8), :] = two_rows(field, send[0, i] * 4, send[0, i + 1] * 4, low)
-
-
-def weights_body(edge_angle, edge_speed, field, weight, base):
+        to_far[pl.ds(4 * i, 8), :] = two_rows(field, send[far, i] * 4, send[far, i + 1] * 4, low)
+        to_near[pl.ds(4 * i, 8), :] = two_rows(field, send[1 - far, i] * 4, send[1 - far, i + 1] * 4, low)
+
+
+def weights_body(
+    send, slots, angle_hbm, speed_hbm, field, weight, base, share_weight, share_base, share_slots,
+    edge_angle, edge_speed, sems,
+):
+    arriving = [
+        pltpu.make_async_copy(angle_hbm, edge_angle, sems.at[0]),
+        pltpu.make_async_copy(speed_hbm, edge_speed, sems.at[1]),
+    ]
+    for copy in arriving:
+        copy.start()
+    for copy in arriving:
+        copy.wait()
     sector = 16
     nodes = edge_angle.shape[1]
     freq = 4 * LANES // sector
@@ -87,30 +111,46 @@
     for c in range(4):
         rows = pl.ds(PAD + c, nodes, stride=4)
         base[rows, :] = field[rows, :] * wide[:, c * LANES : (c + 1) * LANES]
-
-
-def place_ghosts(field, lower, upper, nodes):
-    part = lax.axis_index("dom")
-    last = lax.axis_size("dom") - 1
-    rows = lower.shape[0]
-    field[pl.ds(PAD + 4 * nodes, rows), :] = jnp.where(part > 0, lower[...], 0.0)
-    field[pl.ds(PAD + 4 * nodes + rows, rows), :] = jnp.where(part < last, upper[...], 0.0)
-
-
-def shared_body(send, slots, field_in, lower, upper, weight, base, field, to_upper, to_lower):
-    del field_in
-    nodes = slots.shape[0] // NEIGH
-    place_ghosts(field, lower, upper, nodes)
     low = low_half()
-    ghost = to_upper.shape[0] // 4
-    for row, out in ((1, to_upper), (0, to_lower)):
+    far = odd("dom")
+    ghost = send.shape[1]
+    for k, row in enumerate((far, 1 - far)):
         for i in range(0, ghost, 2):
             n = send[row, i]
             m = send[row, i + 1]
-            total = two_rows(base, n * 4, m * 4, low)
+            s = k * ghost + i
+            share_base[pl.ds(4 * s, 8), :] = two_rows(base, n * 4, m * 4, low)
             for j in range(NEIGH):
-                w = two_rows(weight, n * 4 + j * 4 * nodes, m * 4 + j * 4 * nodes, low)
-                total = total + w * two_rows(field, slots[j * nodes + n], slots[j * nodes + m], low)
+                skip = j * 4 * nodes
+                share_weight[pl.ds((j * 2 * ghost + s) * 4, 8), :] = two_rows(weight, n * 4 + skip, m * 4 + skip, low)
+                share_slots[j * 2 * ghost + s] = slots[j * nodes + n]
+                share_slots[j * 2 * ghost + s + 1] = slots[j * nodes + m]
+
+
+def place_ghosts(field, from_far, from_near, nodes):
+    part = lax.axis_index("dom")
+    last = lax.axis_size("dom") - 1
+    rows = from_far.shape[0]
+    start = PAD + 4 * nodes
+    far = odd("dom")
+    inside = jnp.logical_and(part > 0, part < last)
+    field[pl.ds(pl.multiple_of(start + far * rows, 8), rows), :] = jnp.where(inside, from_far[...], 0.0)
+    field[pl.ds(pl.multiple_of(start + (1 - far) * rows, 8), rows), :] = from_near[...]
+
+
+def shared_body(slots, field_in, from_far, from_near, weight, base, field, to_far, to_near):
+    del field_in
+    ghost = to_far.shape[0] // 4
+    nodes = (field.shape[0] - 2 * PAD) // 4 - 2 * ghost
+    place_ghosts(field, from_far, from_near, nodes)
+    low = low_half()
+    for k, out in enumerate((to_far, to_near)):
+        for i in range(0, ghost, 2):
+            s = k * ghost + i
+            total = base[pl.ds(4 * s, 8), :]
+            for j in range(NEIGH):
+                at = j * 2 * ghost + s
+                total = total + weight[pl.ds(4 * at, 8), :] * two_rows(field, slots[at], slots[at + 1], low)
             out[pl.ds(4 * i, 8), :] = total
 
 
@@ -134,19 +174,19 @@
     sweep_rows(slots, field, weight, base, out, slots.shape[0] // NEIGH, PAD)
 
 
-def last_body(slots, field_in, lower, upper, weight, base, field, swept, first, last, rows):
+def last_body(slots, field_in, from_far, from_near, weight, base, field, swept, to_far, to_near, rows):
     del field_in
     nodes = slots.shape[0] // NEIGH
-    place_ghosts(field, lower, upper, nodes)
+    place_ghosts(field, from_far, from_near, nodes)
     sweep_rows(slots, field, weight, base, rows, nodes, 0)
-    freq = first.shape[0]
+    freq = to_far.shape[0]
     for c in range(4):
-        planes = rows[pl.ds(c, nodes, stride=4), :].T
-        swept[pl.ds(c * LANES, LANES), :] = planes
-        if c == 0:
-            first[...] = planes[:freq, :]
-        if c == 3:
-            last[...] = planes[LANES - freq :, :]
+        swept[pl.ds(c * LANES, LANES), :] = rows[pl.ds(c, nodes, stride=4), :].T
+    first = swept[pl.ds(0, freq), :]
+    last = swept[pl.ds(swept.shape[0] - freq, freq), :]
+    far = odd("dir") > 0
+    to_far[...] = jnp.where(far, last, first)
+    to_near[...] = jnp.where(far, first, last)
 
 
 def finished(plane, before, after, direction, rate, bearing, shift):
@@ -180,16 +220,17 @@
     copy.wait()
 
 
-def edge_body(swept, before, after, rate, bearing, shift, out_in, out, stage, sem):
+def edge_body(swept, from_far, from_near, rate, bearing, shift, out_in, out, stage, sem):
     del out_in
+    far = odd("dir") > 0
     freq, nodes = rate.shape
     sector = swept.shape[0] // freq
     first = jnp.full((1, nodes), lax.axis_index("dir") * sector, jnp.int32)
     copies = []
     for k, d in enumerate((0, sector - 1)):
         plane = swept[pl.ds(d * freq, freq), :]
-        low = before[...] if d == 0 else swept[pl.ds((d - 1) * freq, freq), :]
-        high = after[...] if d == sector - 1 else swept[pl.ds((d + 1) * freq, freq), :]
+        low = jnp.where(far, from_near[...], from_far[...]) if d == 0 else swept[pl.ds((d - 1) * freq, freq), :]
+        high = jnp.where(far, from_far[...], from_near[...]) if d == sector - 1 else swept[pl.ds((d + 1) * freq, freq), :]
         stage[k] = finished(plane, low, high, first + d, rate[...], bearing[...], shift[...])
         copy = pltpu.make_async_copy(stage.at[k], out.at[pl.ds(d * freq, freq), :], sem.at[k])
         copy.start()
@@ -198,9 +239,16 @@
         copy.wait()
 
 
-def around(array, axis, by):
+def swap_far(array, axis, closed):
     count = lax.axis_size(axis)
-    return lax.ppermute(array, axis, [(i, (i + by) % count) for i in range(count)])
+    ends = [(count - 1, 0), (0, count - 1)] if closed else [(0, 0), (count - 1, count - 1)]
+    pairs = [p for i in range(1, count - 1, 2) for p in ((i, i + 1), (i + 1, i))]
+    return lax.ppermute(array, axis, pairs + ends)
+
+
+def swap_near(array, axis):
+    count = lax.axis_size(axis)
+    return lax.ppermute(array, axis, [p for i in range(0, count, 2) for p in ((i, i + 1), (i + 1, i))])
 
 
 def shards(
@@ -217,39 +265,55 @@
     slots = (neighbours * 4).reshape(-1)
     bearing = refract_angle.reshape(1, nodes)
 
-    field, up, down = pl.pallas_call(
+    field, far, near = pl.pallas_call(
         rows_body,
         out_shape=(fields, shares, shares),
-        in_specs=[SMEM, ANY],
+        in_specs=[HBM, HBM],
         out_specs=(VMEM, VMEM, VMEM),
-        scratch_shapes=[pltpu.VMEM((4, LANES, nodes), F32), pltpu.SemaphoreType.DMA((4,))],
+        scratch_shapes=[
+            pltpu.VMEM((4, LANES, nodes), F32),
+            pltpu.SMEM((2, ghost), jnp.int32),
+            pltpu.SemaphoreType.DMA((4,)),
+            pltpu.SemaphoreType.DMA,
+        ],
         compiler_params=params(),
         name="rows",
-    )(send_rows, action.reshape(columns, nodes))
-    lower = around(up, "dom", 1)
-    upper = around(down, "dom", -1)
-    weight, base = pl.pallas_call(
+    )(in_hbm(send_rows), in_hbm(action.reshape(columns, nodes)))
+    far = swap_far(far, "dom", False)
+    near = swap_near(near, "dom")
+    weight, base, share_weight, share_base, share_slots = pl.pallas_call(
         weights_body,
-        out_shape=(weights, bases),
-        in_specs=[VMEM] * 3,
-        out_specs=(VMEM, VMEM),
+        out_shape=(
+            weights,
+            bases,
+            jax.ShapeDtypeStruct((NEIGH * 8 * ghost, LANES), F32),
+            jax.ShapeDtypeStruct((8 * ghost, LANES), F32),
+            jax.ShapeDtypeStruct((NEIGH * 2 * ghost,), jnp.int32),
+        ),
+        in_specs=[SMEM, SMEM, HBM, HBM, VMEM],
+        out_specs=(VMEM, VMEM, VMEM, VMEM, SMEM),
+        scratch_shapes=[
+            pltpu.VMEM((NEIGH, nodes), F32),
+            pltpu.VMEM((NEIGH, nodes), F32),
+            pltpu.SemaphoreType.DMA((2,)),
+        ],
         compiler_params=params(),
         cost_estimate=cost(1 << 30, 8 << 20),
         name="weights",
-    )(edge_angle, edge_speed, field)
+    )(send_rows, slots, in_hbm(edge_angle), in_hbm(edge_speed), field)
 
     for _ in range(2):
-        field, up, down = pl.pallas_call(
+        field, far, near = pl.pallas_call(
             shared_body,
             out_shape=(fields, shares, shares),
-            in_specs=[SMEM, SMEM] + [VMEM] * 5,
+            in_specs=[SMEM] + [VMEM] * 5,
             out_specs=(VMEM, VMEM, VMEM),
-            input_output_aliases={2: 0},
+            input_output_aliases={1: 0},
             compiler_params=params(),
             name="shared",
-        )(send_rows, slots, field, lower, upper, weight, base)
-        lower = around(up, "dom", 1)
-        upper = around(down, "dom", -1)
+        )(share_slots, field, far, near, share_weight, share_base)
+        far = swap_far(far, "dom", False)
+        near = swap_near(near, "dom")
         field = pl.pallas_call(
             sweep_body,
             out_shape=fields,
@@ -262,7 +326,7 @@
 
     edge = jax.ShapeDtypeStruct((freq, nodes), F32)
     plane_shape = jax.ShapeDtypeStruct((columns, nodes), F32)
-    _, swept, first, last = pl.pallas_call(
+    _, swept, far_plane, near_plane = pl.pallas_call(
         last_body,
         out_shape=(fields, plane_shape, edge, edge),
         in_specs=[SMEM] + [VMEM] * 5,
@@ -271,9 +335,9 @@
         scratch_shapes=[pltpu.VMEM((4 * nodes, LANES), F32)],
         compiler_params=params(),
         name="last_sweep",
-    )(slots, field, lower, upper, weight, base)
-    before = around(last, "dir", 1)
-    after = around(first, "dir", -1)
+    )(slots, field, far, near, weight, base)
+    far_plane = swap_far(far_plane, "dir", True)
+    near_plane = swap_near(near_plane, "dir")
     out = pl.pallas_call(
         inner_body,
         out_shape=plane_shape,
@@ -293,7 +357,7 @@
         scratch_shapes=[pltpu.VMEM((2, freq, nodes), F32), pltpu.SemaphoreType.DMA((2,))],
         compiler_params=params(),
         name="edge_planes",
-    )(swept, before, after, refract_rate, bearing, shift_rate, out)
+    )(swept, far_plane, near_plane, refract_rate, bearing, shift_rate, out)
     return out.reshape(sector, freq, nodes)
 
 

time: 52.8 us -> 46.5 us (0.88)
  the two profiles are of different devices: /device:TPU:1 before, /device:TPU:129 now
where the time goes in v2:
time: 46.5 us; the launch traced here: 46 us
  Pallas kernels  21.3 us (46%)
  starting transfers between devices  19.8 us (43%)
  waiting for transfers between devices  3.25 us (7%)
  other arithmetic  0.72 us (2%)
  local copies, waits for them, and re-layouts  0.7 us (2%)
    ppermute x4, starting transfers between devices, swap_far(): return lax.ppermute(array, axis, pairs + ends)  19.6 us
    pallas_call x2, Pallas kernels, shards(): pl.pallas_call(sweep_body, out_shape=fields, in_specs=[SMEM] + [VMEM] * 3...  6.94 us
    pallas_call x1, Pallas kernels, shards(): pl.pallas_call(weights_body, out_shape=(weights, bases, jax.ShapeDtypeStr...  4.48 us
    pallas_call x1, Pallas kernels, shards(): pl.pallas_call(last_body, out_shape=(fields, plane_shape, edge, edge), in...  3.84 us
    ppermute x4, waiting for transfers between devices, swap_far(): return lax.ppermute(array, axis, pairs + ends)  3.24 us
    pallas_call x1, Pallas kernels, shards(): pl.pallas_call(inner_body, out_shape=plane_shape, in_specs=[VMEM] * 4, ou...  1.95 us
    pallas_call x2, Pallas kernels, shards(): pl.pallas_call(shared_body, out_shape=(fields, shares, shares), in_specs=...  1.7 us
    pallas_call x1, Pallas kernels, shards(): pl.pallas_call(rows_body, out_shape=(fields, shares, shares), in_specs=[H...  1.62 us
  transfers between devices with their start and end apart: 8, of which 3 were waited for; matrix products, arithmetic and copies ran while one was open for 2% of the time, Pallas kernels for 29%

profile of v2, /device:TPU:129, one launch (start us, length us, event | category | flops | bytes accessed | tf_op | source)
XLA Modules:
  0.0 46.0 jit_solution(5566437203182468113)
XLA Ops:
  0.0 1.6 %rows.1 = (f32[2320,128]{1,0:T(8,128)S(1)}, f32[128,128]{1,0:T(8,128)S(1)}, f32[128,128]{1,0:T(8,128)S(1)}) custom-call(s32[2,32]{1,0:T(2,128)} %send.1, f32[512,512]{1,0:T(8,128)} %bitcast.5), custom_call_target="tpu_custom_call" | custom-call | tf_op jit(solution)/shard_map/rows/pallas_call | solution.py:268
  1.6 5.1 %collective-permute-start = (f32[128,128]{1,0:T(8,128)S(1)}, f32[128,128]{1,0:T(8,128)S(1)}, u32[]{:S(2)}, u32[]{:S(2)}) collective-permute-start(f32[128,128]{1,0:T(8,128)S(1)} %get-tuple-element.24), channel_id=1, source_target_pairs={{4,8},{8,4},{12,16},{16,12},{20,24},{24,20},{28,32},{32,28},{36,40... | collective-permute-start | bytes 196616 | tf_op jit(solution)/shard_map/ppermute | solution.py:246
  6.8 0.1 collective-permute-start.1
  6.9 0.7 %broadcast_multiply_fusion = s32[6,512]{1,0:T(8,128)S(1)} fusion(s32[6,512]{1,0:T(8,128)} %param.11), kind=kLoop, calls=%fused_computation | loop fusion | flops 3072 | bytes 24576 | tf_op jit(solution)/shard_map/mul | solution.py:265
  7.6 0.7 %copy-done.3 = s32[2,32]{1,0:T(2,128)S(1)} copy-done((s32[2,32]{1,0:T(2,128)S(1)}, s32[2,32]{1,0:T(2,128)}, u32[]{:S(2)}) %copy-start.3) | copy-done | bytes 280
  8.3 4.5 %weights.1 = (f32[12304,128]{1,0:T(8,128)S(1)}, f32[2064,128]{1,0:T(8,128)S(1)}, f32[1536,128]{1,0:T(8,128)S(1)}, f32[256,128]{1,0:T(8,128)S(1)}, s32[384]{0:T(512)S(1)}) custom-call(s32[2,32]{1,0:T(2,128)S(1)} %copy-done.3, s32[3072]{0:T(1024)S(1)} %reshape.12.slots, f32[6,512]{1,0:T(8,128)} %angle_hbm.1, f32[6,512]{1,0:T(8,128)} %speed_hbm.1, ...), custom_call_target="tpu_custom_call" | custom-call | flops 1073741824 | bytes 8388608 | tf_op jit(solution)/shard_map/weights/pallas_call | solution.py:284
  12.8 0.0 collective-permute-done.from_far
  12.8 0.0 collective-permute-done.1.from_near
  12.8 0.9 %shared.2 = (f32[2320,128]{1,0:T(8,128)S(1)}, f32[128,128]{1,0:T(8,128)S(1)}, f32[128,128]{1,0:T(8,128)S(1)}) custom-call(s32[384]{0:T(512)S(1)} %get-tuple-element.23.slots, f32[2320,128]{1,0:T(8,128)S(1)} %get-tuple-element.22.field.field_in, f32[128,128]{1,0:T(8,128)S(1)} %collective-permute-done.from_far, ...), custom_call_target="tpu_custom_call", output_to_operand_aliasing={{0}: (1, {})} | custom-call | tf_op jit(solution)/shard_map/shared/pallas_call | solution.py:306
  13.6 4.4 %collective-permute-start.2 = (f32[128,128]{1,0:T(8,128)S(1)}, f32[128,128]{1,0:T(8,128)S(1)}, u32[]{:S(2)}, u32[]{:S(2)}) collective-permute-start(f32[128,128]{1,0:T(8,128)S(1)} %get-tuple-element.31), channel_id=1, source_target_pairs={{4,8},{8,4},{12,16},{16,12},{20,24},{24,20},{28,32},{32,28},{36,40... | collective-permute-start | bytes 196616 | tf_op jit(solution)/shard_map/ppermute | solution.py:246
  18.0 0.1 collective-permute-start.3
  18.1 3.5 %sweep.2.field_in = f32[2320,128]{1,0:T(8,128)S(1)} custom-call(s32[3072]{0:T(1024)S(1)} %reshape.12.slots, f32[2320,128]{1,0:T(8,128)S(1)} %get-tuple-element.28.field, f32[12304,128]{1,0:T(8,128)S(1)} %get-tuple-element.29.weight, f32[2064,128]{1,0:T(8,128)S(1)} %get-tuple-element.30.base), custom_call_target="tpu_custom_call" | custom-call | flops 1073741824 | bytes 8388608 | tf_op jit(solution)/shard_map/sweep/pallas_call | solution.py:317
  21.6 1.3 %collective-permute-done.2.from_far = f32[128,128]{1,0:T(8,128)S(1)} collective-permute-done((f32[128,128]{1,0:T(8,128)S(1)}, f32[128,128]{1,0:T(8,128)S(1)}, u32[]{:S(2)}, u32[]{:S(2)}) %collective-permute-start.2) | collective-permute-done | bytes 65568 | tf_op jit(solution)/shard_map/ppermute | solution.py:246
  22.9 0.0 collective-permute-done.3.from_near
  22.9 0.9 %shared.3 = (f32[2320,128]{1,0:T(8,128)S(1)}, f32[128,128]{1,0:T(8,128)S(1)}, f32[128,128]{1,0:T(8,128)S(1)}) custom-call(s32[384]{0:T(512)S(1)} %get-tuple-element.23.slots, f32[2320,128]{1,0:T(8,128)S(1)} %sweep.2.field_in, f32[128,128]{1,0:T(8,128)S(1)} %collective-permute-done.2.from_far, ...), custom_call_target="tpu_custom_call", output_to_operand_aliasing={{0}: (1, {})} | custom-call | tf_op jit(solution)/shard_map/shared/pallas_call | solution.py:306
  23.7 4.4 %collective-permute-start.4 = (f32[128,128]{1,0:T(8,128)S(1)}, f32[128,128]{1,0:T(8,128)S(1)}, u32[]{:S(2)}, u32[]{:S(2)}) collective-permute-start(f32[128,128]{1,0:T(8,128)S(1)} %get-tuple-element.34), channel_id=1, source_target_pairs={{4,8},{8,4},{12,16},{16,12},{20,24},{24,20},{28,32},{32,28},{36,40... | collective-permute-start | bytes 196616 | tf_op jit(solution)/shard_map/ppermute | solution.py:246
  28.1 0.1 collective-permute-start.5
  28.2 3.5 %sweep.3.field_in = f32[2320,128]{1,0:T(8,128)S(1)} custom-call(s32[3072]{0:T(1024)S(1)} %reshape.12.slots, f32[2320,128]{1,0:T(8,128)S(1)} %get-tuple-element.33.field, f32[12304,128]{1,0:T(8,128)S(1)} %get-tuple-element.29.weight, f32[2064,128]{1,0:T(8,128)S(1)} %get-tuple-element.30.base), custom_call_target="tpu_custom_call" | custom-call | flops 1073741824 | bytes 8388608 | tf_op jit(solution)/shard_map/sweep/pallas_call | solution.py:317
  31.7 0.0 copy-start
  31.7 0.0 copy-start.1
  31.7 0.0 copy-start.2
  31.7 1.2 %collective-permute-done.4.from_far = f32[128,128]{1,0:T(8,128)S(1)} collective-permute-done((f32[128,128]{1,0:T(8,128)S(1)}, f32[128,128]{1,0:T(8,128)S(1)}, u32[]{:S(2)}, u32[]{:S(2)}) %collective-permute-start.4) | collective-permute-done | bytes 65568 | tf_op jit(solution)/shard_map/ppermute | solution.py:246
  32.9 0.0 collective-permute-done.5.from_near
  32.9 3.8 %last_sweep.1 = (f32[2320,128]{1,0:T(8,128)S(1)}, f32[512,512]{1,0:T(8,128)S(1)}, f32[32,512]{1,0:T(8,128)S(1)}, f32[32,512]{1,0:T(8,128)S(1)}) custom-call(s32[3072]{0:T(1024)S(1)} %reshape.12.slots, f32[2320,128]{1,0:T(8,128)S(1)} %sweep.3.field_in, f32[128,128]{1,0:T(8,128)S(1)} %collective-permute-done.4.from_far, ...), custom_call_target="tpu_custom_call", output_to_operand_aliasing={{0}: (1, {})} | custom-call | tf_op jit(solution)/shard_map/last_sweep/pallas_call | solution.py:329
  36.8 5.7 %collective-permute-start.6 = (f32[32,512]{1,0:T(8,128)S(1)}, f32[32,512]{1,0:T(8,128)S(1)}, u32[]{:S(2)}, u32[]{:S(2)}) collective-permute-start(f32[32,512]{1,0:T(8,128)S(1)} %get-tuple-element.37), channel_id=1, source_target_pairs={{1,2},{2,1},{3,0},{0,3},{5,6},{6,5},{7,4},{4,7},{9,10},{10,9},{11,... | collective-permute-start | bytes 196616 | tf_op jit(solution)/shard_map/ppermute | solution.py:246
  42.5 0.0 collective-permute-start.7
  42.5 0.0 copy-done
  42.5 0.0 copy-done.1
  42.5 1.9 %inner_planes.1.out_in = f32[512,512]{1,0:T(8,128)} custom-call(f32[512,512]{1,0:T(8,128)S(1)} %get-tuple-element.36.swept, f32[32,512]{1,0:T(8,128)S(1)} %copy-done, f32[1,512]{1,0:T(1,128)S(1)} %bitcast.3, f32[32,512]{1,0:T(8,128)S(1)} %copy-done.1), custom_call_target="tpu_custom_call" | custom-call | flops 268435456 | bytes 2097152 | tf_op jit(solution)/shard_map/inner_planes/pallas_call | solution.py:341
  44.4 0.7 %collective-permute-done.6.from_far = f32[32,512]{1,0:T(8,128)S(1)} collective-permute-done((f32[32,512]{1,0:T(8,128)S(1)}, f32[32,512]{1,0:T(8,128)S(1)}, u32[]{:S(2)}, u32[]{:S(2)}) %collective-permute-start.6) | collective-permute-done | bytes 65568 | tf_op jit(solution)/shard_map/ppermute | solution.py:246
  45.2 0.0 collective-permute-done.7.from_near
  45.2 0.8 %edge_planes.1 = f32[512,512]{1,0:T(8,128)} custom-call(f32[512,512]{1,0:T(8,128)S(1)} %get-tuple-element.36.swept, f32[32,512]{1,0:T(8,128)S(1)} %collective-permute-done.6.from_far, f32[32,512]{1,0:T(8,128)S(1)} %collective-permute-done.7.from_near, f32[32,512]{1,0:T(8,128)S(1)} %copy-done, f32[1,512]{1,0:T(1,128)S(1)} %bitcast.4, ...), custom_call_target="tpu_custom_call", output_to_operand_aliasing={{}: (6, {})} | custom-call | tf_op jit(solution)/shard_map/edge_planes/pallas_call | solution.py:351
  (3 shorter events, 0.0 us)
Async XLA Ops:
  1.6 11.1 %collective-permute-start = (f32[128,128]{1,0:T(8,128)S(1)}, f32[128,128]{1,0:T(8,128)S(1)}, u32[]{:S(2)}, u32[]{:S(2)}) collective-permute-start(f32[128,128]{1,0:T(8,128)S(1)} %get-tuple-element.24), channel_id=1, source_target_pairs={{4,8},{8,4},{12,16},{16,12},{20,24},{24,20},{28,32},{32,28},{36,40... | collective-permute-start | bytes 196616 | tf_op jit(solution)/shard_map/ppermute | solution.py:246
  6.8 6.0 %collective-permute-start.1 = (f32[128,128]{1,0:T(8,128)S(1)}, f32[128,128]{1,0:T(8,128)S(1)}, u32[]{:S(2)}, u32[]{:S(2)}) collective-permute-start(f32[128,128]{1,0:T(8,128)S(1)} %get-tuple-element.25), channel_id=1, source_target_pairs={{0,4},{4,0},{8,12},{12,8},{16,20},{20,16},{24,28},{28,24},{32,36},... | collective-permute-start | bytes 196616 | tf_op jit(solution)/shard_map/ppermute | solution.py:251
  7.6 0.7 %copy-start.3 = (s32[2,32]{1,0:T(2,128)S(1)}, s32[2,32]{1,0:T(2,128)}, u32[]{:S(2)}) copy-start(s32[2,32]{1,0:T(2,128)} %send.1) | copy-start | bytes 772
  13.6 9.2 %collective-permute-start.2 = (f32[128,128]{1,0:T(8,128)S(1)}, f32[128,128]{1,0:T(8,128)S(1)}, u32[]{:S(2)}, u32[]{:S(2)}) collective-permute-start(f32[128,128]{1,0:T(8,128)S(1)} %get-tuple-element.31), channel_id=1, source_target_pairs={{4,8},{8,4},{12,16},{16,12},{20,24},{24,20},{28,32},{32,28},{36,40... | collective-permute-start | bytes 196616 | tf_op jit(solution)/shard_map/ppermute | solution.py:246
  18.0 4.8 %collective-permute-start.3 = (f32[128,128]{1,0:T(8,128)S(1)}, f32[128,128]{1,0:T(8,128)S(1)}, u32[]{:S(2)}, u32[]{:S(2)}) collective-permute-start(f32[128,128]{1,0:T(8,128)S(1)} %get-tuple-element.32), channel_id=1, source_target_pairs={{0,4},{4,0},{8,12},{12,8},{16,20},{20,16},{24,28},{28,24},{32,36},... | collective-permute-start | bytes 196616 | tf_op jit(solution)/shard_map/ppermute | solution.py:251
  23.7 9.2 %collective-permute-start.4 = (f32[128,128]{1,0:T(8,128)S(1)}, f32[128,128]{1,0:T(8,128)S(1)}, u32[]{:S(2)}, u32[]{:S(2)}) collective-permute-start(f32[128,128]{1,0:T(8,128)S(1)} %get-tuple-element.34), channel_id=1, source_target_pairs={{4,8},{8,4},{12,16},{16,12},{20,24},{24,20},{28,32},{32,28},{36,40... | collective-permute-start | bytes 196616 | tf_op jit(solution)/shard_map/ppermute | solution.py:246
  28.1 4.8 %collective-permute-start.5 = (f32[128,128]{1,0:T(8,128)S(1)}, f32[128,128]{1,0:T(8,128)S(1)}, u32[]{:S(2)}, u32[]{:S(2)}) collective-permute-start(f32[128,128]{1,0:T(8,128)S(1)} %get-tuple-element.35), channel_id=1, source_target_pairs={{0,4},{4,0},{8,12},{12,8},{16,20},{20,16},{24,28},{28,24},{32,36},... | collective-permute-start | bytes 196616 | tf_op jit(solution)/shard_map/ppermute | solution.py:251
  31.7 10.8 %copy-start = (f32[32,512]{1,0:T(8,128)S(1)}, f32[32,512]{1,0:T(8,128)}, u32[]{:S(2)}) copy-start(f32[32,512]{1,0:T(8,128)} %rate.3) | copy-start | bytes 196612
  31.7 10.8 %copy-start.1 = (f32[32,512]{1,0:T(8,128)S(1)}, f32[32,512]{1,0:T(8,128)}, u32[]{:S(2)}) copy-start(f32[32,512]{1,0:T(8,128)} %shift.3) | copy-start | bytes 196612
  31.7 10.8 %copy-start.2 = (f32[512]{0:T(512)S(1)}, f32[512]{0:T(512)}, u32[]{:S(2)}) copy-start(f32[512]{0:T(512)} %param.14) | copy-start | bytes 6148
  36.8 8.4 %collective-permute-start.6 = (f32[32,512]{1,0:T(8,128)S(1)}, f32[32,512]{1,0:T(8,128)S(1)}, u32[]{:S(2)}, u32[]{:S(2)}) collective-permute-start(f32[32,512]{1,0:T(8,128)S(1)} %get-tuple-element.37), channel_id=1, source_target_pairs={{1,2},{2,1},{3,0},{0,3},{5,6},{6,5},{7,4},{4,7},{9,10},{10,9},{11,... | collective-permute-start | bytes 196616 | tf_op jit(solution)/shard_map/ppermute | solution.py:246
  42.5 2.7 %collective-permute-start.7 = (f32[32,512]{1,0:T(8,128)S(1)}, f32[32,512]{1,0:T(8,128)S(1)}, u32[]{:S(2)}, u32[]{:S(2)}) collective-permute-start(f32[32,512]{1,0:T(8,128)S(1)} %get-tuple-element.38), channel_id=1, source_target_pairs={{0,1},{1,0},{2,3},{3,2},{4,5},{5,4},{6,7},{7,6},{8,9},{9,8},{10,11... | collective-permute-start | bytes 196616 | tf_op jit(solution)/shard_map/ppermute | solution.py:251

commit v3 on v2

--- a/solution.py
+++ b/solution.py
@@ -43,7 +43,10 @@
     return lax.axis_index(axis) % 2
 
 
-def rows_body(send_hbm, action, field, to_far, to_near, stage, send, sems, send_sem):
+def rows_body(
+    send_hbm, action, angle_hbm, speed_hbm, neighbours, field, to_far, to_near, edge_angle, edge_speed, slots,
+    stage, send, listed, sems,
+):
     chunks = action.shape[0] // LANES
     nodes = action.shape[1]
     copies = []
@@ -51,12 +54,18 @@
         copy = pltpu.make_async_copy(action.at[pl.ds(c * LANES, LANES), :], stage.at[c], sems.at[c])
         copy.start()
         copies.append(copy)
-    listed = pltpu.make_async_copy(send_hbm, send, send_sem)
-    listed.start()
+    for k, (source, target) in enumerate(
+        ((send_hbm, send), (angle_hbm, edge_angle), (speed_hbm, edge_speed), (neighbours, listed))
+    ):
+        copy = pltpu.make_async_copy(source, target, sems.at[chunks + k])
+        copy.start()
+        copies.append(copy)
     for c in range(chunks):
         copies[c].wait()
         field[pl.ds(PAD + c, nodes, stride=4), :] = stage[c].T
-    listed.wait()
+    for copy in copies[chunks:]:
+        copy.wait()
+    slots[...] = listed[...] * 4
     low = low_half()
     far = odd("dom")
     ghost = to_far.shape[0] // 4
@@ -66,17 +75,10 @@
 
 
 def weights_body(
-    send, slots, angle_hbm, speed_hbm, field, weight, base, share_weight, share_base, share_slots,
-    edge_angle, edge_speed, sems,
+    send_hbm, slots, edge_angle, edge_speed, field, weight, base, share_weight, share_base, share_slots, send, sem
 ):
-    arriving = [
-        pltpu.make_async_copy(angle_hbm, edge_angle, sems.at[0]),
-        pltpu.make_async_copy(speed_hbm, edge_speed, sems.at[1]),
-    ]
-    for copy in arriving:
-        copy.start()
-    for copy in arriving:
-        copy.wait()
+    listed = pltpu.make_async_copy(send_hbm, send, sem)
+    listed.start()
     sector = 16
     nodes = edge_angle.shape[1]
     freq = 4 * LANES // sector
@@ -111,6 +113,7 @@
     for c in range(4):
         rows = pl.ds(PAD + c, nodes, stride=4)
         base[rows, :] = field[rows, :] * wide[:, c * LANES : (c + 1) * LANES]
+    listed.wait()
     low = low_half()
     far = odd("dom")
     ghost = send.shape[1]
@@ -123,8 +126,8 @@
             for j in range(NEIGH):
                 skip = j * 4 * nodes
                 share_weight[pl.ds((j * 2 * ghost + s) * 4, 8), :] = two_rows(weight, n * 4 + skip, m * 4 + skip, low)
-                share_slots[j * 2 * ghost + s] = slots[j * nodes + n]
-                share_slots[j * 2 * ghost + s + 1] = slots[j * nodes + m]
+                share_slots[j * 2 * ghost + s] = slots[j, n]
+                share_slots[j * 2 * ghost + s + 1] = slots[j, m]
 
 
 def place_ghosts(field, from_far, from_near, nodes):
@@ -162,7 +165,7 @@
         row = pl.multiple_of(i * 8, 8)
         total = base[pl.ds(PAD + row, 8), :]
         for j in range(NEIGH):
-            value = two_rows(field, slots[j * nodes + n], slots[j * nodes + n + 1], low)
+            value = two_rows(field, slots[j, n], slots[j, n + 1], low)
             total = total + weight[pl.ds(PAD + j * 4 * nodes + row, 8), :] * value
         out[pl.ds(offset + row, 8), :] = total
         return carry
@@ -171,12 +174,12 @@
 
 
 def sweep_body(slots, field, weight, base, out):
-    sweep_rows(slots, field, weight, base, out, slots.shape[0] // NEIGH, PAD)
+    sweep_rows(slots, field, weight, base, out, slots.shape[1], PAD)
 
 
 def last_body(slots, field_in, from_far, from_near, weight, base, field, swept, to_far, to_near, rows):
     del field_in
-    nodes = slots.shape[0] // NEIGH
+    nodes = slots.shape[1]
     place_ghosts(field, from_far, from_near, nodes)
     sweep_rows(slots, field, weight, base, rows, nodes, 0)
     freq = to_far.shape[0]
@@ -239,11 +242,22 @@
         copy.wait()
 
 
-def swap_far(array, axis, closed):
-    count = lax.axis_size(axis)
-    ends = [(count - 1, 0), (0, count - 1)] if closed else [(0, 0), (count - 1, count - 1)]
-    pairs = [p for i in range(1, count - 1, 2) for p in ((i, i + 1), (i + 1, i))]
-    return lax.ppermute(array, axis, pairs + ends)
+def swap_far_parts(array):
+    count, width = (lax.axis_size("dom"), lax.axis_size("dir"))
+    pairs = []
+    for d in range(width):
+        for i in range(1, count - 1, 2):
+            here, there = (i * width + d, (i + 1) * width + d)
+            pairs += [(here, there), (there, here)]
+        for i in (0, count - 1):
+            pairs.append((i * width + d, i * width + (d ^ 1)))
+    return lax.ppermute(array, ("dom", "dir"), pairs)
+
+
+def swap_far_sectors(array):
+    count = lax.axis_size("dir")
+    pairs = [p for i in range(1, count, 2) for p in ((i, (i + 1) % count), ((i + 1) % count, i))]
+    return lax.ppermute(array, "dir", pairs)
 
 
 def swap_near(array, axis):
@@ -262,24 +276,24 @@
     weights = jax.ShapeDtypeStruct((NEIGH * 4 * nodes + 2 * PAD, LANES), F32)
     bases = jax.ShapeDtypeStruct((4 * nodes + 2 * PAD, LANES), F32)
     columns = sector * freq
-    slots = (neighbours * 4).reshape(-1)
     bearing = refract_angle.reshape(1, nodes)
 
-    field, far, near = pl.pallas_call(
+    edges = jax.ShapeDtypeStruct((NEIGH, nodes), F32)
+    field, far, near, angle, speed, slots = pl.pallas_call(
         rows_body,
-        out_shape=(fields, shares, shares),
-        in_specs=[HBM, HBM],
-        out_specs=(VMEM, VMEM, VMEM),
+        out_shape=(fields, shares, shares, edges, edges, jax.ShapeDtypeStruct((NEIGH, nodes), jnp.int32)),
+        in_specs=[HBM] * 5,
+        out_specs=(VMEM,) * 6,
         scratch_shapes=[
             pltpu.VMEM((4, LANES, nodes), F32),
             pltpu.SMEM((2, ghost), jnp.int32),
-            pltpu.SemaphoreType.DMA((4,)),
-            pltpu.SemaphoreType.DMA,
+            pltpu.VMEM((NEIGH, nodes), jnp.int32),
+            pltpu.SemaphoreType.DMA((8,)),
         ],
         compiler_params=params(),
         name="rows",
-    )(in_hbm(send_rows), in_hbm(action.reshape(columns, nodes)))
-    far = swap_far(far, "dom", False)
+    )(*(in_hbm(x) for x in (send_rows, action.reshape(columns, nodes), edge_angle, edge_speed, neighbours)))
+    far = swap_far_parts(far)
     near = swap_near(near, "dom")
     weight, base, share_weight, share_base, share_slots = pl.pallas_call(
         weights_body,
@@ -290,17 +304,13 @@
             jax.ShapeDtypeStruct((8 * ghost, LANES), F32),
             jax.ShapeDtypeStruct((NEIGH * 2 * ghost,), jnp.int32),
         ),
-        in_specs=[SMEM, SMEM, HBM, HBM, VMEM],
+        in_specs=[HBM, SMEM] + [VMEM] * 3,
         out_specs=(VMEM, VMEM, VMEM, VMEM, SMEM),
-        scratch_shapes=[
-            pltpu.VMEM((NEIGH, nodes), F32),
-            pltpu.VMEM((NEIGH, nodes), F32),
-            pltpu.SemaphoreType.DMA((2,)),
-        ],
+        scratch_shapes=[pltpu.SMEM((2, ghost), jnp.int32), pltpu.SemaphoreType.DMA],
         compiler_params=params(),
         cost_estimate=cost(1 << 30, 8 << 20),
         name="weights",
-    )(send_rows, slots, in_hbm(edge_angle), in_hbm(edge_speed), field)
+    )(in_hbm(send_rows), slots, angle, speed, field)
 
     for _ in range(2):
         field, far, near = pl.pallas_call(
@@ -312,7 +322,7 @@
             compiler_params=params(),
             name="shared",
         )(share_slots, field, far, near, share_weight, share_base)
-        far = swap_far(far, "dom", False)
+        far = swap_far_parts(far)
         near = swap_near(near, "dom")
         field = pl.pallas_call(
             sweep_body,
@@ -336,7 +346,7 @@
         compiler_params=params(),
         name="last_sweep",
     )(slots, field, far, near, weight, base)
-    far_plane = swap_far(far_plane, "dir", True)
+    far_plane = swap_far_sectors(far_plane)
     near_plane = swap_near(near_plane, "dir")
     out = pl.pallas_call(
         inner_body,

time: 46.5 us -> 41.3 us (0.89)
  starting transfers between devices: 19.8 us -> 15.5 us
  Pallas kernels: 21.3 us -> 24.4 us
  waiting for transfers between devices: 3.25 us -> 1.15 us
  other arithmetic: 0.72 us -> 0 us
  local copies, waits for them, and re-layouts: 0.7 us -> 0.02 us
    ppermute x4, starting transfers between devices: 19.6 us -> 15.5 us  [the longest x3 9.29 us: swap_far_parts(): return lax.ppermute(array, ('dom', 'dir'), pairs)]
    pallas_call x2, Pallas kernels: 6.94 us -> 9.35 us  [shards(): pl.pallas_call(sweep_body, out_shape=fields, in_specs=[SMEM] + [VMEM] * 3...]
    ppermute x4, waiting for transfers between devices: 3.24 us -> 1.14 us  [the longest x1 0.79 us: swap_far_sectors(): return lax.ppermute(array, 'dir', pairs)]
    pallas_call x1, Pallas kernels: 3.84 us -> 5.08 us  [shards(): pl.pallas_call(last_body, out_shape=(fields, plane_shape, edge, edge), in...]
    mul x1 -> x0, other arithmetic: 0.72 us -> none  [shards(): slots = (neighbours * 4).reshape(-1)]
    pallas_call x1, Pallas kernels: 4.48 us -> 3.78 us  [shards(): pl.pallas_call(weights_body, out_shape=(weights, bases, jax.ShapeDtypeStr...]
    unnamed x8 -> x6, local copies, waits for them, and re-layouts: 0.7 us -> 0.02 us
  transfers between devices with their start and end apart: 8 -> 8, of which waited for: 3 -> 2; matrix products, arithmetic and copies ran while one was open for 2% -> 0% of each run, Pallas kernels for 29% -> 37%
where the time goes in v3:
time: 41.3 us; the launch traced here: 41.2 us
  Pallas kernels  24.4 us (59%)
  starting transfers between devices  15.5 us (38%)
  waiting for transfers between devices  1.15 us (3%)
    pallas_call x2, Pallas kernels, shards(): pl.pallas_call(sweep_body, out_shape=fields, in_specs=[SMEM] + [VMEM] * 3...  9.35 us
    ppermute x3, starting transfers between devices, swap_far_parts(): return lax.ppermute(array, ('dom', 'dir'), pairs)  9.29 us
    ppermute x1, starting transfers between devices, swap_far_sectors(): return lax.ppermute(array, 'dir', pairs)  6.23 us
    pallas_call x1, Pallas kernels, shards(): pl.pallas_call(last_body, out_shape=(fields, plane_shape, edge, edge), in...  5.08 us
    pallas_call x1, Pallas kernels, shards(): pl.pallas_call(weights_body, out_shape=(weights, bases, jax.ShapeDtypeStr...  3.78 us
    pallas_call x1, Pallas kernels, shards(): pl.pallas_call(inner_body, out_shape=plane_shape, in_specs=[VMEM] * 4, ou...  1.98 us
    pallas_call x2, Pallas kernels, shards(): pl.pallas_call(shared_body, out_shape=(fields, shares, shares), in_specs=...  1.7 us
    pallas_call x1, Pallas kernels, shards(): pl.pallas_call(rows_body, out_shape=(fields, shares, shares, edges, edges...  1.65 us
  transfers between devices with their start and end apart: 8, of which 2 were waited for; matrix products, arithmetic and copies ran while one was open for 0% of the time, Pallas kernels for 37%

profile of v3, /device:TPU:129, one launch (start us, length us, event | category | flops | bytes accessed | tf_op | source)
XLA Modules:
  0.0 41.2 jit_solution(9252695679878711317)
XLA Ops:
  0.0 1.7 %rows.1 = (f32[2320,128]{1,0:T(8,128)S(1)}, f32[128,128]{1,0:T(8,128)S(1)}, f32[128,128]{1,0:T(8,128)S(1)}, f32[6,512]{1,0:T(8,128)S(1)}, f32[6,512]{1,0:T(8,128)S(1)}, /*index=5*/s32[6,512]{1,0:T(8,128)S(1)}) custom-call(s32[2,32]{1,0:T(2,128)} %send_hbm.3, f32[512,512]{1,0:T(8,128)} %bitcast.5, f32[6,512]{1,0:T(8,128)} %angle_hbm.1, f32[6,512]{1,0:T(8,128)} %speed_hbm.1, ...), custom_call_target="tpu_custom_call" | custom-call | tf_op jit(solution)/shard_map/rows/pallas_call | solution.py:282
  1.7 3.3 %collective-permute-start = (f32[128,128]{1,0:T(8,128)S(1)}, f32[128,128]{1,0:T(8,128)S(1)}, u32[]{:S(2)}, u32[]{:S(2)}) collective-permute-start(f32[128,128]{1,0:T(8,128)S(1)} %get-tuple-element.30), channel_id=1, source_target_pairs={{4,8},{8,4},{12,16},{16,12},{20,24},{24,20},{28,32},{32,28},{36,40... | collective-permute-start | bytes 196616 | tf_op jit(solution)/shard_map/ppermute | solution.py:254
  5.0 0.0 collective-permute-start.1
  5.0 3.8 %weights.1 = (f32[12304,128]{1,0:T(8,128)S(1)}, f32[2064,128]{1,0:T(8,128)S(1)}, f32[1536,128]{1,0:T(8,128)S(1)}, f32[256,128]{1,0:T(8,128)S(1)}, s32[384]{0:T(512)S(1)}) custom-call(s32[2,32]{1,0:T(2,128)} %send_hbm.3, s32[6,512]{1,0:T(8,128)S(1)} %get-tuple-element.25.slots, f32[6,512]{1,0:T(8,128)S(1)} %get-tuple-element.26.edge_angle, ...), custom_call_target="tpu_custom_call" | custom-call | flops 1073741824 | bytes 8388608 | tf_op jit(solution)/shard_map/weights/pallas_call | solution.py:298
  8.7 0.3 collective-permute-done.from_far
  9.1 0.0 collective-permute-done.1.from_near
  9.1 0.8 %shared.2 = (f32[2320,128]{1,0:T(8,128)S(1)}, f32[128,128]{1,0:T(8,128)S(1)}, f32[128,128]{1,0:T(8,128)S(1)}) custom-call(s32[384]{0:T(512)S(1)} %get-tuple-element.29.slots, f32[2320,128]{1,0:T(8,128)S(1)} %get-tuple-element.28.field.field_in, f32[128,128]{1,0:T(8,128)S(1)} %collective-permute-done.from_far, ...), custom_call_target="tpu_custom_call", output_to_operand_aliasing={{0}: (1, {})} | custom-call | tf_op jit(solution)/shard_map/shared/pallas_call | solution.py:316
  9.9 3.3 %collective-permute-start.2 = (f32[128,128]{1,0:T(8,128)S(1)}, f32[128,128]{1,0:T(8,128)S(1)}, u32[]{:S(2)}, u32[]{:S(2)}) collective-permute-start(f32[128,128]{1,0:T(8,128)S(1)} %get-tuple-element.37), channel_id=1, source_target_pairs={{4,8},{8,4},{12,16},{16,12},{20,24},{24,20},{28,32},{32,28},{36,40... | collective-permute-start | bytes 196616 | tf_op jit(solution)/shard_map/ppermute | solution.py:254
  13.2 0.0 collective-permute-start.3
  13.2 4.7 %sweep.2.field_in = f32[2320,128]{1,0:T(8,128)S(1)} custom-call(s32[6,512]{1,0:T(8,128)S(1)} %get-tuple-element.25.slots, f32[2320,128]{1,0:T(8,128)S(1)} %get-tuple-element.34.field, f32[12304,128]{1,0:T(8,128)S(1)} %get-tuple-element.35.weight, f32[2064,128]{1,0:T(8,128)S(1)} %get-tuple-element.36.base), custom_call_target="tpu_custom_call" | custom-call | flops 1073741824 | bytes 8388608 | tf_op jit(solution)/shard_map/sweep/pallas_call | solution.py:327
  17.9 0.0 collective-permute-done.2.from_far
  17.9 0.0 collective-permute-done.3.from_near
  17.9 0.9 %shared.3 = (f32[2320,128]{1,0:T(8,128)S(1)}, f32[128,128]{1,0:T(8,128)S(1)}, f32[128,128]{1,0:T(8,128)S(1)}) custom-call(s32[384]{0:T(512)S(1)} %get-tuple-element.29.slots, f32[2320,128]{1,0:T(8,128)S(1)} %sweep.2.field_in, f32[128,128]{1,0:T(8,128)S(1)} %collective-permute-done.2.from_far, ...), custom_call_target="tpu_custom_call", output_to_operand_aliasing={{0}: (1, {})} | custom-call | tf_op jit(solution)/shard_map/shared/pallas_call | solution.py:316
  18.8 2.7 %collective-permute-start.4 = (f32[128,128]{1,0:T(8,128)S(1)}, f32[128,128]{1,0:T(8,128)S(1)}, u32[]{:S(2)}, u32[]{:S(2)}) collective-permute-start(f32[128,128]{1,0:T(8,128)S(1)} %get-tuple-element.40), channel_id=1, source_target_pairs={{4,8},{8,4},{12,16},{16,12},{20,24},{24,20},{28,32},{32,28},{36,40... | collective-permute-start | bytes 196616 | tf_op jit(solution)/shard_map/ppermute | solution.py:254
  21.5 0.0 collective-permute-start.5
  21.5 4.7 %sweep.3.field_in = f32[2320,128]{1,0:T(8,128)S(1)} custom-call(s32[6,512]{1,0:T(8,128)S(1)} %get-tuple-element.25.slots, f32[2320,128]{1,0:T(8,128)S(1)} %get-tuple-element.39.field, f32[12304,128]{1,0:T(8,128)S(1)} %get-tuple-element.35.weight, f32[2064,128]{1,0:T(8,128)S(1)} %get-tuple-element.36.base), custom_call_target="tpu_custom_call" | custom-call | flops 1073741824 | bytes 8388608 | tf_op jit(solution)/shard_map/sweep/pallas_call | solution.py:327
  26.2 0.0 copy-start
  26.2 0.0 copy-start.1
  26.2 0.0 copy-start.2
  26.2 0.0 collective-permute-done.4.from_far
  26.2 0.0 collective-permute-done.5.from_near
  26.3 5.1 %last_sweep.1 = (f32[2320,128]{1,0:T(8,128)S(1)}, f32[512,512]{1,0:T(8,128)S(1)}, f32[32,512]{1,0:T(8,128)S(1)}, f32[32,512]{1,0:T(8,128)S(1)}) custom-call(s32[6,512]{1,0:T(8,128)S(1)} %get-tuple-element.25.slots, f32[2320,128]{1,0:T(8,128)S(1)} %sweep.3.field_in, f32[128,128]{1,0:T(8,128)S(1)} %collective-permute-done.4.from_far, ...), custom_call_target="tpu_custom_call", output_to_operand_aliasing={{0}: (1, {})} | custom-call | tf_op jit(solution)/shard_map/last_sweep/pallas_call | solution.py:339
  31.3 6.2 %collective-permute-start.6 = (f32[32,512]{1,0:T(8,128)S(1)}, f32[32,512]{1,0:T(8,128)S(1)}, u32[]{:S(2)}, u32[]{:S(2)}) collective-permute-start(f32[32,512]{1,0:T(8,128)S(1)} %get-tuple-element.43), channel_id=1, source_target_pairs={{1,2},{2,1},{3,0},{0,3},{5,6},{6,5},{7,4},{4,7},{9,10},{10,9},{11,... | collective-permute-start | bytes 196616 | tf_op jit(solution)/shard_map/ppermute | solution.py:260
  37.6 0.0 collective-permute-start.7
  37.6 0.0 copy-done
  37.6 0.0 copy-done.1
  37.6 0.0 copy-done.2
  37.6 2.0 %inner_planes.1.out_in = f32[512,512]{1,0:T(8,128)} custom-call(f32[512,512]{1,0:T(8,128)S(1)} %get-tuple-element.42.swept, f32[32,512]{1,0:T(8,128)S(1)} %copy-done, f32[1,512]{1,0:T(1,128)S(1)} %bitcast.3, f32[32,512]{1,0:T(8,128)S(1)} %copy-done.1), custom_call_target="tpu_custom_call" | custom-call | flops 268435456 | bytes 2097152 | tf_op jit(solution)/shard_map/inner_planes/pallas_call | solution.py:351
  39.6 0.8 %collective-permute-done.6.from_far = f32[32,512]{1,0:T(8,128)S(1)} collective-permute-done((f32[32,512]{1,0:T(8,128)S(1)}, f32[32,512]{1,0:T(8,128)S(1)}, u32[]{:S(2)}, u32[]{:S(2)}) %collective-permute-start.6) | collective-permute-done | bytes 65568 | tf_op jit(solution)/shard_map/ppermute | solution.py:260
  40.4 0.0 collective-permute-done.7.from_near
  40.4 0.8 %edge_planes.1 = f32[512,512]{1,0:T(8,128)} custom-call(f32[512,512]{1,0:T(8,128)S(1)} %get-tuple-element.42.swept, f32[32,512]{1,0:T(8,128)S(1)} %collective-permute-done.6.from_far, f32[32,512]{1,0:T(8,128)S(1)} %collective-permute-done.7.from_near, f32[32,512]{1,0:T(8,128)S(1)} %copy-done, f32[1,512]{1,0:T(1,128)S(1)} %bitcast.4, ...), custom_call_target="tpu_custom_call", output_to_operand_aliasing={{}: (6, {})} | custom-call | tf_op jit(solution)/shard_map/edge_planes/pallas_call | solution.py:361
Async XLA Ops:
  1.7 7.4 %collective-permute-start = (f32[128,128]{1,0:T(8,128)S(1)}, f32[128,128]{1,0:T(8,128)S(1)}, u32[]{:S(2)}, u32[]{:S(2)}) collective-permute-start(f32[128,128]{1,0:T(8,128)S(1)} %get-tuple-element.30), channel_id=1, source_target_pairs={{4,8},{8,4},{12,16},{16,12},{20,24},{24,20},{28,32},{32,28},{36,40... | collective-permute-start | bytes 196616 | tf_op jit(solution)/shard_map/ppermute | solution.py:254
  5.0 4.1 %collective-permute-start.1 = (f32[128,128]{1,0:T(8,128)S(1)}, f32[128,128]{1,0:T(8,128)S(1)}, u32[]{:S(2)}, u32[]{:S(2)}) collective-permute-start(f32[128,128]{1,0:T(8,128)S(1)} %get-tuple-element.31), channel_id=1, source_target_pairs={{0,4},{4,0},{8,12},{12,8},{16,20},{20,16},{24,28},{28,24},{32,36},... | collective-permute-start | bytes 196616 | tf_op jit(solution)/shard_map/ppermute | solution.py:265
  9.9 8.0 %collective-permute-start.2 = (f32[128,128]{1,0:T(8,128)S(1)}, f32[128,128]{1,0:T(8,128)S(1)}, u32[]{:S(2)}, u32[]{:S(2)}) collective-permute-start(f32[128,128]{1,0:T(8,128)S(1)} %get-tuple-element.37), channel_id=1, source_target_pairs={{4,8},{8,4},{12,16},{16,12},{20,24},{24,20},{28,32},{32,28},{36,40... | collective-permute-start | bytes 196616 | tf_op jit(solution)/shard_map/ppermute | solution.py:254
  13.2 4.7 %collective-permute-start.3 = (f32[128,128]{1,0:T(8,128)S(1)}, f32[128,128]{1,0:T(8,128)S(1)}, u32[]{:S(2)}, u32[]{:S(2)}) collective-permute-start(f32[128,128]{1,0:T(8,128)S(1)} %get-tuple-element.38), channel_id=1, source_target_pairs={{0,4},{4,0},{8,12},{12,8},{16,20},{20,16},{24,28},{28,24},{32,36},... | collective-permute-start | bytes 196616 | tf_op jit(solution)/shard_map/ppermute | solution.py:265
  18.8 7.4 %collective-permute-start.4 = (f32[128,128]{1,0:T(8,128)S(1)}, f32[128,128]{1,0:T(8,128)S(1)}, u32[]{:S(2)}, u32[]{:S(2)}) collective-permute-start(f32[128,128]{1,0:T(8,128)S(1)} %get-tuple-element.40), channel_id=1, source_target_pairs={{4,8},{8,4},{12,16},{16,12},{20,24},{24,20},{28,32},{32,28},{36,40... | collective-permute-start | bytes 196616 | tf_op jit(solution)/shard_map/ppermute | solution.py:254
  21.5 4.7 %collective-permute-start.5 = (f32[128,128]{1,0:T(8,128)S(1)}, f32[128,128]{1,0:T(8,128)S(1)}, u32[]{:S(2)}, u32[]{:S(2)}) collective-permute-start(f32[128,128]{1,0:T(8,128)S(1)} %get-tuple-element.41), channel_id=1, source_target_pairs={{0,4},{4,0},{8,12},{12,8},{16,20},{20,16},{24,28},{28,24},{32,36},... | collective-permute-start | bytes 196616 | tf_op jit(solution)/shard_map/ppermute | solution.py:265
  26.2 11.4 %copy-start = (f32[32,512]{1,0:T(8,128)S(1)}, f32[32,512]{1,0:T(8,128)}, u32[]{:S(2)}) copy-start(f32[32,512]{1,0:T(8,128)} %rate.3) | copy-start | bytes 196612
  26.2 11.4 %copy-start.1 = (f32[32,512]{1,0:T(8,128)S(1)}, f32[32,512]{1,0:T(8,128)}, u32[]{:S(2)}) copy-start(f32[32,512]{1,0:T(8,128)} %shift.3) | copy-start | bytes 196612
  26.2 11.4 %copy-start.2 = (f32[512]{0:T(512)S(1)}, f32[512]{0:T(512)}, u32[]{:S(2)}) copy-start(f32[512]{0:T(512)} %param.14) | copy-start | bytes 6148
  31.3 9.0 %collective-permute-start.6 = (f32[32,512]{1,0:T(8,128)S(1)}, f32[32,512]{1,0:T(8,128)S(1)}, u32[]{:S(2)}, u32[]{:S(2)}) collective-permute-start(f32[32,512]{1,0:T(8,128)S(1)} %get-tuple-element.43), channel_id=1, source_target_pairs={{1,2},{2,1},{3,0},{0,3},{5,6},{6,5},{7,4},{4,7},{9,10},{10,9},{11,... | collective-permute-start | bytes 196616 | tf_op jit(solution)/shard_map/ppermute | solution.py:260
  37.6 2.8 %collective-permute-start.7 = (f32[32,512]{1,0:T(8,128)S(1)}, f32[32,512]{1,0:T(8,128)S(1)}, u32[]{:S(2)}, u32[]{:S(2)}) collective-permute-start(f32[32,512]{1,0:T(8,128)S(1)} %get-tuple-element.44), channel_id=1, source_target_pairs={{0,1},{1,0},{2,3},{3,2},{4,5},{5,4},{6,7},{7,6},{8,9},{9,8},{10,11... | collective-permute-start | bytes 196616 | tf_op jit(solution)/shard_map/ppermute | solution.py:265

commit v4 on v3

--- a/solution.py
+++ b/solution.py
@@ -65,7 +65,10 @@
         field[pl.ds(PAD + c, nodes, stride=4), :] = stage[c].T
     for copy in copies[chunks:]:
         copy.wait()
-    slots[...] = listed[...] * 4
+    for j in range(NEIGH):
+        for c in range(nodes // LANES):
+            at = j * (nodes // LANES) + c
+            slots[pl.ds(at, 1), :] = listed[pl.ds(j, 1), c * LANES : (c + 1) * LANES] * 4
     low = low_half()
     far = odd("dom")
     ghost = to_far.shape[0] // 4
@@ -126,8 +129,8 @@
             for j in range(NEIGH):
                 skip = j * 4 * nodes
                 share_weight[pl.ds((j * 2 * ghost + s) * 4, 8), :] = two_rows(weight, n * 4 + skip, m * 4 + skip, low)
-                share_slots[j * 2 * ghost + s] = slots[j, n]
-                share_slots[j * 2 * ghost + s + 1] = slots[j, m]
+                share_slots[j * 2 * ghost + s] = slots[j * nodes + n]
+                share_slots[j * 2 * ghost + s + 1] = slots[j * nodes + m]
 
 
 def place_ghosts(field, from_far, from_near, nodes):
@@ -165,7 +168,7 @@
         row = pl.multiple_of(i * 8, 8)
         total = base[pl.ds(PAD + row, 8), :]
         for j in range(NEIGH):
-            value = two_rows(field, slots[j, n], slots[j, n + 1], low)
+            value = two_rows(field, slots[j * nodes + n], slots[j * nodes + n + 1], low)
             total = total + weight[pl.ds(PAD + j * 4 * nodes + row, 8), :] * value
         out[pl.ds(offset + row, 8), :] = total
         return carry
@@ -174,19 +177,17 @@
 
 
 def sweep_body(slots, field, weight, base, out):
-    sweep_rows(slots, field, weight, base, out, slots.shape[1], PAD)
-
-
-def last_body(slots, field_in, from_far, from_near, weight, base, field, swept, to_far, to_near, rows):
+    sweep_rows(slots, field, weight, base, out, slots.shape[0] // NEIGH, PAD)
+
+
+def last_body(slots, field_in, from_far, from_near, weight, base, field, rows, to_far, to_near):
     del field_in
-    nodes = slots.shape[1]
+    nodes = slots.shape[0] // NEIGH
     place_ghosts(field, from_far, from_near, nodes)
     sweep_rows(slots, field, weight, base, rows, nodes, 0)
     freq = to_far.shape[0]
-    for c in range(4):
-        swept[pl.ds(c * LANES, LANES), :] = rows[pl.ds(c, nodes, stride=4), :].T
-    first = swept[pl.ds(0, freq), :]
-    last = swept[pl.ds(swept.shape[0] - freq, freq), :]
+    first = rows[pl.ds(0, nodes, stride=4), :].T[:freq, :]
+    last = rows[pl.ds(3, nodes, stride=4), :].T[LANES - freq :, :]
     far = odd("dir") > 0
     to_far[...] = jnp.where(far, last, first)
     to_near[...] = jnp.where(far, first, last)
@@ -203,37 +204,53 @@
     return value - (jnp.maximum(shift, 0.0) * (value - under) + jnp.minimum(shift, 0.0) * (over - value))
 
 
-def inner_body(swept, rate, bearing, shift, out, stage, sem):
+def inner_body(rows, rate, bearing, shift, out, ends, swept, stage, sems):
     freq, nodes = rate.shape
-    sector = swept.shape[0] // freq
+    chunks = swept.shape[0] // LANES
+    width = LANES // freq
+    sector = chunks * width
     first = jnp.full((1, nodes), lax.axis_index("dir") * sector, jnp.int32)
-    for d in range(1, sector - 1):
-        plane = swept[pl.ds(d * freq, freq), :]
-        stage[pl.ds((d - 1) * freq, freq), :] = finished(
-            plane,
-            swept[pl.ds((d - 1) * freq, freq), :],
-            swept[pl.ds((d + 1) * freq, freq), :],
-            first + d,
-            rate[...],
-            bearing[...],
-            shift[...],
+    copies = []
+    done = 1
+    for c in range(chunks):
+        swept[pl.ds(c * LANES, LANES), :] = rows[pl.ds(c, nodes, stride=4), :].T
+        until = (c + 1) * width - 1
+        for d in range(done, until):
+            stage[pl.ds((d - 1) * freq, freq), :] = finished(
+                swept[pl.ds(d * freq, freq), :],
+                swept[pl.ds((d - 1) * freq, freq), :],
+                swept[pl.ds((d + 1) * freq, freq), :],
+                first + d,
+                rate[...],
+                bearing[...],
+                shift[...],
+            )
+        copy = pltpu.make_async_copy(
+            stage.at[pl.ds((done - 1) * freq, (until - done) * freq), :],
+            out.at[pl.ds(done * freq, (until - done) * freq), :],
+            sems.at[c],
         )
-    copy = pltpu.make_async_copy(stage, out.at[pl.ds(freq, (sector - 2) * freq), :], sem)
-    copy.start()
-    copy.wait()
-
-
-def edge_body(swept, from_far, from_near, rate, bearing, shift, out_in, out, stage, sem):
+        copy.start()
+        copies.append(copy)
+        done = until
+    for k, d in enumerate((0, 1, sector - 2, sector - 1)):
+        ends[k] = swept[pl.ds(d * freq, freq), :]
+    for copy in copies:
+        copy.wait()
+
+
+def edge_body(ends, from_far, from_near, rate, bearing, shift, out_in, out, stage, sem):
     del out_in
     far = odd("dir") > 0
     freq, nodes = rate.shape
-    sector = swept.shape[0] // freq
+    sector = out.shape[0] // freq
     first = jnp.full((1, nodes), lax.axis_index("dir") * sector, jnp.int32)
+    before = jnp.where(far, from_near[...], from_far[...])
+    after = jnp.where(far, from_far[...], from_near[...])
     copies = []
-    for k, d in enumerate((0, sector - 1)):
-        plane = swept[pl.ds(d * freq, freq), :]
-        low = jnp.where(far, from_near[...], from_far[...]) if d == 0 else swept[pl.ds((d - 1) * freq, freq), :]
-        high = jnp.where(far, from_far[...], from_near[...]) if d == sector - 1 else swept[pl.ds((d + 1) * freq, freq), :]
+    for k, (d, low, plane, high) in enumerate(
+        ((0, before, ends[0], ends[1]), (sector - 1, ends[2], ends[3], after))
+    ):
         stage[k] = finished(plane, low, high, first + d, rate[...], bearing[...], shift[...])
         copy = pltpu.make_async_copy(stage.at[k], out.at[pl.ds(d * freq, freq), :], sem.at[k])
         copy.start()
@@ -281,7 +298,7 @@
     edges = jax.ShapeDtypeStruct((NEIGH, nodes), F32)
     field, far, near, angle, speed, slots = pl.pallas_call(
         rows_body,
-        out_shape=(fields, shares, shares, edges, edges, jax.ShapeDtypeStruct((NEIGH, nodes), jnp.int32)),
+        out_shape=(fields, shares, shares, edges, edges, jax.ShapeDtypeStruct((NEIGH * nodes // LANES, LANES), jnp.int32)),
         in_specs=[HBM] * 5,
         out_specs=(VMEM,) * 6,
         scratch_shapes=[
@@ -293,6 +310,7 @@
         compiler_params=params(),
         name="rows",
     )(*(in_hbm(x) for x in (send_rows, action.reshape(columns, nodes), edge_angle, edge_speed, neighbours)))
+    slots = slots.reshape(-1)
     far = swap_far_parts(far)
     near = swap_near(near, "dom")
     weight, base, share_weight, share_base, share_slots = pl.pallas_call(
@@ -336,28 +354,31 @@
 
     edge = jax.ShapeDtypeStruct((freq, nodes), F32)
     plane_shape = jax.ShapeDtypeStruct((columns, nodes), F32)
-    _, swept, far_plane, near_plane = pl.pallas_call(
+    _, rows, far_plane, near_plane = pl.pallas_call(
         last_body,
-        out_shape=(fields, plane_shape, edge, edge),
+        out_shape=(fields, jax.ShapeDtypeStruct((4 * nodes, LANES), F32), edge, edge),
         in_specs=[SMEM] + [VMEM] * 5,
         out_specs=(VMEM,) * 4,
         input_output_aliases={1: 0},
-        scratch_shapes=[pltpu.VMEM((4 * nodes, LANES), F32)],
         compiler_params=params(),
         name="last_sweep",
     )(slots, field, far, near, weight, base)
     far_plane = swap_far_sectors(far_plane)
     near_plane = swap_near(near_plane, "dir")
-    out = pl.pallas_call(
+    out, ends = pl.pallas_call(
         inner_body,
-        out_shape=plane_shape,
+        out_shape=(plane_shape, jax.ShapeDtypeStruct((4, freq, nodes), F32)),
         in_specs=[VMEM] * 4,
-        out_specs=ANY,
-        scratch_shapes=[pltpu.VMEM((columns - 2 * freq, nodes), F32), pltpu.SemaphoreType.DMA],
+        out_specs=(ANY, VMEM),
+        scratch_shapes=[
+            pltpu.VMEM((columns, nodes), F32),
+            pltpu.VMEM((columns - 2 * freq, nodes), F32),
+            pltpu.SemaphoreType.DMA((4,)),
+        ],
         compiler_params=params(),
         cost_estimate=cost(1 << 28, 2 << 20),
         name="inner_planes",
-    )(swept, refract_rate, bearing, shift_rate)
+    )(rows, refract_rate, bearing, shift_rate)
     out = pl.pallas_call(
         edge_body,
         out_shape=plane_shape,
@@ -367,7 +388,7 @@
         scratch_shapes=[pltpu.VMEM((2, freq, nodes), F32), pltpu.SemaphoreType.DMA((2,))],
         compiler_params=params(),
         name="edge_planes",
-    )(swept, far_plane, near_plane, refract_rate, bearing, shift_rate, out)
+    )(ends, far_plane, near_plane, refract_rate, bearing, shift_rate, out)
     return out.reshape(sector, freq, nodes)
 
 

time: 41.3 us -> 39.9 us (0.966)
  Pallas kernels: 24.4 us -> 20 us
  waiting for transfers between devices: 1.15 us -> 2.96 us
  starting transfers between devices: 15.5 us -> 16.7 us
    pallas_call x2, Pallas kernels: 9.35 us -> 6.92 us  [shards(): pl.pallas_call(sweep_body, out_shape=fields, in_specs=[SMEM] + [VMEM] * 3...]
    pallas_call x2, Pallas kernels: 7.05 us -> 5.31 us  [the longest x1 3.68 us: shards(): pl.pallas_call(last_body, out_shape=(fields, jax.ShapeDtypeStruct((4 * no...]
    ppermute x3, waiting for transfers between devices: 0.35 us -> 1.81 us  [swap_far_parts(): return lax.ppermute(array, ('dom', 'dir'), pairs)]
    ppermute x1, starting transfers between devices: 6.23 us -> 6.84 us  [swap_far_sectors(): return lax.ppermute(array, 'dir', pairs)]
    ppermute x3, starting transfers between devices: 9.29 us -> 9.86 us  [swap_far_parts(): return lax.ppermute(array, ('dom', 'dir'), pairs)]
  transfers between devices with their start and end apart: 8 -> 8, of which waited for: 2 -> 4; matrix products, arithmetic and copies ran while one was open for 0% -> 0% of each run, Pallas kernels for 37% -> 31%
where the time goes in v4:
time: 39.9 us; the launch traced here: 39.8 us
  Pallas kernels  20 us (50%)
  starting transfers between devices  16.7 us (42%)
  waiting for transfers between devices  2.96 us (7%)
    ppermute x3, starting transfers between devices, swap_far_parts(): return lax.ppermute(array, ('dom', 'dir'), pairs)  9.86 us
    pallas_call x2, Pallas kernels, shards(): pl.pallas_call(sweep_body, out_shape=fields, in_specs=[SMEM] + [VMEM] * 3...  6.92 us
    ppermute x1, starting transfers between devices, swap_far_sectors(): return lax.ppermute(array, 'dir', pairs)  6.84 us
    pallas_call x1, Pallas kernels, shards(): pl.pallas_call(last_body, out_shape=(fields, jax.ShapeDtypeStruct((4 * no...  3.68 us
    pallas_call x1, Pallas kernels, shards(): pl.pallas_call(weights_body, out_shape=(weights, bases, jax.ShapeDtypeStr...  3.62 us
    ppermute x3, waiting for transfers between devices, swap_far_parts(): return lax.ppermute(array, ('dom', 'dir'), pairs)  1.81 us
    pallas_call x2, Pallas kernels, shards(): pl.pallas_call(shared_body, out_shape=(fields, shares, shares), in_specs=...  1.71 us
    pallas_call x1, Pallas kernels, shards(): pl.pallas_call(rows_body, out_shape=(fields, shares, shares, edges, edges...  1.66 us
  transfers between devices with their start and end apart: 8, of which 4 were waited for; matrix products, arithmetic and copies ran while one was open for 0% of the time, Pallas kernels for 31%

profile of v4, /device:TPU:129, one launch (start us, length us, event | category | flops | bytes accessed | tf_op | source)
XLA Modules:
  0.0 39.8 jit_solution(18242081833412363826)
XLA Ops:
  0.0 1.7 %rows.1 = (f32[2320,128]{1,0:T(8,128)S(1)}, f32[128,128]{1,0:T(8,128)S(1)}, f32[128,128]{1,0:T(8,128)S(1)}, f32[6,512]{1,0:T(8,128)S(1)}, f32[6,512]{1,0:T(8,128)S(1)}, /*index=5*/s32[24,128]{1,0:T(8,128)S(1)}) custom-call(s32[2,32]{1,0:T(2,128)} %send_hbm.3, f32[512,512]{1,0:T(8,128)} %bitcast.10, f32[6,512]{1,0:T(8,128)} %angle_hbm.1, f32[6,512]{1,0:T(8,128)} %speed_hbm.1, ...), custom_call_target="tpu_custom_call" | custom-call | tf_op jit(solution)/shard_map/rows/pallas_call | solution.py:299
  1.7 3.3 %collective-permute-start = (f32[128,128]{1,0:T(8,128)S(1)}, f32[128,128]{1,0:T(8,128)S(1)}, u32[]{:S(2)}, u32[]{:S(2)}) collective-permute-start(f32[128,128]{1,0:T(8,128)S(1)} %get-tuple-element.32), channel_id=1, source_target_pairs={{4,8},{8,4},{12,16},{16,12},{20,24},{24,20},{28,32},{32,28},{36,40... | collective-permute-start | bytes 196616 | tf_op jit(solution)/shard_map/ppermute | solution.py:271
  5.0 0.0 collective-permute-start.1
  5.0 3.6 %weights.1 = (f32[12304,128]{1,0:T(8,128)S(1)}, f32[2064,128]{1,0:T(8,128)S(1)}, f32[1536,128]{1,0:T(8,128)S(1)}, f32[256,128]{1,0:T(8,128)S(1)}, s32[384]{0:T(512)S(1)}) custom-call(s32[2,32]{1,0:T(2,128)} %send_hbm.3, s32[3072]{0:T(1024)S(1)} %bitcast.4, f32[6,512]{1,0:T(8,128)S(1)} %get-tuple-element.28.edge_angle, ...), custom_call_target="tpu_custom_call" | custom-call | flops 1073741824 | bytes 8388608 | tf_op jit(solution)/shard_map/weights/pallas_call | solution.py:316
  8.6 0.5 %collective-permute-done.from_far = f32[128,128]{1,0:T(8,128)S(1)} collective-permute-done((f32[128,128]{1,0:T(8,128)S(1)}, f32[128,128]{1,0:T(8,128)S(1)}, u32[]{:S(2)}, u32[]{:S(2)}) %collective-permute-start) | collective-permute-done | bytes 65568 | tf_op jit(solution)/shard_map/ppermute | solution.py:271
  9.1 0.0 collective-permute-done.1.from_near
  9.1 0.9 %shared.2 = (f32[2320,128]{1,0:T(8,128)S(1)}, f32[128,128]{1,0:T(8,128)S(1)}, f32[128,128]{1,0:T(8,128)S(1)}) custom-call(s32[384]{0:T(512)S(1)} %get-tuple-element.31.slots, f32[2320,128]{1,0:T(8,128)S(1)} %get-tuple-element.30.field.field_in, f32[128,128]{1,0:T(8,128)S(1)} %collective-permute-done.from_far, ...), custom_call_target="tpu_custom_call", output_to_operand_aliasing={{0}: (1, {})} | custom-call | tf_op jit(solution)/shard_map/shared/pallas_call | solution.py:334
  10.0 3.3 %collective-permute-start.2 = (f32[128,128]{1,0:T(8,128)S(1)}, f32[128,128]{1,0:T(8,128)S(1)}, u32[]{:S(2)}, u32[]{:S(2)}) collective-permute-start(f32[128,128]{1,0:T(8,128)S(1)} %get-tuple-element.39), channel_id=1, source_target_pairs={{4,8},{8,4},{12,16},{16,12},{20,24},{24,20},{28,32},{32,28},{36,40... | collective-permute-start | bytes 196616 | tf_op jit(solution)/shard_map/ppermute | solution.py:271
  13.2 0.0 collective-permute-start.3
  13.2 3.5 %sweep.2.field_in = f32[2320,128]{1,0:T(8,128)S(1)} custom-call(s32[3072]{0:T(1024)S(1)} %bitcast.5, f32[2320,128]{1,0:T(8,128)S(1)} %get-tuple-element.36.field, f32[12304,128]{1,0:T(8,128)S(1)} %get-tuple-element.37.weight, f32[2064,128]{1,0:T(8,128)S(1)} %get-tuple-element.38.base), custom_call_target="tpu_custom_call" | custom-call | flops 1073741824 | bytes 8388608 | tf_op jit(solution)/shard_map/sweep/pallas_call | solution.py:345
  16.7 0.7 %collective-permute-done.2.from_far = f32[128,128]{1,0:T(8,128)S(1)} collective-permute-done((f32[128,128]{1,0:T(8,128)S(1)}, f32[128,128]{1,0:T(8,128)S(1)}, u32[]{:S(2)}, u32[]{:S(2)}) %collective-permute-start.2) | collective-permute-done | bytes 65568 | tf_op jit(solution)/shard_map/ppermute | solution.py:271
  17.4 0.0 collective-permute-done.3.from_near
  17.4 0.9 %shared.3 = (f32[2320,128]{1,0:T(8,128)S(1)}, f32[128,128]{1,0:T(8,128)S(1)}, f32[128,128]{1,0:T(8,128)S(1)}) custom-call(s32[384]{0:T(512)S(1)} %get-tuple-element.31.slots, f32[2320,128]{1,0:T(8,128)S(1)} %sweep.2.field_in, f32[128,128]{1,0:T(8,128)S(1)} %collective-permute-done.2.from_far, ...), custom_call_target="tpu_custom_call", output_to_operand_aliasing={{0}: (1, {})} | custom-call | tf_op jit(solution)/shard_map/shared/pallas_call | solution.py:334
  18.2 3.3 %collective-permute-start.4 = (f32[128,128]{1,0:T(8,128)S(1)}, f32[128,128]{1,0:T(8,128)S(1)}, u32[]{:S(2)}, u32[]{:S(2)}) collective-permute-start(f32[128,128]{1,0:T(8,128)S(1)} %get-tuple-element.42), channel_id=1, source_target_pairs={{4,8},{8,4},{12,16},{16,12},{20,24},{24,20},{28,32},{32,28},{36,40... | collective-permute-start | bytes 196616 | tf_op jit(solution)/shard_map/ppermute | solution.py:271
  21.5 0.0 collective-permute-start.5
  21.5 3.5 %sweep.3.field_in = f32[2320,128]{1,0:T(8,128)S(1)} custom-call(s32[3072]{0:T(1024)S(1)} %bitcast.6, f32[2320,128]{1,0:T(8,128)S(1)} %get-tuple-element.41.field, f32[12304,128]{1,0:T(8,128)S(1)} %get-tuple-element.37.weight, f32[2064,128]{1,0:T(8,128)S(1)} %get-tuple-element.38.base), custom_call_target="tpu_custom_call" | custom-call | flops 1073741824 | bytes 8388608 | tf_op jit(solution)/shard_map/sweep/pallas_call | solution.py:345
  25.0 0.0 copy-start
  25.0 0.0 copy-start.1
  25.0 0.0 copy-start.2
  25.0 0.6 %collective-permute-done.4.from_far = f32[128,128]{1,0:T(8,128)S(1)} collective-permute-done((f32[128,128]{1,0:T(8,128)S(1)}, f32[128,128]{1,0:T(8,128)S(1)}, u32[]{:S(2)}, u32[]{:S(2)}) %collective-permute-start.4) | collective-permute-done | bytes 65568 | tf_op jit(solution)/shard_map/ppermute | solution.py:271
  25.7 0.0 collective-permute-done.5.from_near
  25.7 3.7 %last_sweep.1 = (f32[2320,128]{1,0:T(8,128)S(1)}, f32[2048,128]{1,0:T(8,128)S(1)}, f32[32,512]{1,0:T(8,128)S(1)}, f32[32,512]{1,0:T(8,128)S(1)}) custom-call(s32[3072]{0:T(1024)S(1)} %bitcast.7, f32[2320,128]{1,0:T(8,128)S(1)} %sweep.3.field_in, f32[128,128]{1,0:T(8,128)S(1)} %collective-permute-done.4.from_far, ...), custom_call_target="tpu_custom_call", output_to_operand_aliasing={{0}: (1, {})} | custom-call | tf_op jit(solution)/shard_map/last_sweep/pallas_call | solution.py:357
  29.4 6.8 %collective-permute-start.6 = (f32[32,512]{1,0:T(8,128)S(1)}, f32[32,512]{1,0:T(8,128)S(1)}, u32[]{:S(2)}, u32[]{:S(2)}) collective-permute-start(f32[32,512]{1,0:T(8,128)S(1)} %get-tuple-element.46), channel_id=1, source_target_pairs={{1,2},{2,1},{3,0},{0,3},{5,6},{6,5},{7,4},{4,7},{9,10},{10,9},{11,... | collective-permute-start | bytes 196616 | tf_op jit(solution)/shard_map/ppermute | solution.py:277
  36.2 0.0 collective-permute-start.7
  36.2 0.0 copy-done
  36.2 0.0 copy-done.1
  36.2 0.0 copy-done.2
  36.2 1.6 %inner_planes.1 = (f32[512,512]{1,0:T(8,128)}, f32[4,32,512]{2,1,0:T(8,128)S(1)}) custom-call(f32[2048,128]{1,0:T(8,128)S(1)} %get-tuple-element.44.rows, f32[32,512]{1,0:T(8,128)S(1)} %copy-done, f32[1,512]{1,0:T(1,128)S(1)} %bitcast.8, f32[32,512]{1,0:T(8,128)S(1)} %copy-done.1), custom_call_target="tpu_custom_call" | custom-call | flops 268435456 | bytes 2097152 | tf_op jit(solution)/shard_map/inner_planes/pallas_call | solution.py:368
  37.8 1.1 %collective-permute-done.6.from_far = f32[32,512]{1,0:T(8,128)S(1)} collective-permute-done((f32[32,512]{1,0:T(8,128)S(1)}, f32[32,512]{1,0:T(8,128)S(1)}, u32[]{:S(2)}, u32[]{:S(2)}) %collective-permute-start.6) | collective-permute-done | bytes 65568 | tf_op jit(solution)/shard_map/ppermute | solution.py:277
  39.0 0.0 collective-permute-done.7.from_near
  39.0 0.8 %edge_planes.1 = f32[512,512]{1,0:T(8,128)} custom-call(f32[4,32,512]{2,1,0:T(8,128)S(1)} %get-tuple-element.45.ends, f32[32,512]{1,0:T(8,128)S(1)} %collective-permute-done.6.from_far, f32[32,512]{1,0:T(8,128)S(1)} %collective-permute-done.7.from_near, f32[32,512]{1,0:T(8,128)S(1)} %copy-done, ...), custom_call_target="tpu_custom_call", output_to_operand_aliasing={{}: (6, {})} | custom-call | tf_op jit(solution)/shard_map/edge_planes/pallas_call | solution.py:382
Async XLA Ops:
  1.7 7.4 %collective-permute-start = (f32[128,128]{1,0:T(8,128)S(1)}, f32[128,128]{1,0:T(8,128)S(1)}, u32[]{:S(2)}, u32[]{:S(2)}) collective-permute-start(f32[128,128]{1,0:T(8,128)S(1)} %get-tuple-element.32), channel_id=1, source_target_pairs={{4,8},{8,4},{12,16},{16,12},{20,24},{24,20},{28,32},{32,28},{36,40... | collective-permute-start | bytes 196616 | tf_op jit(solution)/shard_map/ppermute | solution.py:271
  5.0 4.1 %collective-permute-start.1 = (f32[128,128]{1,0:T(8,128)S(1)}, f32[128,128]{1,0:T(8,128)S(1)}, u32[]{:S(2)}, u32[]{:S(2)}) collective-permute-start(f32[128,128]{1,0:T(8,128)S(1)} %get-tuple-element.33), channel_id=1, source_target_pairs={{0,4},{4,0},{8,12},{12,8},{16,20},{20,16},{24,28},{28,24},{32,36},... | collective-permute-start | bytes 196616 | tf_op jit(solution)/shard_map/ppermute | solution.py:282
  10.0 7.4 %collective-permute-start.2 = (f32[128,128]{1,0:T(8,128)S(1)}, f32[128,128]{1,0:T(8,128)S(1)}, u32[]{:S(2)}, u32[]{:S(2)}) collective-permute-start(f32[128,128]{1,0:T(8,128)S(1)} %get-tuple-element.39), channel_id=1, source_target_pairs={{4,8},{8,4},{12,16},{16,12},{20,24},{24,20},{28,32},{32,28},{36,40... | collective-permute-start | bytes 196616 | tf_op jit(solution)/shard_map/ppermute | solution.py:271
  13.2 4.1 %collective-permute-start.3 = (f32[128,128]{1,0:T(8,128)S(1)}, f32[128,128]{1,0:T(8,128)S(1)}, u32[]{:S(2)}, u32[]{:S(2)}) collective-permute-start(f32[128,128]{1,0:T(8,128)S(1)} %get-tuple-element.40), channel_id=1, source_target_pairs={{0,4},{4,0},{8,12},{12,8},{16,20},{20,16},{24,28},{28,24},{32,36},... | collective-permute-start | bytes 196616 | tf_op jit(solution)/shard_map/ppermute | solution.py:282
  18.2 7.4 %collective-permute-start.4 = (f32[128,128]{1,0:T(8,128)S(1)}, f32[128,128]{1,0:T(8,128)S(1)}, u32[]{:S(2)}, u32[]{:S(2)}) collective-permute-start(f32[128,128]{1,0:T(8,128)S(1)} %get-tuple-element.42), channel_id=1, source_target_pairs={{4,8},{8,4},{12,16},{16,12},{20,24},{24,20},{28,32},{32,28},{36,40... | collective-permute-start | bytes 196616 | tf_op jit(solution)/shard_map/ppermute | solution.py:271
  21.5 4.1 %collective-permute-start.5 = (f32[128,128]{1,0:T(8,128)S(1)}, f32[128,128]{1,0:T(8,128)S(1)}, u32[]{:S(2)}, u32[]{:S(2)}) collective-permute-start(f32[128,128]{1,0:T(8,128)S(1)} %get-tuple-element.43), channel_id=1, source_target_pairs={{0,4},{4,0},{8,12},{12,8},{16,20},{20,16},{24,28},{28,24},{32,36},... | collective-permute-start | bytes 196616 | tf_op jit(solution)/shard_map/ppermute | solution.py:282
  25.0 11.2 %copy-start = (f32[32,512]{1,0:T(8,128)S(1)}, f32[32,512]{1,0:T(8,128)}, u32[]{:S(2)}) copy-start(f32[32,512]{1,0:T(8,128)} %rate.3) | copy-start | bytes 196612
  25.0 11.2 %copy-start.1 = (f32[32,512]{1,0:T(8,128)S(1)}, f32[32,512]{1,0:T(8,128)}, u32[]{:S(2)}) copy-start(f32[32,512]{1,0:T(8,128)} %shift.3) | copy-start | bytes 196612
  25.0 11.2 %copy-start.2 = (f32[512]{0:T(512)S(1)}, f32[512]{0:T(512)}, u32[]{:S(2)}) copy-start(f32[512]{0:T(512)} %param.14) | copy-start | bytes 6148
  29.4 9.6 %collective-permute-start.6 = (f32[32,512]{1,0:T(8,128)S(1)}, f32[32,512]{1,0:T(8,128)S(1)}, u32[]{:S(2)}, u32[]{:S(2)}) collective-permute-start(f32[32,512]{1,0:T(8,128)S(1)} %get-tuple-element.46), channel_id=1, source_target_pairs={{1,2},{2,1},{3,0},{0,3},{5,6},{6,5},{7,4},{4,7},{9,10},{10,9},{11,... | collective-permute-start | bytes 196616 | tf_op jit(solution)/shard_map/ppermute | solution.py:277
  36.2 2.8 %collective-permute-start.7 = (f32[32,512]{1,0:T(8,128)S(1)}, f32[32,512]{1,0:T(8,128)S(1)}, u32[]{:S(2)}, u32[]{:S(2)}) collective-permute-start(f32[32,512]{1,0:T(8,128)S(1)} %get-tuple-element.47), channel_id=1, source_target_pairs={{0,1},{1,0},{2,3},{3,2},{4,5},{5,4},{6,7},{7,6},{8,9},{9,8},{10,11... | collective-permute-start | bytes 196616 | tf_op jit(solution)/shard_map/ppermute | solution.py:282

commit v5 on v4

--- a/solution.py
+++ b/solution.py
@@ -10,6 +10,7 @@
 NDIR = 64
 NEIGH = 6
 LANES = 128
+EARLY = 12
 PAD = 8
 
 F32 = jnp.float32
@@ -49,26 +50,33 @@
 ):
     chunks = action.shape[0] // LANES
     nodes = action.shape[1]
+    blocks = nodes // LANES
     copies = []
     for c in range(chunks):
-        copy = pltpu.make_async_copy(action.at[pl.ds(c * LANES, LANES), :], stage.at[c], sems.at[c])
-        copy.start()
-        copies.append(copy)
+        for b in range(blocks):
+            k = c * blocks + b
+            tile = action.at[pl.ds(c * LANES, LANES), pl.ds(b * LANES, LANES)]
+            copies.append(pltpu.make_async_copy(tile, stage.at[k], sems.at[k]))
     for k, (source, target) in enumerate(
         ((send_hbm, send), (angle_hbm, edge_angle), (speed_hbm, edge_speed), (neighbours, listed))
     ):
-        copy = pltpu.make_async_copy(source, target, sems.at[chunks + k])
+        copies.append(pltpu.make_async_copy(source, target, sems.at[chunks * blocks + k]))
+    for copy in copies:
         copy.start()
-        copies.append(copy)
     for c in range(chunks):
-        copies[c].wait()
-        field[pl.ds(PAD + c, nodes, stride=4), :] = stage[c].T
-    for copy in copies[chunks:]:
+        for b in range(blocks):
+            k = c * blocks + b
+            copies[k].wait()
+            field[pl.ds(PAD + b * 4 * LANES + c, LANES, stride=4), :] = stage[k].T
+    for copy in copies[chunks * blocks :]:
         copy.wait()
     for j in range(NEIGH):
-        for c in range(nodes // LANES):
-            at = j * (nodes // LANES) + c
-            slots[pl.ds(at, 1), :] = listed[pl.ds(j, 1), c * LANES : (c + 1) * LANES] * 4
+        for b in range(blocks):
+            slots[pl.ds(j * blocks + b, 1), :] = listed[pl.ds(j, 1), b * LANES : (b + 1) * LANES] * 4
+    most = jnp.max(listed[...], axis=0, keepdims=True) * 4
+    for b in range(blocks):
+        own = most[:, b * LANES : (b + 1) * LANES]
+        slots[pl.ds(NEIGH * blocks + b, 1), :] = jnp.maximum(own, pltpu.roll(own, LANES - 1, 1))
     low = low_half()
     far = odd("dom")
     ghost = to_far.shape[0] // 4
@@ -78,7 +86,7 @@
 
 
 def weights_body(
-    send_hbm, slots, edge_angle, edge_speed, field, weight, base, share_weight, share_base, share_slots, send, sem
+    send_hbm, slots, edge_angle, edge_speed, field, weight, base, share_weight, share_base, share_slots, order, send, sem
 ):
     listed = pltpu.make_async_copy(send_hbm, send, sem)
     listed.start()
@@ -132,6 +140,17 @@
                 share_slots[j * 2 * ghost + s] = slots[j * nodes + n]
                 share_slots[j * 2 * ghost + s + 1] = slots[j * nodes + m]
 
+    pairs = nodes // 2
+
+    def place(i, counts):
+        own, other = counts
+        shared = (slots[NEIGH * nodes + 2 * i] >= 4 * nodes).astype(jnp.int32)
+        order[jnp.where(shared > 0, pairs - 1 - other, own)] = i
+        return own + 1 - shared, other + shared
+
+    own, _ = lax.fori_loop(0, pairs, place, (jnp.int32(0), jnp.int32(0)), unroll=8)
+    order[pairs] = own
+
 
 def place_ghosts(field, from_far, from_near, nodes):
     part = lax.axis_index("dom")
@@ -144,47 +163,77 @@
     field[pl.ds(pl.multiple_of(start + (1 - far) * rows, 8), rows), :] = from_near[...]
 
 
-def shared_body(slots, field_in, from_far, from_near, weight, base, field, to_far, to_near):
+def share_rows(slots, field, weight, base, out, first):
+    low = low_half()
+    ghost = out.shape[0] // 4
+    for i in range(0, ghost, 2):
+        s = first + i
+        total = base[pl.ds(4 * s, 8), :]
+        for j in range(NEIGH):
+            at = j * 2 * ghost + s
+            total = total + weight[pl.ds(4 * at, 8), :] * two_rows(field, slots[at], slots[at + 1], low)
+        out[pl.ds(4 * i, 8), :] = total
+
+
+def far_body(slots, field_in, from_far, from_near, weight, base, field, to_far):
     del field_in
     ghost = to_far.shape[0] // 4
-    nodes = (field.shape[0] - 2 * PAD) // 4 - 2 * ghost
+    place_ghosts(field, from_far, from_near, (field.shape[0] - 2 * PAD) // 4 - 2 * ghost)
+    share_rows(slots, field, weight, base, to_far, 0)
+
+
+def near_body(slots, field, weight, base, to_near):
+    share_rows(slots, field, weight, base, to_near, to_near.shape[0] // 4)
+
+
+def pair_row(slots, field, weight, base, i, nodes, low):
+    n = i * 2
+    row = pl.multiple_of(i * 8, 8)
+    total = base[pl.ds(PAD + row, 8), :]
+    for j in range(NEIGH):
+        value = two_rows(field, slots[j * nodes + n], slots[j * nodes + n + 1], low)
+        total = total + weight[pl.ds(PAD + j * 4 * nodes + row, 8), :] * value
+    return row, total
+
+
+def sweep_body(slots, field, weight, base, out):
+    low = low_half()
+    nodes = (base.shape[0] - 2 * PAD) // 4
+
+    def step(i, carry):
+        row, total = pair_row(slots, field, weight, base, i, nodes, low)
+        out[pl.ds(PAD + row, 8), :] = total
+        return carry
+
+    lax.fori_loop(0, nodes // 2, step, 0, unroll=8)
+
+
+def listed_pairs(order, slots, field, weight, base, rows, first, until):
+    low = low_half()
+    nodes = rows.shape[0] // 4
+
+    def step(g, carry):
+        for u in range(8):
+            row, total = pair_row(slots, field, weight, base, order[g * 8 + u], nodes, low)
+            rows[pl.ds(row, 8), :] = total
+        return carry
+
+    lax.fori_loop(first, until, step, 0)
+
+
+def early_groups(order, nodes):
+    return jnp.minimum(order[nodes // 2] // 8, EARLY)
+
+
+def early_body(order, slots, field, weight, base, rows):
+    listed_pairs(order, slots, field, weight, base, rows, 0, early_groups(order, rows.shape[0] // 4))
+
+
+def last_body(order, slots, field_in, from_far, from_near, weight, base, rows_in, field, rows, to_far, to_near):
+    del field_in, rows_in
+    nodes = rows.shape[0] // 4
     place_ghosts(field, from_far, from_near, nodes)
-    low = low_half()
-    for k, out in enumerate((to_far, to_near)):
-        for i in range(0, ghost, 2):
-            s = k * ghost + i
-            total = base[pl.ds(4 * s, 8), :]
-            for j in range(NEIGH):
-                at = j * 2 * ghost + s
-                total = total + weight[pl.ds(4 * at, 8), :] * two_rows(field, slots[at], slots[at + 1], low)
-            out[pl.ds(4 * i, 8), :] = total
-
-
-def sweep_rows(slots, field, weight, base, out, nodes, offset):
-    low = low_half()
-
-    def step(i, carry):
-        n = i * 2
-        row = pl.multiple_of(i * 8, 8)
-        total = base[pl.ds(PAD + row, 8), :]
-        for j in range(NEIGH):
-            value = two_rows(field, slots[j * nodes + n], slots[j * nodes + n + 1], low)
-            total = total + weight[pl.ds(PAD + j * 4 * nodes + row, 8), :] * value
-        out[pl.ds(offset + row, 8), :] = total
-        return carry
-
-    lax.fori_loop(0, nodes // 2, step, 0, unroll=8)
-
-
-def sweep_body(slots, field, weight, base, out):
-    sweep_rows(slots, field, weight, base, out, slots.shape[0] // NEIGH, PAD)
-
-
-def last_body(slots, field_in, from_far, from_near, weight, base, field, rows, to_far, to_near):
-    del field_in
-    nodes = slots.shape[0] // NEIGH
-    place_ghosts(field, from_far, from_near, nodes)
-    sweep_rows(slots, field, weight, base, rows, nodes, 0)
+    listed_pairs(order, slots, field, weight, base, rows, early_groups(order, nodes), nodes // 16)
     freq = to_far.shape[0]
     first = rows[pl.ds(0, nodes, stride=4), :].T[:freq, :]
     last = rows[pl.ds(3, nodes, stride=4), :].T[LANES - freq :, :]
@@ -298,14 +347,14 @@
     edges = jax.ShapeDtypeStruct((NEIGH, nodes), F32)
     field, far, near, angle, speed, slots = pl.pallas_call(
         rows_body,
-        out_shape=(fields, shares, shares, edges, edges, jax.ShapeDtypeStruct((NEIGH * nodes // LANES, LANES), jnp.int32)),
+        out_shape=(fields, shares, shares, edges, edges, jax.ShapeDtypeStruct(((NEIGH + 2) * nodes // LANES, LANES), jnp.int32)),
         in_specs=[HBM] * 5,
         out_specs=(VMEM,) * 6,
         scratch_shapes=[
-            pltpu.VMEM((4, LANES, nodes), F32),
+            pltpu.VMEM((columns // LANES * nodes // LANES, LANES, LANES), F32),
             pltpu.SMEM((2, ghost), jnp.int32),
             pltpu.VMEM((NEIGH, nodes), jnp.int32),
-            pltpu.SemaphoreType.DMA((8,)),
+            pltpu.SemaphoreType.DMA((columns // LANES * nodes // LANES + 4,)),
         ],
         compiler_params=params(),
         name="rows",
@@ -313,7 +362,7 @@
     slots = slots.reshape(-1)
     far = swap_far_parts(far)
     near = swap_near(near, "dom")
-    weight, base, share_weight, share_base, share_slots = pl.pallas_call(
+    weight, base, share_weight, share_base, share_slots, order = pl.pallas_call(
         weights_body,
         out_shape=(
             weights,
@@ -321,9 +370,10 @@
             jax.ShapeDtypeStruct((NEIGH * 8 * ghost, LANES), F32),
             jax.ShapeDtypeStruct((8 * ghost, LANES), F32),
             jax.ShapeDtypeStruct((NEIGH * 2 * ghost,), jnp.int32),
+            jax.ShapeDtypeStruct((nodes // 2 + 8,), jnp.int32),
         ),
         in_specs=[HBM, SMEM] + [VMEM] * 3,
-        out_specs=(VMEM, VMEM, VMEM, VMEM, SMEM),
+        out_specs=(VMEM, VMEM, VMEM, VMEM, SMEM, SMEM),
         scratch_shapes=[pltpu.SMEM((2, ghost), jnp.int32), pltpu.SemaphoreType.DMA],
         compiler_params=params(),
         cost_estimate=cost(1 << 30, 8 << 20),
@@ -331,16 +381,25 @@
     )(in_hbm(send_rows), slots, angle, speed, field)
 
     for _ in range(2):
-        field, far, near = pl.pallas_call(
-            shared_body,
-            out_shape=(fields, shares, shares),
+        field, far = pl.pallas_call(
+            far_body,
+            out_shape=(fields, shares),
             in_specs=[SMEM] + [VMEM] * 5,
-            out_specs=(VMEM, VMEM, VMEM),
+            out_specs=(VMEM, VMEM),
             input_output_aliases={1: 0},
             compiler_params=params(),
-            name="shared",
+            name="shared_far",
         )(share_slots, field, far, near, share_weight, share_base)
         far = swap_far_parts(far)
+        near = pl.pallas_call(
+            near_body,
+            out_shape=shares,
+            in_specs=[SMEM] + [VMEM] * 3,
+            out_specs=VMEM,
+            compiler_params=params(),
+            cost_estimate=cost(1 << 27, 1 << 20),
+            name="shared_near",
+        )(share_slots, field, share_weight, share_base)
         near = swap_near(near, "dom")
         field = pl.pallas_call(
             sweep_body,
@@ -354,15 +413,25 @@
 
     edge = jax.ShapeDtypeStruct((freq, nodes), F32)
     plane_shape = jax.ShapeDtypeStruct((columns, nodes), F32)
+    swept_rows = jax.ShapeDtypeStruct((4 * nodes, LANES), F32)
+    rows = pl.pallas_call(
+        early_body,
+        out_shape=swept_rows,
+        in_specs=[SMEM, SMEM] + [VMEM] * 3,
+        out_specs=VMEM,
+        compiler_params=params(),
+        cost_estimate=cost(1 << 29, 4 << 20),
+        name="last_sweep_early",
+    )(order, slots, field, weight, base)
     _, rows, far_plane, near_plane = pl.pallas_call(
         last_body,
-        out_shape=(fields, jax.ShapeDtypeStruct((4 * nodes, LANES), F32), edge, edge),
-        in_specs=[SMEM] + [VMEM] * 5,
+        out_shape=(fields, swept_rows, edge, edge),
+        in_specs=[SMEM, SMEM] + [VMEM] * 6,
         out_specs=(VMEM,) * 4,
-        input_output_aliases={1: 0},
+        input_output_aliases={2: 0, 7: 1},
         compiler_params=params(),
         name="last_sweep",
-    )(slots, field, far, near, weight, base)
+    )(order, slots, field, far, near, weight, base, rows)
     far_plane = swap_far_sectors(far_plane)
     near_plane = swap_near(near_plane, "dir")
     out, ends = pl.pallas_call(

time: 39.9 us -> 43.7 us (1.095)
  Pallas kernels: 20 us -> 24.9 us
  starting transfers between devices: 16.7 us -> 15.6 us
    pallas_call x3 -> x6, Pallas kernels: 5.4 us -> 7.92 us  [the longest x1 3.05 us: shards(): pl.pallas_call(last_body, out_shape=(fields, swept_rows, edge, edge), in_...]
    ppermute x4, starting transfers between devices: 0.01 us -> 1.56 us  [swap_near(): lax.ppermute(array, axis, [p for i in range(0, count, 2) for p in ((i, i...]
    ppermute x3, starting transfers between devices: 9.86 us -> 8.33 us  [swap_far_parts(): return lax.ppermute(array, ('dom', 'dir'), pairs)]
    ppermute x1, starting transfers between devices: 6.84 us -> 5.66 us  [swap_far_sectors(): return lax.ppermute(array, 'dir', pairs)]
    pallas_call x1, Pallas kernels: 3.62 us -> 4.76 us  [shards(): pl.pallas_call(weights_body, out_shape=(weights, bases, jax.ShapeDtypeStr...]
    pallas_call x1, Pallas kernels: 1.66 us -> 2.74 us  [shards(): pl.pallas_call(rows_body, out_shape=(fields, shares, shares, edges, edges...]
    ppermute x3, waiting for transfers between devices: 1.81 us -> 1.31 us  [swap_far_parts(): return lax.ppermute(array, ('dom', 'dir'), pairs)]
  transfers between devices with their start and end apart: 8 -> 8, of which waited for: 4 -> 2; matrix products, arithmetic and copies ran while one was open for 0% -> 0% of each run, Pallas kernels for 31% -> 36%
where the time goes in v5:
time: 43.7 us; the launch traced here: 43.2 us
  Pallas kernels  24.9 us (57%)
  starting transfers between devices  15.6 us (36%)
  waiting for transfers between devices  2.6 us (6%)
    ppermute x3, starting transfers between devices, swap_far_parts(): return lax.ppermute(array, ('dom', 'dir'), pairs)  8.33 us
    pallas_call x2, Pallas kernels, shards(): pl.pallas_call(sweep_body, out_shape=fields, in_specs=[SMEM] + [VMEM] * 3...  7.07 us
    ppermute x1, starting transfers between devices, swap_far_sectors(): return lax.ppermute(array, 'dir', pairs)  5.66 us
    pallas_call x1, Pallas kernels, shards(): pl.pallas_call(weights_body, out_shape=(weights, bases, jax.ShapeDtypeStr...  4.76 us
    pallas_call x1, Pallas kernels, shards(): pl.pallas_call(last_body, out_shape=(fields, swept_rows, edge, edge), in_...  3.05 us
    pallas_call x1, Pallas kernels, shards(): pl.pallas_call(rows_body, out_shape=(fields, shares, shares, edges, edges...  2.74 us
    pallas_call x1, Pallas kernels, shards(): pl.pallas_call(early_body, out_shape=swept_rows, in_specs=[SMEM, SMEM] +...  2.03 us
    pallas_call x1, Pallas kernels, shards(): pl.pallas_call(inner_body, out_shape=(plane_shape, jax.ShapeDtypeStruct((...  1.63 us
  transfers between devices with their start and end apart: 8, of which 2 were waited for; matrix products, arithmetic and copies ran while one was open for 0% of the time, Pallas kernels for 36%

profile of v5, /device:TPU:129, one launch (start us, length us, event | category | flops | bytes accessed | tf_op | source)
XLA Modules:
  0.0 43.2 jit_solution(213323913197225313)
XLA Ops:
  0.0 2.7 %rows.1 = (f32[2320,128]{1,0:T(8,128)S(1)}, f32[128,128]{1,0:T(8,128)S(1)}, f32[128,128]{1,0:T(8,128)S(1)}, f32[6,512]{1,0:T(8,128)S(1)}, f32[6,512]{1,0:T(8,128)S(1)}, /*index=5*/s32[32,128]{1,0:T(8,128)S(1)}) custom-call(s32[2,32]{1,0:T(2,128)} %send_hbm.3, f32[512,512]{1,0:T(8,128)} %bitcast.11, f32[6,512]{1,0:T(8,128)} %angle_hbm.1, f32[6,512]{1,0:T(8,128)} %speed_hbm.1, ...), custom_call_target="tpu_custom_call" | custom-call | tf_op jit(solution)/shard_map/rows/pallas_call | solution.py:348
  2.7 3.3 %collective-permute-start = (f32[128,128]{1,0:T(8,128)S(1)}, f32[128,128]{1,0:T(8,128)S(1)}, u32[]{:S(2)}, u32[]{:S(2)}) collective-permute-start(f32[128,128]{1,0:T(8,128)S(1)} %get-tuple-element.32), channel_id=1, source_target_pairs={{4,8},{8,4},{12,16},{16,12},{20,24},{24,20},{28,32},{32,28},{36,40... | collective-permute-start | bytes 196616 | tf_op jit(solution)/shard_map/ppermute | solution.py:320
  6.0 0.0 collective-permute-start.1
  6.0 4.8 %weights.1 = (f32[12304,128]{1,0:T(8,128)S(1)}, f32[2064,128]{1,0:T(8,128)S(1)}, f32[1536,128]{1,0:T(8,128)S(1)}, f32[256,128]{1,0:T(8,128)S(1)}, s32[384]{0:T(512)S(1)}, /*index=5*/s32[264]{0:T(512)S(1)}) custom-call(s32[2,32]{1,0:T(2,128)} %send_hbm.3, s32[4096]{0:T(1024)S(1)} %bitcast.4, f32[6,512]{1,0:T(8,128)S(1)} %get-tuple-element.27.edge_angle, ...), custom_call_target="tpu_custom_call" | custom-call | flops 1073741824 | bytes 8388608 | tf_op jit(solution)/shard_map/weights/pallas_call | solution.py:365
  10.8 0.0 collective-permute-done.from_far
  10.8 0.0 collective-permute-done.1.from_near
  10.8 0.7 %shared_far.2 = (f32[2320,128]{1,0:T(8,128)S(1)}, f32[128,128]{1,0:T(8,128)S(1)}) custom-call(s32[384]{0:T(512)S(1)} %get-tuple-element.31.slots, f32[2320,128]{1,0:T(8,128)S(1)} %get-tuple-element.29.field.field_in, f32[128,128]{1,0:T(8,128)S(1)} %collective-permute-done.from_far, ...), custom_call_target="tpu_custom_call", output_to_operand_aliasing={{0}: (1, {})} | custom-call | tf_op jit(solution)/shard_map/shared_far/pallas_call | solution.py:384
  11.6 0.7 %shared_near.2 = f32[128,128]{1,0:T(8,128)S(1)} custom-call(s32[384]{0:T(512)S(1)} %get-tuple-element.31.slots, f32[2320,128]{1,0:T(8,128)S(1)} %get-tuple-element.36.field, f32[1536,128]{1,0:T(8,128)S(1)} %get-tuple-element.34.weight, f32[256,128]{1,0:T(8,128)S(1)} %get-tuple-element.35.base), custom_call_target="tpu_custom_call" | custom-call | flops 134217728 | bytes 1048576 | tf_op jit(solution)/shard_map/shared_near/pallas_call | solution.py:394
  12.2 1.5 %collective-permute-start.3 = (f32[128,128]{1,0:T(8,128)S(1)}, f32[128,128]{1,0:T(8,128)S(1)}, u32[]{:S(2)}, u32[]{:S(2)}) collective-permute-start(f32[128,128]{1,0:T(8,128)S(1)} %shared_near.2), channel_id=1, source_target_pairs={{0,4},{4,0},{8,12},{12,8},{16,20},{20,16},{24,28},{28,24},{32,36},... | collective-permute-start | bytes 196616 | tf_op jit(solution)/shard_map/ppermute | solution.py:331
  13.8 2.5 %collective-permute-start.2 = (f32[128,128]{1,0:T(8,128)S(1)}, f32[128,128]{1,0:T(8,128)S(1)}, u32[]{:S(2)}, u32[]{:S(2)}) collective-permute-start(f32[128,128]{1,0:T(8,128)S(1)} %get-tuple-element.39), channel_id=1, source_target_pairs={{4,8},{8,4},{12,16},{16,12},{20,24},{24,20},{28,32},{32,28},{36,40... | collective-permute-start | bytes 196616 | tf_op jit(solution)/shard_map/ppermute | solution.py:320
  16.3 3.5 %sweep.2.field_in = f32[2320,128]{1,0:T(8,128)S(1)} custom-call(s32[4096]{0:T(1024)S(1)} %bitcast.5, f32[2320,128]{1,0:T(8,128)S(1)} %get-tuple-element.36.field, f32[12304,128]{1,0:T(8,128)S(1)} %get-tuple-element.37.weight, f32[2064,128]{1,0:T(8,128)S(1)} %get-tuple-element.38.base), custom_call_target="tpu_custom_call" | custom-call | flops 1073741824 | bytes 8388608 | tf_op jit(solution)/shard_map/sweep/pallas_call | solution.py:404
  19.8 0.0 collective-permute-done.3.from_near
  19.8 1.3 %collective-permute-done.2.from_far = f32[128,128]{1,0:T(8,128)S(1)} collective-permute-done((f32[128,128]{1,0:T(8,128)S(1)}, f32[128,128]{1,0:T(8,128)S(1)}, u32[]{:S(2)}, u32[]{:S(2)}) %collective-permute-start.2) | collective-permute-done | bytes 65568 | tf_op jit(solution)/shard_map/ppermute | solution.py:320
  21.1 0.7 %shared_far.3 = (f32[2320,128]{1,0:T(8,128)S(1)}, f32[128,128]{1,0:T(8,128)S(1)}) custom-call(s32[384]{0:T(512)S(1)} %get-tuple-element.31.slots, f32[2320,128]{1,0:T(8,128)S(1)} %sweep.2.field_in, f32[128,128]{1,0:T(8,128)S(1)} %collective-permute-done.2.from_far, f32[128,128]{1,0:T(8,128)S(1)} %collective-permute-done.3.from_near, ...), custom_call_target="tpu_custom_call", output_to_operand_aliasing={{0}: (1, {})} | custom-call | tf_op jit(solution)/shard_map/shared_far/pallas_call | solution.py:384
  21.9 0.7 %shared_near.3 = f32[128,128]{1,0:T(8,128)S(1)} custom-call(s32[384]{0:T(512)S(1)} %get-tuple-element.31.slots, f32[2320,128]{1,0:T(8,128)S(1)} %get-tuple-element.40.field, f32[1536,128]{1,0:T(8,128)S(1)} %get-tuple-element.34.weight, f32[256,128]{1,0:T(8,128)S(1)} %get-tuple-element.35.base), custom_call_target="tpu_custom_call" | custom-call | flops 134217728 | bytes 1048576 | tf_op jit(solution)/shard_map/shared_near/pallas_call | solution.py:394
  22.6 2.6 %collective-permute-start.4 = (f32[128,128]{1,0:T(8,128)S(1)}, f32[128,128]{1,0:T(8,128)S(1)}, u32[]{:S(2)}, u32[]{:S(2)}) collective-permute-start(f32[128,128]{1,0:T(8,128)S(1)} %get-tuple-element.41), channel_id=1, source_target_pairs={{4,8},{8,4},{12,16},{16,12},{20,24},{24,20},{28,32},{32,28},{36,40... | collective-permute-start | bytes 196616 | tf_op jit(solution)/shard_map/ppermute | solution.py:320
  25.1 0.0 collective-permute-start.5
  25.1 3.5 %sweep.3.field.field_in = f32[2320,128]{1,0:T(8,128)S(1)} custom-call(s32[4096]{0:T(1024)S(1)} %bitcast.6, f32[2320,128]{1,0:T(8,128)S(1)} %get-tuple-element.40.field, f32[12304,128]{1,0:T(8,128)S(1)} %get-tuple-element.37.weight, f32[2064,128]{1,0:T(8,128)S(1)} %get-tuple-element.38.base), custom_call_target="tpu_custom_call" | custom-call | flops 1073741824 | bytes 8388608 | tf_op jit(solution)/shard_map/sweep/pallas_call | solution.py:404
  28.7 2.0 %last_sweep_early.1.rows_in = f32[2048,128]{1,0:T(8,128)S(1)} custom-call(s32[264]{0:T(512)S(1)} %get-tuple-element.30.order, s32[4096]{0:T(1024)S(1)} %bitcast.7, f32[2320,128]{1,0:T(8,128)S(1)} %sweep.3.field.field_in, f32[12304,128]{1,0:T(8,128)S(1)} %get-tuple-element.37.weight, f32[2064,128]{1,0:T(8,128)S(1)} %get-tuple-element.38.base), custom_call_target="tpu_custom_call" | custom-call | flops 536870912 | bytes 4194304 | tf_op jit(solution)/shard_map/last_sweep_early/pallas_call | solution.py:417
  30.7 0.0 copy-start
  30.7 0.0 copy-start.1
  30.7 0.0 copy-start.2
  30.7 0.0 collective-permute-done.4.from_far
  30.7 0.0 collective-permute-done.5.from_near
  30.8 3.1 %last_sweep.1 = (f32[2320,128]{1,0:T(8,128)S(1)}, f32[2048,128]{1,0:T(8,128)S(1)}, f32[32,512]{1,0:T(8,128)S(1)}, f32[32,512]{1,0:T(8,128)S(1)}) custom-call(s32[264]{0:T(512)S(1)} %get-tuple-element.30.order, s32[4096]{0:T(1024)S(1)} %bitcast.8, f32[2320,128]{1,0:T(8,128)S(1)} %sweep.3.field.field_in, ...), custom_call_target="tpu_custom_call", output_to_operand_aliasing={{0}: (2, {}), {1}: (7, {})} | custom-call | tf_op jit(solution)/shard_map/last_sweep/pallas_call | solution.py:426
  33.8 5.7 %collective-permute-start.6 = (f32[32,512]{1,0:T(8,128)S(1)}, f32[32,512]{1,0:T(8,128)S(1)}, u32[]{:S(2)}, u32[]{:S(2)}) collective-permute-start(f32[32,512]{1,0:T(8,128)S(1)} %get-tuple-element.44), channel_id=1, source_target_pairs={{1,2},{2,1},{3,0},{0,3},{5,6},{6,5},{7,4},{4,7},{9,10},{10,9},{11,... | collective-permute-start | bytes 196616 | tf_op jit(solution)/shard_map/ppermute | solution.py:326
  39.5 0.0 collective-permute-start.7
  39.5 0.0 copy-done.1
  39.5 1.6 %inner_planes.1 = (f32[512,512]{1,0:T(8,128)}, f32[4,32,512]{2,1,0:T(8,128)S(1)}) custom-call(f32[2048,128]{1,0:T(8,128)S(1)} %get-tuple-element.42.rows, f32[32,512]{1,0:T(8,128)S(1)} %copy-done, f32[1,512]{1,0:T(1,128)S(1)} %bitcast.9, f32[32,512]{1,0:T(8,128)S(1)} %copy-done.1), custom_call_target="tpu_custom_call" | custom-call | flops 268435456 | bytes 2097152 | tf_op jit(solution)/shard_map/inner_planes/pallas_call | solution.py:437
  41.1 1.3 %collective-permute-done.6.from_far = f32[32,512]{1,0:T(8,128)S(1)} collective-permute-done((f32[32,512]{1,0:T(8,128)S(1)}, f32[32,512]{1,0:T(8,128)S(1)}, u32[]{:S(2)}, u32[]{:S(2)}) %collective-permute-start.6) | collective-permute-done | bytes 65568 | tf_op jit(solution)/shard_map/ppermute | solution.py:326
  42.4 0.0 collective-permute-done.7.from_near
  42.4 0.8 %edge_planes.1 = f32[512,512]{1,0:T(8,128)} custom-call(f32[4,32,512]{2,1,0:T(8,128)S(1)} %get-tuple-element.43.ends, f32[32,512]{1,0:T(8,128)S(1)} %collective-permute-done.6.from_far, f32[32,512]{1,0:T(8,128)S(1)} %collective-permute-done.7.from_near, f32[32,512]{1,0:T(8,128)S(1)} %copy-done, ...), custom_call_target="tpu_custom_call", output_to_operand_aliasing={{}: (6, {})} | custom-call | tf_op jit(solution)/shard_map/edge_planes/pallas_call | solution.py:451
  (2 shorter events, 0.0 us)
Async XLA Ops:
  2.7 8.1 %collective-permute-start = (f32[128,128]{1,0:T(8,128)S(1)}, f32[128,128]{1,0:T(8,128)S(1)}, u32[]{:S(2)}, u32[]{:S(2)}) collective-permute-start(f32[128,128]{1,0:T(8,128)S(1)} %get-tuple-element.32), channel_id=1, source_target_pairs={{4,8},{8,4},{12,16},{16,12},{20,24},{24,20},{28,32},{32,28},{36,40... | collective-permute-start | bytes 196616 | tf_op jit(solution)/shard_map/ppermute | solution.py:320
  6.0 4.8 %collective-permute-start.1 = (f32[128,128]{1,0:T(8,128)S(1)}, f32[128,128]{1,0:T(8,128)S(1)}, u32[]{:S(2)}, u32[]{:S(2)}) collective-permute-start(f32[128,128]{1,0:T(8,128)S(1)} %get-tuple-element.33), channel_id=1, source_target_pairs={{0,4},{4,0},{8,12},{12,8},{16,20},{20,16},{24,28},{28,24},{32,36},... | collective-permute-start | bytes 196616 | tf_op jit(solution)/shard_map/ppermute | solution.py:331
  12.2 7.6 %collective-permute-start.3 = (f32[128,128]{1,0:T(8,128)S(1)}, f32[128,128]{1,0:T(8,128)S(1)}, u32[]{:S(2)}, u32[]{:S(2)}) collective-permute-start(f32[128,128]{1,0:T(8,128)S(1)} %shared_near.2), channel_id=1, source_target_pairs={{0,4},{4,0},{8,12},{12,8},{16,20},{20,16},{24,28},{28,24},{32,36},... | collective-permute-start | bytes 196616 | tf_op jit(solution)/shard_map/ppermute | solution.py:331
  13.8 7.3 %collective-permute-start.2 = (f32[128,128]{1,0:T(8,128)S(1)}, f32[128,128]{1,0:T(8,128)S(1)}, u32[]{:S(2)}, u32[]{:S(2)}) collective-permute-start(f32[128,128]{1,0:T(8,128)S(1)} %get-tuple-element.39), channel_id=1, source_target_pairs={{4,8},{8,4},{12,16},{16,12},{20,24},{24,20},{28,32},{32,28},{36,40... | collective-permute-start | bytes 196616 | tf_op jit(solution)/shard_map/ppermute | solution.py:320
  22.6 8.2 %collective-permute-start.4 = (f32[128,128]{1,0:T(8,128)S(1)}, f32[128,128]{1,0:T(8,128)S(1)}, u32[]{:S(2)}, u32[]{:S(2)}) collective-permute-start(f32[128,128]{1,0:T(8,128)S(1)} %get-tuple-element.41), channel_id=1, source_target_pairs={{4,8},{8,4},{12,16},{16,12},{20,24},{24,20},{28,32},{32,28},{36,40... | collective-permute-start | bytes 196616 | tf_op jit(solution)/shard_map/ppermute | solution.py:320
  25.1 5.6 %collective-permute-start.5 = (f32[128,128]{1,0:T(8,128)S(1)}, f32[128,128]{1,0:T(8,128)S(1)}, u32[]{:S(2)}, u32[]{:S(2)}) collective-permute-start(f32[128,128]{1,0:T(8,128)S(1)} %shared_near.3), channel_id=1, source_target_pairs={{0,4},{4,0},{8,12},{12,8},{16,20},{20,16},{24,28},{28,24},{32,36},... | collective-permute-start | bytes 196616 | tf_op jit(solution)/shard_map/ppermute | solution.py:331
  30.7 8.8 %copy-start = (f32[32,512]{1,0:T(8,128)S(1)}, f32[32,512]{1,0:T(8,128)}, u32[]{:S(2)}) copy-start(f32[32,512]{1,0:T(8,128)} %rate.3) | copy-start | bytes 196612
  30.7 8.8 %copy-start.1 = (f32[32,512]{1,0:T(8,128)S(1)}, f32[32,512]{1,0:T(8,128)}, u32[]{:S(2)}) copy-start(f32[32,512]{1,0:T(8,128)} %shift.3) | copy-start | bytes 196612
  30.7 8.8 %copy-start.2 = (f32[512]{0:T(512)S(1)}, f32[512]{0:T(512)}, u32[]{:S(2)}) copy-start(f32[512]{0:T(512)} %param.14) | copy-start | bytes 6148
  33.8 8.6 %collective-permute-start.6 = (f32[32,512]{1,0:T(8,128)S(1)}, f32[32,512]{1,0:T(8,128)S(1)}, u32[]{:S(2)}, u32[]{:S(2)}) collective-permute-start(f32[32,512]{1,0:T(8,128)S(1)} %get-tuple-element.44), channel_id=1, source_target_pairs={{1,2},{2,1},{3,0},{0,3},{5,6},{6,5},{7,4},{4,7},{9,10},{10,9},{11,... | collective-permute-start | bytes 196616 | tf_op jit(solution)/shard_map/ppermute | solution.py:326
  39.5 2.9 %collective-permute-start.7 = (f32[32,512]{1,0:T(8,128)S(1)}, f32[32,512]{1,0:T(8,128)S(1)}, u32[]{:S(2)}, u32[]{:S(2)}) collective-permute-start(f32[32,512]{1,0:T(8,128)S(1)} %get-tuple-element.45), channel_id=1, source_target_pairs={{0,1},{1,0},{2,3},{3,2},{4,5},{5,4},{6,7},{7,6},{8,9},{9,8},{10,11... | collective-permute-start | bytes 196616 | tf_op jit(solution)/shard_map/ppermute | solution.py:331

commit v6 on v5

--- a/solution.py
+++ b/solution.py
@@ -10,7 +10,7 @@
 NDIR = 64
 NEIGH = 6
 LANES = 128
-EARLY = 12
+EARLY = 14
 PAD = 8
 
 F32 = jnp.float32
@@ -53,22 +53,17 @@
     blocks = nodes // LANES
     copies = []
     for c in range(chunks):
-        for b in range(blocks):
-            k = c * blocks + b
-            tile = action.at[pl.ds(c * LANES, LANES), pl.ds(b * LANES, LANES)]
-            copies.append(pltpu.make_async_copy(tile, stage.at[k], sems.at[k]))
+        copies.append(pltpu.make_async_copy(action.at[pl.ds(c * LANES, LANES), :], stage.at[c], sems.at[c]))
     for k, (source, target) in enumerate(
         ((send_hbm, send), (angle_hbm, edge_angle), (speed_hbm, edge_speed), (neighbours, listed))
     ):
-        copies.append(pltpu.make_async_copy(source, target, sems.at[chunks * blocks + k]))
+        copies.append(pltpu.make_async_copy(source, target, sems.at[chunks + k]))
     for copy in copies:
         copy.start()
     for c in range(chunks):
-        for b in range(blocks):
-            k = c * blocks + b
-            copies[k].wait()
-            field[pl.ds(PAD + b * 4 * LANES + c, LANES, stride=4), :] = stage[k].T
-    for copy in copies[chunks * blocks :]:
+        copies[c].wait()
+        field[pl.ds(PAD + c, nodes, stride=4), :] = stage[c].T
+    for copy in copies[chunks:]:
         copy.wait()
     for j in range(NEIGH):
         for b in range(blocks):
@@ -86,10 +81,16 @@
 
 
 def weights_body(
-    send_hbm, slots, edge_angle, edge_speed, field, weight, base, share_weight, share_base, share_slots, order, send, sem
+    send_hbm, listed, edge_angle, edge_speed, field,
+    weight, base, share_weight, share_base, slots, share_slots, order, send, sems,
 ):
-    listed = pltpu.make_async_copy(send_hbm, send, sem)
-    listed.start()
+    rows = listed.shape[0]
+    copies = [
+        pltpu.make_async_copy(listed.at[r], slots.at[pl.ds(r * LANES, LANES)], sems.at[r]) for r in range(rows)
+    ]
+    copies.append(pltpu.make_async_copy(send_hbm, send, sems.at[rows]))
+    for copy in copies:
+        copy.start()
     sector = 16
     nodes = edge_angle.shape[1]
     freq = 4 * LANES // sector
@@ -124,7 +125,8 @@
     for c in range(4):
         rows = pl.ds(PAD + c, nodes, stride=4)
         base[rows, :] = field[rows, :] * wide[:, c * LANES : (c + 1) * LANES]
-    listed.wait()
+    for copy in copies:
+        copy.wait()
     low = low_half()
     far = odd("dom")
     ghost = send.shape[1]
@@ -175,15 +177,12 @@
         out[pl.ds(4 * i, 8), :] = total
 
 
-def far_body(slots, field_in, from_far, from_near, weight, base, field, to_far):
+def shared_body(slots, field_in, from_far, from_near, weight, base, field, to_far, to_near):
     del field_in
     ghost = to_far.shape[0] // 4
     place_ghosts(field, from_far, from_near, (field.shape[0] - 2 * PAD) // 4 - 2 * ghost)
     share_rows(slots, field, weight, base, to_far, 0)
-
-
-def near_body(slots, field, weight, base, to_near):
-    share_rows(slots, field, weight, base, to_near, to_near.shape[0] // 4)
+    share_rows(slots, field, weight, base, to_near, ghost)
 
 
 def pair_row(slots, field, weight, base, i, nodes, low):
@@ -351,55 +350,49 @@
         in_specs=[HBM] * 5,
         out_specs=(VMEM,) * 6,
         scratch_shapes=[
-            pltpu.VMEM((columns // LANES * nodes // LANES, LANES, LANES), F32),
+            pltpu.VMEM((columns // LANES, LANES, nodes), F32),
             pltpu.SMEM((2, ghost), jnp.int32),
             pltpu.VMEM((NEIGH, nodes), jnp.int32),
-            pltpu.SemaphoreType.DMA((columns // LANES * nodes // LANES + 4,)),
+            pltpu.SemaphoreType.DMA((columns // LANES + 4,)),
         ],
         compiler_params=params(),
         name="rows",
     )(*(in_hbm(x) for x in (send_rows, action.reshape(columns, nodes), edge_angle, edge_speed, neighbours)))
-    slots = slots.reshape(-1)
     far = swap_far_parts(far)
     near = swap_near(near, "dom")
-    weight, base, share_weight, share_base, share_slots, order = pl.pallas_call(
+    weight, base, share_weight, share_base, slots, share_slots, order = pl.pallas_call(
         weights_body,
         out_shape=(
             weights,
             bases,
             jax.ShapeDtypeStruct((NEIGH * 8 * ghost, LANES), F32),
             jax.ShapeDtypeStruct((8 * ghost, LANES), F32),
-            jax.ShapeDtypeStruct((NEIGH * 2 * ghost,), jnp.int32),
-            jax.ShapeDtypeStruct((nodes // 2 + 8,), jnp.int32),
+            pltpu.SMEM(((NEIGH + 2) * nodes,), jnp.int32),
+            pltpu.SMEM((NEIGH * 2 * ghost,), jnp.int32),
+            pltpu.SMEM((nodes // 2 + 8,), jnp.int32),
         ),
-        in_specs=[HBM, SMEM] + [VMEM] * 3,
-        out_specs=(VMEM, VMEM, VMEM, VMEM, SMEM, SMEM),
-        scratch_shapes=[pltpu.SMEM((2, ghost), jnp.int32), pltpu.SemaphoreType.DMA],
+        in_specs=[HBM] + [VMEM] * 4,
+        out_specs=(VMEM,) * 4 + (SMEM,) * 3,
+        scratch_shapes=[
+            pltpu.SMEM((2, ghost), jnp.int32),
+            pltpu.SemaphoreType.DMA(((NEIGH + 2) * nodes // LANES + 1,)),
+        ],
         compiler_params=params(),
         cost_estimate=cost(1 << 30, 8 << 20),
         name="weights",
     )(in_hbm(send_rows), slots, angle, speed, field)
 
     for _ in range(2):
-        field, far = pl.pallas_call(
-            far_body,
-            out_shape=(fields, shares),
+        field, far, near = pl.pallas_call(
+            shared_body,
+            out_shape=(fields, shares, shares),
             in_specs=[SMEM] + [VMEM] * 5,
-            out_specs=(VMEM, VMEM),
+            out_specs=(VMEM, VMEM, VMEM),
             input_output_aliases={1: 0},
             compiler_params=params(),
-            name="shared_far",
+            name="shared",
         )(share_slots, field, far, near, share_weight, share_base)
         far = swap_far_parts(far)
-        near = pl.pallas_call(
-            near_body,
-            out_shape=shares,
-            in_specs=[SMEM] + [VMEM] * 3,
-            out_specs=VMEM,
-            compiler_params=params(),
-            cost_estimate=cost(1 << 27, 1 << 20),
-            name="shared_near",
-        )(share_slots, field, share_weight, share_base)
         near = swap_near(near, "dom")
         field = pl.pallas_call(
             sweep_body,

time: 43.7 us -> 37.4 us (0.86)
  Pallas kernels: 24.9 us -> 17.9 us
  starting transfers between devices: 15.6 us -> 16.6 us
    pallas_call x4 -> x2, Pallas kernels: 2.83 us -> 0.68 us  [shards(): pl.pallas_call(shared_body, out_shape=(fields, shares, shares), in_specs=...]
    pallas_call x2, Pallas kernels: 7.07 us -> 5.46 us  [shards(): pl.pallas_call(sweep_body, out_shape=fields, in_specs=[SMEM] + [VMEM] * 3...]
    ppermute x4, starting transfers between devices: 1.56 us -> 0.01 us  [swap_near(): lax.ppermute(array, axis, [p for i in range(0, count, 2) for p in ((i, i...]
    ppermute x3, starting transfers between devices: 8.33 us -> 9.87 us  [swap_far_parts(): return lax.ppermute(array, ('dom', 'dir'), pairs)]
    pallas_call x1, Pallas kernels: 2.74 us -> 1.66 us  [shards(): pl.pallas_call(rows_body, out_shape=(fields, shares, shares, edges, edges...]
    ppermute x1, starting transfers between devices: 5.66 us -> 6.74 us  [swap_far_sectors(): return lax.ppermute(array, 'dir', pairs)]
    pallas_call x1, Pallas kernels: 4.76 us -> 3.95 us  [shards(): pl.pallas_call(weights_body, out_shape=(weights, bases, jax.ShapeDtypeStr...]
    pallas_call x1, Pallas kernels: 3.05 us -> 2.27 us  [shards(): pl.pallas_call(last_body, out_shape=(fields, swept_rows, edge, edge), in_...]
  transfers between devices with their start and end apart: 8 -> 8, of which waited for: 2 -> 3; matrix products, arithmetic and copies ran while one was open for 0% -> 0% of each run, Pallas kernels for 36% -> 33%
where the time goes in v6:
time: 37.4 us
  Pallas kernels  17.9 us (48%)
  starting transfers between devices  16.6 us (44%)
  waiting for transfers between devices  2.72 us (7%)
    ppermute x3, starting transfers between devices, swap_far_parts(): return lax.ppermute(array, ('dom', 'dir'), pairs)  9.87 us
    ppermute x1, starting transfers between devices, swap_far_sectors(): return lax.ppermute(array, 'dir', pairs)  6.74 us
    pallas_call x2, Pallas kernels, shards(): pl.pallas_call(sweep_body, out_shape=fields, in_specs=[SMEM] + [VMEM] * 3...  5.46 us
    pallas_call x1, Pallas kernels, shards(): pl.pallas_call(weights_body, out_shape=(weights, bases, jax.ShapeDtypeStr...  3.95 us
    pallas_call x1, Pallas kernels, shards(): pl.pallas_call(last_body, out_shape=(fields, swept_rows, edge, edge), in_...  2.27 us
    pallas_call x1, Pallas kernels, shards(): pl.pallas_call(rows_body, out_shape=(fields, shares, shares, edges, edges...  1.66 us
    pallas_call x1, Pallas kernels, shards(): pl.pallas_call(inner_body, out_shape=(plane_shape, jax.ShapeDtypeStruct((...  1.63 us
    ppermute x3, waiting for transfers between devices, swap_far_parts(): return lax.ppermute(array, ('dom', 'dir'), pairs)  1.56 us
  transfers between devices with their start and end apart: 8, of which 3 were waited for; matrix products, arithmetic and copies ran while one was open for 0% of the time, Pallas kernels for 33%

profile of v6, /device:TPU:129, one launch (start us, length us, event | category | flops | bytes accessed | tf_op | source)
XLA Modules:
  0.0 37.4 jit_solution(958225525549628552)
XLA Ops:
  0.0 1.7 %rows.1 = (f32[2320,128]{1,0:T(8,128)S(1)}, f32[128,128]{1,0:T(8,128)S(1)}, f32[128,128]{1,0:T(8,128)S(1)}, f32[6,512]{1,0:T(8,128)S(1)}, f32[6,512]{1,0:T(8,128)S(1)}, /*index=5*/s32[32,128]{1,0:T(8,128)S(1)}) custom-call(s32[2,32]{1,0:T(2,128)} %send_hbm.3, f32[512,512]{1,0:T(8,128)} %bitcast.5, f32[6,512]{1,0:T(8,128)} %angle_hbm.1, f32[6,512]{1,0:T(8,128)} %speed_hbm.1, ...), custom_call_target="tpu_custom_call" | custom-call | tf_op jit(solution)/shard_map/rows/pallas_call | solution.py:347
  1.7 3.3 %collective-permute-start = (f32[128,128]{1,0:T(8,128)S(1)}, f32[128,128]{1,0:T(8,128)S(1)}, u32[]{:S(2)}, u32[]{:S(2)}) collective-permute-start(f32[128,128]{1,0:T(8,128)S(1)} %get-tuple-element.36), channel_id=1, source_target_pairs={{4,8},{8,4},{12,16},{16,12},{20,24},{24,20},{28,32},{32,28},{36,40... | collective-permute-start | bytes 196616 | tf_op jit(solution)/shard_map/ppermute | solution.py:319
  5.0 0.0 collective-permute-start.1
  5.0 4.0 %weights.1 = (f32[12304,128]{1,0:T(8,128)S(1)}, f32[2064,128]{1,0:T(8,128)S(1)}, f32[1536,128]{1,0:T(8,128)S(1)}, f32[256,128]{1,0:T(8,128)S(1)}, s32[4096]{0:T(...) custom-call(s32[2,32]{1,0:T(2,128)} %send_hbm.3, s32[32,128]{1,0:T(8,128)S(1)} %get-tuple-element.29.listed, ...), custom_call_target="tpu_custom_call" | custom-call | flops 1073741824 | bytes 8388608 | tf_op jit(solution)/shard_map/weights/pallas_call | solution.py:363
  8.9 0.2 collective-permute-done.from_far
  9.1 0.0 collective-permute-done.1.from_near
  9.1 0.3 shared.2
  9.4 3.3 %collective-permute-start.2 = (f32[128,128]{1,0:T(8,128)S(1)}, f32[128,128]{1,0:T(8,128)S(1)}, u32[]{:S(2)}, u32[]{:S(2)}) collective-permute-start(f32[128,128]{1,0:T(8,128)S(1)} %get-tuple-element.43), channel_id=1, source_target_pairs={{4,8},{8,4},{12,16},{16,12},{20,24},{24,20},{28,32},{32,28},{36,40... | collective-permute-start | bytes 196616 | tf_op jit(solution)/shard_map/ppermute | solution.py:319
  12.7 0.0 collective-permute-start.3
  12.7 2.7 %sweep.2.field_in = f32[2320,128]{1,0:T(8,128)S(1)} custom-call(s32[4096]{0:T(1024)S(4)} %get-tuple-element.34.slots, f32[2320,128]{1,0:T(8,128)S(1)} %get-tuple-element.40.field, f32[12304,128]{1,0:T(8,128)S(1)} %get-tuple-element.41.weight, f32[2064,128]{1,0:T(8,128)S(1)} %get-tuple-element.42.base), custom_call_target="tpu_custom_call" | custom-call | flops 1073741824 | bytes 8388608 | tf_op jit(solution)/shard_map/sweep/pallas_call | solution.py:397
  15.5 1.4 %collective-permute-done.2.from_far = f32[128,128]{1,0:T(8,128)S(1)} collective-permute-done((f32[128,128]{1,0:T(8,128)S(1)}, f32[128,128]{1,0:T(8,128)S(1)}, u32[]{:S(2)}, u32[]{:S(2)}) %collective-permute-start.2) | collective-permute-done | bytes 65568 | tf_op jit(solution)/shard_map/ppermute | solution.py:319
  16.9 0.0 collective-permute-done.3.from_near
  16.9 0.3 shared.3
  17.2 3.3 %collective-permute-start.4 = (f32[128,128]{1,0:T(8,128)S(1)}, f32[128,128]{1,0:T(8,128)S(1)}, u32[]{:S(2)}, u32[]{:S(2)}) collective-permute-start(f32[128,128]{1,0:T(8,128)S(1)} %get-tuple-element.46), channel_id=1, source_target_pairs={{4,8},{8,4},{12,16},{16,12},{20,24},{24,20},{28,32},{32,28},{36,40... | collective-permute-start | bytes 196616 | tf_op jit(solution)/shard_map/ppermute | solution.py:319
  20.5 0.0 collective-permute-start.5
  20.5 2.7 %sweep.3.field.field_in = f32[2320,128]{1,0:T(8,128)S(1)} custom-call(s32[4096]{0:T(1024)S(4)} %get-tuple-element.34.slots, f32[2320,128]{1,0:T(8,128)S(1)} %get-tuple-element.45.field, f32[12304,128]{1,0:T(8,128)S(1)} %get-tuple-element.41.weight, f32[2064,128]{1,0:T(8,128)S(1)} %get-tuple-element.42.base), custom_call_target="tpu_custom_call" | custom-call | flops 1073741824 | bytes 8388608 | tf_op jit(solution)/shard_map/sweep/pallas_call | solution.py:397
  23.2 1.4 %last_sweep_early.1.rows_in = f32[2048,128]{1,0:T(8,128)S(1)} custom-call(s32[264]{0:T(512)S(4)} %get-tuple-element.33.order, s32[4096]{0:T(1024)S(4)} %get-tuple-element.34.slots, f32[2320,128]{1,0:T(8,128)S(1)} %sweep.3.field.field_in, f32[12304,128]{1,0:T(8,128)S(1)} %get-tuple-element.41.weight, f32[2064,128]{1,0:T(8,128)S(1)} %get-tuple-element.42.base), custom_call_target="tpu_custom_call" | custom-call | flops 536870912 | bytes 4194304 | tf_op jit(solution)/shard_map/last_sweep_early/pallas_call | solution.py:410
  24.7 0.0 copy-start
  24.7 0.0 copy-start.1
  24.7 0.0 copy-start.2
  24.7 0.0 collective-permute-done.4.from_far
  24.7 0.0 collective-permute-done.5.from_near
  24.7 2.3 %last_sweep.1 = (f32[2320,128]{1,0:T(8,128)S(1)}, f32[2048,128]{1,0:T(8,128)S(1)}, f32[32,512]{1,0:T(8,128)S(1)}, f32[32,512]{1,0:T(8,128)S(1)}) custom-call(s32[264]{0:T(512)S(4)} %get-tuple-element.33.order, s32[4096]{0:T(1024)S(4)} %get-tuple-element.34.slots, f32[2320,128]{1,0:T(8,128)S(1)} %sweep.3.field.field_in, ...), custom_call_target="tpu_custom_call", output_to_operand_aliasing={{0}: (2, {}), {1}: (7, {})} | custom-call | tf_op jit(solution)/shard_map/last_sweep/pallas_call | solution.py:419
  27.0 6.7 %collective-permute-start.6 = (f32[32,512]{1,0:T(8,128)S(1)}, f32[32,512]{1,0:T(8,128)S(1)}, u32[]{:S(2)}, u32[]{:S(2)}) collective-permute-start(f32[32,512]{1,0:T(8,128)S(1)} %get-tuple-element.50), channel_id=1, source_target_pairs={{1,2},{2,1},{3,0},{0,3},{5,6},{6,5},{7,4},{4,7},{9,10},{10,9},{11,... | collective-permute-start | bytes 196616 | tf_op jit(solution)/shard_map/ppermute | solution.py:325
  33.7 0.0 collective-permute-start.7
  33.7 0.0 copy-done
  33.7 0.0 copy-done.1
  33.7 0.0 copy-done.2
  33.8 1.6 %inner_planes.1 = (f32[512,512]{1,0:T(8,128)}, f32[4,32,512]{2,1,0:T(8,128)S(1)}) custom-call(f32[2048,128]{1,0:T(8,128)S(1)} %get-tuple-element.48.rows, f32[32,512]{1,0:T(8,128)S(1)} %copy-done, f32[1,512]{1,0:T(1,128)S(1)} %bitcast.3, f32[32,512]{1,0:T(8,128)S(1)} %copy-done.1), custom_call_target="tpu_custom_call" | custom-call | flops 268435456 | bytes 2097152 | tf_op jit(solution)/shard_map/inner_planes/pallas_call | solution.py:430
  35.4 1.1 %collective-permute-done.6.from_far = f32[32,512]{1,0:T(8,128)S(1)} collective-permute-done((f32[32,512]{1,0:T(8,128)S(1)}, f32[32,512]{1,0:T(8,128)S(1)}, u32[]{:S(2)}, u32[]{:S(2)}) %collective-permute-start.6) | collective-permute-done | bytes 65568 | tf_op jit(solution)/shard_map/ppermute | solution.py:325
  36.5 0.0 collective-permute-done.7.from_near
  36.5 0.8 %edge_planes.1 = f32[512,512]{1,0:T(8,128)} custom-call(f32[4,32,512]{2,1,0:T(8,128)S(1)} %get-tuple-element.49.ends, f32[32,512]{1,0:T(8,128)S(1)} %collective-permute-done.6.from_far, f32[32,512]{1,0:T(8,128)S(1)} %collective-permute-done.7.from_near, f32[32,512]{1,0:T(8,128)S(1)} %copy-done, ...), custom_call_target="tpu_custom_call", output_to_operand_aliasing={{}: (6, {})} | custom-call | tf_op jit(solution)/shard_map/edge_planes/pallas_call | solution.py:444
Async XLA Ops:
  1.7 7.4 %collective-permute-start = (f32[128,128]{1,0:T(8,128)S(1)}, f32[128,128]{1,0:T(8,128)S(1)}, u32[]{:S(2)}, u32[]{:S(2)}) collective-permute-start(f32[128,128]{1,0:T(8,128)S(1)} %get-tuple-element.36), channel_id=1, source_target_pairs={{4,8},{8,4},{12,16},{16,12},{20,24},{24,20},{28,32},{32,28},{36,40... | collective-permute-start | bytes 196616 | tf_op jit(solution)/shard_map/ppermute | solution.py:319
  5.0 4.1 %collective-permute-start.1 = (f32[128,128]{1,0:T(8,128)S(1)}, f32[128,128]{1,0:T(8,128)S(1)}, u32[]{:S(2)}, u32[]{:S(2)}) collective-permute-start(f32[128,128]{1,0:T(8,128)S(1)} %get-tuple-element.37), channel_id=1, source_target_pairs={{0,4},{4,0},{8,12},{12,8},{16,20},{20,16},{24,28},{28,24},{32,36},... | collective-permute-start | bytes 196616 | tf_op jit(solution)/shard_map/ppermute | solution.py:330
  9.4 7.4 %collective-permute-start.2 = (f32[128,128]{1,0:T(8,128)S(1)}, f32[128,128]{1,0:T(8,128)S(1)}, u32[]{:S(2)}, u32[]{:S(2)}) collective-permute-start(f32[128,128]{1,0:T(8,128)S(1)} %get-tuple-element.43), channel_id=1, source_target_pairs={{4,8},{8,4},{12,16},{16,12},{20,24},{24,20},{28,32},{32,28},{36,40... | collective-permute-start | bytes 196616 | tf_op jit(solution)/shard_map/ppermute | solution.py:319
  12.7 4.1 %collective-permute-start.3 = (f32[128,128]{1,0:T(8,128)S(1)}, f32[128,128]{1,0:T(8,128)S(1)}, u32[]{:S(2)}, u32[]{:S(2)}) collective-permute-start(f32[128,128]{1,0:T(8,128)S(1)} %get-tuple-element.44), channel_id=1, source_target_pairs={{0,4},{4,0},{8,12},{12,8},{16,20},{20,16},{24,28},{28,24},{32,36},... | collective-permute-start | bytes 196616 | tf_op jit(solution)/shard_map/ppermute | solution.py:330
  17.2 7.5 %collective-permute-start.4 = (f32[128,128]{1,0:T(8,128)S(1)}, f32[128,128]{1,0:T(8,128)S(1)}, u32[]{:S(2)}, u32[]{:S(2)}) collective-permute-start(f32[128,128]{1,0:T(8,128)S(1)} %get-tuple-element.46), channel_id=1, source_target_pairs={{4,8},{8,4},{12,16},{16,12},{20,24},{24,20},{28,32},{32,28},{36,40... | collective-permute-start | bytes 196616 | tf_op jit(solution)/shard_map/ppermute | solution.py:319
  20.5 4.2 %collective-permute-start.5 = (f32[128,128]{1,0:T(8,128)S(1)}, f32[128,128]{1,0:T(8,128)S(1)}, u32[]{:S(2)}, u32[]{:S(2)}) collective-permute-start(f32[128,128]{1,0:T(8,128)S(1)} %get-tuple-element.47), channel_id=1, source_target_pairs={{0,4},{4,0},{8,12},{12,8},{16,20},{20,16},{24,28},{28,24},{32,36},... | collective-permute-start | bytes 196616 | tf_op jit(solution)/shard_map/ppermute | solution.py:330
  24.7 9.1 %copy-start = (f32[32,512]{1,0:T(8,128)S(1)}, f32[32,512]{1,0:T(8,128)}, u32[]{:S(2)}) copy-start(f32[32,512]{1,0:T(8,128)} %rate.3) | copy-start | bytes 196612
  24.7 9.1 %copy-start.1 = (f32[32,512]{1,0:T(8,128)S(1)}, f32[32,512]{1,0:T(8,128)}, u32[]{:S(2)}) copy-start(f32[32,512]{1,0:T(8,128)} %shift.3) | copy-start | bytes 196612
  24.7 9.1 %copy-start.2 = (f32[512]{0:T(512)S(1)}, f32[512]{0:T(512)}, u32[]{:S(2)}) copy-start(f32[512]{0:T(512)} %param.14) | copy-start | bytes 6148
  27.0 9.5 %collective-permute-start.6 = (f32[32,512]{1,0:T(8,128)S(1)}, f32[32,512]{1,0:T(8,128)S(1)}, u32[]{:S(2)}, u32[]{:S(2)}) collective-permute-start(f32[32,512]{1,0:T(8,128)S(1)} %get-tuple-element.50), channel_id=1, source_target_pairs={{1,2},{2,1},{3,0},{0,3},{5,6},{6,5},{7,4},{4,7},{9,10},{10,9},{11,... | collective-permute-start | bytes 196616 | tf_op jit(solution)/shard_map/ppermute | solution.py:325
  33.7 2.8 %collective-permute-start.7 = (f32[32,512]{1,0:T(8,128)S(1)}, f32[32,512]{1,0:T(8,128)S(1)}, u32[]{:S(2)}, u32[]{:S(2)}) collective-permute-start(f32[32,512]{1,0:T(8,128)S(1)} %get-tuple-element.51), channel_id=1, source_target_pairs={{0,1},{1,0},{2,3},{3,2},{4,5},{5,4},{6,7},{7,6},{8,9},{9,8},{10,11... | collective-permute-start | bytes 196616 | tf_op jit(solution)/shard_map/ppermute | solution.py:330

commit v7 on v6

--- a/solution.py
+++ b/solution.py
@@ -10,7 +10,8 @@
 NDIR = 64
 NEIGH = 6
 LANES = 128
-EARLY = 14
+GROUP = 16
+EARLY = 7
 PAD = 8
 
 F32 = jnp.float32
@@ -82,7 +83,7 @@
 
 def weights_body(
     send_hbm, listed, edge_angle, edge_speed, field,
-    weight, base, share_weight, share_base, slots, share_slots, order, send, sems,
+    weight, base, share_weight, share_base, plane_weight, pick, slots, share_slots, order, send, sems,
 ):
     rows = listed.shape[0]
     copies = [
@@ -117,7 +118,14 @@
         pieces = jnp.concatenate([high, middle, last], axis=0)
         return lax.dot_general(pieces, spread, (((0,), (0,)), ((), ())), preferred_element_type=F32)
 
+    ghost = send.shape[1]
+    number = (lax.broadcasted_iota(jnp.int32, (2 * ghost, LANES), 0) + nodes) * 4
+    blocks = nodes // LANES
     for j in range(NEIGH):
+        for b in range(blocks):
+            chosen = (number == listed[pl.ds(j * blocks + b, 1), :]).astype(F32).astype(jnp.bfloat16)
+            pick[pl.ds(j * 6 * ghost, 6 * ghost), b * LANES : (b + 1) * LANES] = jnp.concatenate([chosen] * 3, axis=0)
+        plane_weight[pl.ds(j * sector, sector), :] = parts[j] * inverse
         wide = widened(parts[j] * inverse)
         for c in range(4):
             weight[pl.ds(PAD + j * 4 * nodes + c, nodes, stride=4), :] = wide[:, c * LANES : (c + 1) * LANES]
@@ -129,7 +137,6 @@
         copy.wait()
     low = low_half()
     far = odd("dom")
-    ghost = send.shape[1]
     for k, row in enumerate((far, 1 - far)):
         for i in range(0, ghost, 2):
             n = send[row, i]
@@ -195,47 +202,93 @@
     return row, total
 
 
-def sweep_body(slots, field, weight, base, out):
+def clear_ghosts(out, nodes):
+    rows = out.shape[0] - 2 * PAD - 4 * nodes
+    out[pl.ds(PAD + 4 * nodes, rows), :] = jnp.zeros((rows, LANES), F32)
+
+
+def all_pairs(slots, field, weight, base, out, offset):
     low = low_half()
     nodes = (base.shape[0] - 2 * PAD) // 4
 
     def step(i, carry):
         row, total = pair_row(slots, field, weight, base, i, nodes, low)
-        out[pl.ds(PAD + row, 8), :] = total
+        out[pl.ds(offset + row, 8), :] = total
         return carry
 
-    lax.fori_loop(0, nodes // 2, step, 0, unroll=8)
-
-
-def listed_pairs(order, slots, field, weight, base, rows, first, until):
+    lax.fori_loop(0, nodes // 2, step, 0, unroll=GROUP)
+
+
+def listed_pairs(order, slots, field, weight, base, out, first, until):
     low = low_half()
-    nodes = rows.shape[0] // 4
+    nodes = (base.shape[0] - 2 * PAD) // 4
 
     def step(g, carry):
-        for u in range(8):
-            row, total = pair_row(slots, field, weight, base, order[g * 8 + u], nodes, low)
-            rows[pl.ds(row, 8), :] = total
+        for u in range(GROUP):
+            row, total = pair_row(slots, field, weight, base, order[g * GROUP + u], nodes, low)
+            out[pl.ds(PAD + row, 8), :] = total
         return carry
 
     lax.fori_loop(first, until, step, 0)
 
 
 def early_groups(order, nodes):
-    return jnp.minimum(order[nodes // 2] // 8, EARLY)
-
-
-def early_body(order, slots, field, weight, base, rows):
-    listed_pairs(order, slots, field, weight, base, rows, 0, early_groups(order, rows.shape[0] // 4))
-
-
-def last_body(order, slots, field_in, from_far, from_near, weight, base, rows_in, field, rows, to_far, to_near):
-    del field_in, rows_in
-    nodes = rows.shape[0] // 4
-    place_ghosts(field, from_far, from_near, nodes)
-    listed_pairs(order, slots, field, weight, base, rows, early_groups(order, nodes), nodes // 16)
+    return jnp.minimum(order[nodes // 2] // GROUP, EARLY)
+
+
+def first_body(order, slots, field, weight, base, swept, second):
+    nodes = (base.shape[0] - 2 * PAD) // 4
+    all_pairs(slots, field, weight, base, swept, PAD)
+    clear_ghosts(second, nodes)
+    listed_pairs(order, slots, swept, weight, base, second, 0, early_groups(order, nodes))
+
+
+def second_body(order, slots, field, weight, base, second_in, second, planes, rows):
+    del second_in
+    nodes = (base.shape[0] - 2 * PAD) // 4
+    listed_pairs(order, slots, field, weight, base, second, early_groups(order, nodes), nodes // (2 * GROUP))
+    all_pairs(slots, second, weight, base, rows, 0)
+    for c in range(planes.shape[0] // LANES):
+        planes[pl.ds(c * LANES, LANES), :] = rows[pl.ds(c, nodes, stride=4), :].T
+
+
+def received_rows(from_far, from_near, c):
+    count = from_far.shape[0] // 4
+    part = lax.axis_index("dom")
+    inside = jnp.logical_and(part > 0, part < lax.axis_size("dom") - 1)
+    far = jnp.where(inside, from_far[pl.ds(c, count, stride=4), :], 0.0)
+    near = from_near[pl.ds(c, count, stride=4), :]
+    swap = odd("dom") > 0
+    return jnp.concatenate([jnp.where(swap, near, far), jnp.where(swap, far, near)], axis=0)
+
+
+def in_pieces(value):
+    high = value.astype(jnp.bfloat16)
+    rest = value - high.astype(F32)
+    middle = rest.astype(jnp.bfloat16)
+    last = (rest - middle.astype(F32)).astype(jnp.bfloat16)
+    return jnp.concatenate([high, middle, last], axis=0)
+
+
+def selected(pieces, pick, j):
+    depth = pieces.shape[0]
+    return lax.dot_general(
+        pieces, pick[pl.ds(j * depth, depth), :], (((0,), (0,)), ((), ())), preferred_element_type=F32
+    )
+
+
+def arrive_body(from_far, from_near, pick, plane_weight, planes, to_far, to_near):
     freq = to_far.shape[0]
-    first = rows[pl.ds(0, nodes, stride=4), :].T[:freq, :]
-    last = rows[pl.ds(3, nodes, stride=4), :].T[LANES - freq :, :]
+    sector = planes.shape[0] // freq
+    rows = received_rows(from_far, from_near, 0)
+    lane = lax.broadcasted_iota(jnp.int32, rows.shape, 1)
+    pieces = in_pieces(jnp.where(lane < freq, rows, received_rows(from_far, from_near, 3)))
+    first = planes[pl.ds(0, freq), :]
+    last = planes[pl.ds((sector - 1) * freq, freq), :]
+    for j in range(NEIGH):
+        found = selected(pieces, pick, j)
+        first = first + plane_weight[pl.ds(j * sector, 1), :] * found[:freq, :]
+        last = last + plane_weight[pl.ds(j * sector + sector - 1, 1), :] * found[LANES - freq :, :]
     far = odd("dir") > 0
     to_far[...] = jnp.where(far, last, first)
     to_near[...] = jnp.where(far, first, last)
@@ -252,7 +305,9 @@
     return value - (jnp.maximum(shift, 0.0) * (value - under) + jnp.minimum(shift, 0.0) * (over - value))
 
 
-def inner_body(rows, rate, bearing, shift, out, ends, swept, stage, sems):
+def inner_body(
+    from_far, from_near, pick, plane_weight, planes, rate, bearing, shift, out, ends, swept, stage, sems
+):
     freq, nodes = rate.shape
     chunks = swept.shape[0] // LANES
     width = LANES // freq
@@ -261,7 +316,15 @@
     copies = []
     done = 1
     for c in range(chunks):
-        swept[pl.ds(c * LANES, LANES), :] = rows[pl.ds(c, nodes, stride=4), :].T
+        pieces = in_pieces(received_rows(from_far, from_near, c))
+        total = [planes[pl.ds((c * width + k) * freq, freq), :] for k in range(width)]
+        for j in range(NEIGH):
+            found = selected(pieces, pick, j)
+            for k in range(width):
+                w = plane_weight[pl.ds(j * sector + c * width + k, 1), :]
+                total[k] = total[k] + w * found[k * freq : (k + 1) * freq, :]
+        for k in range(width):
+            swept[pl.ds((c * width + k) * freq, freq), :] = total[k]
         until = (c + 1) * width - 1
         for d in range(done, until):
             stage[pl.ds((d - 1) * freq, freq), :] = finished(
@@ -360,19 +423,21 @@
     )(*(in_hbm(x) for x in (send_rows, action.reshape(columns, nodes), edge_angle, edge_speed, neighbours)))
     far = swap_far_parts(far)
     near = swap_near(near, "dom")
-    weight, base, share_weight, share_base, slots, share_slots, order = pl.pallas_call(
+    weight, base, share_weight, share_base, plane_weight, pick, slots, share_slots, order = pl.pallas_call(
         weights_body,
         out_shape=(
             weights,
             bases,
             jax.ShapeDtypeStruct((NEIGH * 8 * ghost, LANES), F32),
             jax.ShapeDtypeStruct((8 * ghost, LANES), F32),
+            jax.ShapeDtypeStruct((NEIGH * sector, nodes), F32),
+            jax.ShapeDtypeStruct((NEIGH * 6 * ghost, nodes), jnp.bfloat16),
             pltpu.SMEM(((NEIGH + 2) * nodes,), jnp.int32),
             pltpu.SMEM((NEIGH * 2 * ghost,), jnp.int32),
             pltpu.SMEM((nodes // 2 + 8,), jnp.int32),
         ),
         in_specs=[HBM] + [VMEM] * 4,
-        out_specs=(VMEM,) * 4 + (SMEM,) * 3,
+        out_specs=(VMEM,) * 6 + (SMEM,) * 3,
         scratch_shapes=[
             pltpu.SMEM((2, ghost), jnp.int32),
             pltpu.SemaphoreType.DMA(((NEIGH + 2) * nodes // LANES + 1,)),
@@ -382,7 +447,7 @@
         name="weights",
     )(in_hbm(send_rows), slots, angle, speed, field)
 
-    for _ in range(2):
+    def shared(field, far, near):
         field, far, near = pl.pallas_call(
             shared_body,
             out_shape=(fields, shares, shares),
@@ -392,45 +457,47 @@
             compiler_params=params(),
             name="shared",
         )(share_slots, field, far, near, share_weight, share_base)
-        far = swap_far_parts(far)
-        near = swap_near(near, "dom")
-        field = pl.pallas_call(
-            sweep_body,
-            out_shape=fields,
-            in_specs=[SMEM] + [VMEM] * 3,
-            out_specs=VMEM,
-            compiler_params=params(),
-            cost_estimate=cost(1 << 30, 8 << 20),
-            name="sweep",
-        )(slots, field, weight, base)
+        return field, swap_far_parts(far), swap_near(near, "dom")
+
+    field, far, near = shared(field, far, near)
+    field, second = pl.pallas_call(
+        first_body,
+        out_shape=(fields, fields),
+        in_specs=[SMEM, SMEM] + [VMEM] * 3,
+        out_specs=(VMEM, VMEM),
+        compiler_params=params(),
+        cost_estimate=cost(1 << 30, 8 << 20),
+        name="first_sweep",
+    )(order, slots, field, weight, base)
+    field, far, near = shared(field, far, near)
+    _, planes = pl.pallas_call(
+        second_body,
+        out_shape=(fields, jax.ShapeDtypeStruct((columns, nodes), F32)),
+        in_specs=[SMEM, SMEM] + [VMEM] * 4,
+        out_specs=(VMEM, VMEM),
+        input_output_aliases={5: 0},
+        scratch_shapes=[pltpu.VMEM((4 * nodes, LANES), F32)],
+        compiler_params=params(),
+        cost_estimate=cost(1 << 31, 16 << 20),
+        name="second_sweep",
+    )(order, slots, field, weight, base, second)
 
     edge = jax.ShapeDtypeStruct((freq, nodes), F32)
     plane_shape = jax.ShapeDtypeStruct((columns, nodes), F32)
-    swept_rows = jax.ShapeDtypeStruct((4 * nodes, LANES), F32)
-    rows = pl.pallas_call(
-        early_body,
-        out_shape=swept_rows,
-        in_specs=[SMEM, SMEM] + [VMEM] * 3,
-        out_specs=VMEM,
-        compiler_params=params(),
-        cost_estimate=cost(1 << 29, 4 << 20),
-        name="last_sweep_early",
-    )(order, slots, field, weight, base)
-    _, rows, far_plane, near_plane = pl.pallas_call(
-        last_body,
-        out_shape=(fields, swept_rows, edge, edge),
-        in_specs=[SMEM, SMEM] + [VMEM] * 6,
-        out_specs=(VMEM,) * 4,
-        input_output_aliases={2: 0, 7: 1},
-        compiler_params=params(),
-        name="last_sweep",
-    )(order, slots, field, far, near, weight, base, rows)
+    far_plane, near_plane = pl.pallas_call(
+        arrive_body,
+        out_shape=(edge, edge),
+        in_specs=[VMEM] * 5,
+        out_specs=(VMEM, VMEM),
+        compiler_params=params(),
+        name="last_sweep_edges",
+    )(far, near, pick, plane_weight, planes)
     far_plane = swap_far_sectors(far_plane)
     near_plane = swap_near(near_plane, "dir")
     out, ends = pl.pallas_call(
         inner_body,
         out_shape=(plane_shape, jax.ShapeDtypeStruct((4, freq, nodes), F32)),
-        in_specs=[VMEM] * 4,
+        in_specs=[VMEM] * 8,
         out_specs=(ANY, VMEM),
         scratch_shapes=[
             pltpu.VMEM((columns, nodes), F32),
@@ -440,7 +507,7 @@
         compiler_params=params(),
         cost_estimate=cost(1 << 28, 2 << 20),
         name="inner_planes",
-    )(rows, refract_rate, bearing, shift_rate)
+    )(far, near, pick, plane_weight, planes, refract_rate, bearing, shift_rate)
     out = pl.pallas_call(
         edge_body,
         out_shape=plane_shape,

time: 37.4 us -> 35.8 us (0.957)
  waiting for transfers between devices: 2.72 us -> 0.37 us
  Pallas kernels: 17.9 us -> 19.6 us
  starting transfers between devices: 16.6 us -> 15.5 us
    ppermute x3, waiting for transfers between devices: 1.56 us -> 0.36 us  [swap_far_parts(): return lax.ppermute(array, ('dom', 'dir'), pairs)]
    pallas_call x1, Pallas kernels: 1.63 us -> 2.78 us  [shards(): pl.pallas_call(inner_body, out_shape=(plane_shape, jax.ShapeDtypeStruct((...]
    ppermute x1, waiting for transfers between devices: 1.14 us -> 0.01 us  [swap_far_sectors(): return lax.ppermute(array, 'dir', pairs)]
    ppermute x1, starting transfers between devices: 6.74 us -> 6.1 us  [swap_far_sectors(): return lax.ppermute(array, 'dir', pairs)]
    ppermute x3, starting transfers between devices: 9.87 us -> 9.34 us  [swap_far_parts(): return lax.ppermute(array, ('dom', 'dir'), pairs)]
    pallas_call x1, Pallas kernels: 3.95 us -> 4.36 us  [shards(): pl.pallas_call(weights_body, out_shape=(weights, bases, jax.ShapeDtypeStr...]
    pallas_call x6 -> x5, Pallas kernels: 9.83 us -> 9.97 us  [the longest x1 4.82 us: shards(): pl.pallas_call(second_body, out_shape=(fields, jax.ShapeDtypeStruct((colu...]
  transfers between devices with their start and end apart: 8 -> 8, of which waited for: 3 -> 1; matrix products, arithmetic and copies ran while one was open for 0% -> 0% of each run, Pallas kernels for 33% -> 45%
where the time goes in v7:
time: 35.8 us; the launch traced here: 35.6 us
  Pallas kernels  19.6 us (55%)
  starting transfers between devices  15.5 us (43%)
  waiting for transfers between devices  0.37 us (1%)
    ppermute x3, starting transfers between devices, swap_far_parts(): return lax.ppermute(array, ('dom', 'dir'), pairs)  9.34 us
    ppermute x1, starting transfers between devices, swap_far_sectors(): return lax.ppermute(array, 'dir', pairs)  6.1 us
    pallas_call x1, Pallas kernels, shards(): pl.pallas_call(second_body, out_shape=(fields, jax.ShapeDtypeStruct((colu...  4.82 us
    pallas_call x1, Pallas kernels, shards(): pl.pallas_call(weights_body, out_shape=(weights, bases, jax.ShapeDtypeStr...  4.36 us
    pallas_call x1, Pallas kernels, shards(): pl.pallas_call(first_body, out_shape=(fields, fields), in_specs=[SMEM, SM...  4.04 us
    pallas_call x1, Pallas kernels, shards(): pl.pallas_call(inner_body, out_shape=(plane_shape, jax.ShapeDtypeStruct((...  2.78 us
    pallas_call x1, Pallas kernels, shards(): pl.pallas_call(rows_body, out_shape=(fields, shares, shares, edges, edges...  1.66 us
    pallas_call x1, Pallas kernels, shards(): pl.pallas_call(edge_body, out_shape=plane_shape, in_specs=[VMEM] * 6 + [A...  0.82 us
  transfers between devices with their start and end apart: 8, of which 1 were waited for; matrix products, arithmetic and copies ran while one was open for 0% of the time, Pallas kernels for 45%

profile of v7, /device:TPU:129, one launch (start us, length us, event | category | flops | bytes accessed | tf_op | source)
XLA Modules:
  0.0 35.6 jit_solution(2062107208323976368)
XLA Ops:
  0.0 1.7 %rows.1 = (f32[2320,128]{1,0:T(8,128)S(1)}, f32[128,128]{1,0:T(8,128)S(1)}, f32[128,128]{1,0:T(8,128)S(1)}, f32[6,512]{1,0:T(8,128)S(1)}, f32[6,512]{1,0:T(8,128)S(1)}, /*index=5*/s32[32,128]{1,0:T(8,128)S(1)}) custom-call(s32[2,32]{1,0:T(2,128)} %send_hbm.3, f32[512,512]{1,0:T(8,128)} %bitcast.5, f32[6,512]{1,0:T(8,128)} %angle_hbm.1, f32[6,512]{1,0:T(8,128)} %speed_hbm.1, ...), custom_call_target="tpu_custom_call" | custom-call | tf_op jit(solution)/shard_map/rows/pallas_call | solution.py:410
  1.7 3.3 %collective-permute-start = (f32[128,128]{1,0:T(8,128)S(1)}, f32[128,128]{1,0:T(8,128)S(1)}, u32[]{:S(2)}, u32[]{:S(2)}) collective-permute-start(f32[128,128]{1,0:T(8,128)S(1)} %get-tuple-element.40), channel_id=1, source_target_pairs={{4,8},{8,4},{12,16},{16,12},{20,24},{24,20},{28,32},{32,28},{36,40... | collective-permute-start | bytes 196616 | tf_op jit(solution)/shard_map/ppermute | solution.py:382
  5.0 0.0 collective-permute-start.1
  5.0 4.4 %weights.1 = (f32[12304,128]{1,0:T(8,128)S(1)}, f32[2064,128]{1,0:T(8,128)S(1)}, f32[1536,128]{1,0:T(8,128)S(1)}, f32[256,128]{1,0:T(8,128)S(1)}, f32[96,512]{1,...) custom-call(s32[2,32]{1,0:T(2,128)} %send_hbm.3, ...), custom_call_target="tpu_custom_call" | custom-call | flops 1073741824 | bytes 8388608 | tf_op jit(solution)/shard_map/weights/pallas_call | solution.py:426
  9.3 0.0 collective-permute-done.from_far
  9.3 0.0 collective-permute-done.1.from_near
  9.4 0.3 shared.2
  9.7 3.0 %collective-permute-start.2 = (f32[128,128]{1,0:T(8,128)S(1)}, f32[128,128]{1,0:T(8,128)S(1)}, u32[]{:S(2)}, u32[]{:S(2)}) collective-permute-start(f32[128,128]{1,0:T(8,128)S(1)} %get-tuple-element.48), channel_id=1, source_target_pairs={{4,8},{8,4},{12,16},{16,12},{20,24},{24,20},{28,32},{32,28},{36,40... | collective-permute-start | bytes 196616 | tf_op jit(solution)/shard_map/ppermute | solution.py:382
  12.7 0.0 collective-permute-start.3
  12.7 4.0 %first_sweep.1 = (f32[2320,128]{1,0:T(8,128)S(1)}, f32[2320,128]{1,0:T(8,128)S(1)}) custom-call(s32[264]{0:T(512)S(4)} %get-tuple-element.38.order, s32[4096]{0:T(1024)S(4)} %get-tuple-element.39.slots, f32[2320,128]{1,0:T(8,128)S(1)} %get-tuple-element.44.field, f32[12304,128]{1,0:T(8,128)S(1)} %get-tuple-element.45.weight, ...), custom_call_target="tpu_custom_call" | custom-call | flops 1073741824 | bytes 8388608 | tf_op jit(solution)/shard_map/first_sweep/pallas_call | solution.py:463
  16.8 0.3 collective-permute-done.2.from_far
  17.1 0.0 collective-permute-done.3.from_near
  17.1 0.3 shared.3
  17.5 3.0 %collective-permute-start.4 = (f32[128,128]{1,0:T(8,128)S(1)}, f32[128,128]{1,0:T(8,128)S(1)}, u32[]{:S(2)}, u32[]{:S(2)}) collective-permute-start(f32[128,128]{1,0:T(8,128)S(1)} %get-tuple-element.50), channel_id=1, source_target_pairs={{4,8},{8,4},{12,16},{16,12},{20,24},{24,20},{28,32},{32,28},{36,40... | collective-permute-start | bytes 196616 | tf_op jit(solution)/shard_map/ppermute | solution.py:382
  20.5 0.0 collective-permute-start.5
  20.5 4.8 %second_sweep.1 = (f32[2320,128]{1,0:T(8,128)S(1)}, f32[512,512]{1,0:T(8,128)S(1)}) custom-call(s32[264]{0:T(512)S(4)} %get-tuple-element.38.order, s32[4096]{0:T(1024)S(4)} %get-tuple-element.39.slots, f32[2320,128]{1,0:T(8,128)S(1)} %get-tuple-element.54.field, f32[12304,128]{1,0:T(8,128)S(1)} %get-tuple-element.45.weight, ...), custom_call_target="tpu_custom_call", output_to_operand_aliasing={{0}: (5, {})} | custom-call | flops 2147483648 | bytes 16777216 | tf_op jit(solution)/shard_map/second_sweep/pallas_call | solution.py:473
  25.3 0.0 collective-permute-done.4.from_far
  25.3 0.0 collective-permute-done.5.from_near
  25.3 0.0 copy-start
  25.4 0.0 copy-start.1
  25.4 0.0 copy-start.2
  25.4 0.4 %last_sweep_edges.1 = (f32[32,512]{1,0:T(8,128)S(1)}, f32[32,512]{1,0:T(8,128)S(1)}) custom-call(f32[128,128]{1,0:T(8,128)S(1)} %collective-permute-done.4.from_far, f32[128,128]{1,0:T(8,128)S(1)} %collective-permute-done.5.from_near, bf16[1152,512]{1,0:T(8,128)(2,1)S(1)} %get-tuple-element.52.pick, f32[96,512]{1,0:T(8,128)S(1)} %get-tuple-element.53.plane_weight, ...), custom_call_target="tpu_custom_call" | custom-call | tf_op jit(solution)/shard_map/last_sweep_edges/pallas_call | solution.py:487
  25.8 6.1 %collective-permute-start.6 = (f32[32,512]{1,0:T(8,128)S(1)}, f32[32,512]{1,0:T(8,128)S(1)}, u32[]{:S(2)}, u32[]{:S(2)}) collective-permute-start(f32[32,512]{1,0:T(8,128)S(1)} %get-tuple-element.58), channel_id=1, source_target_pairs={{1,2},{2,1},{3,0},{0,3},{5,6},{6,5},{7,4},{4,7},{9,10},{10,9},{11,... | collective-permute-start | bytes 196616 | tf_op jit(solution)/shard_map/ppermute | solution.py:388
  31.9 0.0 collective-permute-start.7
  31.9 0.0 copy-done
  31.9 0.0 copy-done.1
  31.9 0.0 copy-done.2
  31.9 2.8 %inner_planes.1 = (f32[512,512]{1,0:T(8,128)}, f32[4,32,512]{2,1,0:T(8,128)S(1)}) custom-call(f32[128,128]{1,0:T(8,128)S(1)} %collective-permute-done.4.from_far, f32[128,128]{1,0:T(8,128)S(1)} %collective-permute-done.5.from_near, bf16[1152,512]{1,0:T(8,128)(2,1)S(1)} %get-tuple-element.52.pick, f32[96,512]{1,0:T(8,128)S(1)} %get-tuple-element.53.plane_weight, ...), custom_call_target="tpu_custom_call" | custom-call | flops 268435456 | bytes 2097152 | tf_op jit(solution)/shard_map/inner_planes/pallas_call | solution.py:497
  34.7 0.0 collective-permute-done.6.from_far
  34.7 0.0 collective-permute-done.7.from_near
  34.8 0.8 %edge_planes.1 = f32[512,512]{1,0:T(8,128)} custom-call(f32[4,32,512]{2,1,0:T(8,128)S(1)} %get-tuple-element.57.ends, f32[32,512]{1,0:T(8,128)S(1)} %collective-permute-done.6.from_far, f32[32,512]{1,0:T(8,128)S(1)} %collective-permute-done.7.from_near, f32[32,512]{1,0:T(8,128)S(1)} %copy-done, ...), custom_call_target="tpu_custom_call", output_to_operand_aliasing={{}: (6, {})} | custom-call | tf_op jit(solution)/shard_map/edge_planes/pallas_call | solution.py:511
Async XLA Ops:
  1.7 7.7 %collective-permute-start = (f32[128,128]{1,0:T(8,128)S(1)}, f32[128,128]{1,0:T(8,128)S(1)}, u32[]{:S(2)}, u32[]{:S(2)}) collective-permute-start(f32[128,128]{1,0:T(8,128)S(1)} %get-tuple-element.40), channel_id=1, source_target_pairs={{4,8},{8,4},{12,16},{16,12},{20,24},{24,20},{28,32},{32,28},{36,40... | collective-permute-start | bytes 196616 | tf_op jit(solution)/shard_map/ppermute | solution.py:382
  5.0 4.4 %collective-permute-start.1 = (f32[128,128]{1,0:T(8,128)S(1)}, f32[128,128]{1,0:T(8,128)S(1)}, u32[]{:S(2)}, u32[]{:S(2)}) collective-permute-start(f32[128,128]{1,0:T(8,128)S(1)} %get-tuple-element.41), channel_id=1, source_target_pairs={{0,4},{4,0},{8,12},{12,8},{16,20},{20,16},{24,28},{28,24},{32,36},... | collective-permute-start | bytes 196616 | tf_op jit(solution)/shard_map/ppermute | solution.py:393
  9.7 7.4 %collective-permute-start.2 = (f32[128,128]{1,0:T(8,128)S(1)}, f32[128,128]{1,0:T(8,128)S(1)}, u32[]{:S(2)}, u32[]{:S(2)}) collective-permute-start(f32[128,128]{1,0:T(8,128)S(1)} %get-tuple-element.48), channel_id=1, source_target_pairs={{4,8},{8,4},{12,16},{16,12},{20,24},{24,20},{28,32},{32,28},{36,40... | collective-permute-start | bytes 196616 | tf_op jit(solution)/shard_map/ppermute | solution.py:382
  12.7 4.4 %collective-permute-start.3 = (f32[128,128]{1,0:T(8,128)S(1)}, f32[128,128]{1,0:T(8,128)S(1)}, u32[]{:S(2)}, u32[]{:S(2)}) collective-permute-start(f32[128,128]{1,0:T(8,128)S(1)} %get-tuple-element.49), channel_id=1, source_target_pairs={{0,4},{4,0},{8,12},{12,8},{16,20},{20,16},{24,28},{28,24},{32,36},... | collective-permute-start | bytes 196616 | tf_op jit(solution)/shard_map/ppermute | solution.py:393
  17.5 7.9 %collective-permute-start.4 = (f32[128,128]{1,0:T(8,128)S(1)}, f32[128,128]{1,0:T(8,128)S(1)}, u32[]{:S(2)}, u32[]{:S(2)}) collective-permute-start(f32[128,128]{1,0:T(8,128)S(1)} %get-tuple-element.50), channel_id=1, source_target_pairs={{4,8},{8,4},{12,16},{16,12},{20,24},{24,20},{28,32},{32,28},{36,40... | collective-permute-start | bytes 196616 | tf_op jit(solution)/shard_map/ppermute | solution.py:382
  20.5 4.8 %collective-permute-start.5 = (f32[128,128]{1,0:T(8,128)S(1)}, f32[128,128]{1,0:T(8,128)S(1)}, u32[]{:S(2)}, u32[]{:S(2)}) collective-permute-start(f32[128,128]{1,0:T(8,128)S(1)} %get-tuple-element.51), channel_id=1, source_target_pairs={{0,4},{4,0},{8,12},{12,8},{16,20},{20,16},{24,28},{28,24},{32,36},... | collective-permute-start | bytes 196616 | tf_op jit(solution)/shard_map/ppermute | solution.py:393
  25.3 6.6 %copy-start = (f32[32,512]{1,0:T(8,128)S(1)}, f32[32,512]{1,0:T(8,128)}, u32[]{:S(2)}) copy-start(f32[32,512]{1,0:T(8,128)} %rate.3) | copy-start | bytes 196612
  25.4 6.6 %copy-start.1 = (f32[32,512]{1,0:T(8,128)S(1)}, f32[32,512]{1,0:T(8,128)}, u32[]{:S(2)}) copy-start(f32[32,512]{1,0:T(8,128)} %shift.3) | copy-start | bytes 196612
  25.4 6.6 %copy-start.2 = (f32[512]{0:T(512)S(1)}, f32[512]{0:T(512)}, u32[]{:S(2)}) copy-start(f32[512]{0:T(512)} %param.14) | copy-start | bytes 6148
  25.8 8.9 %collective-permute-start.6 = (f32[32,512]{1,0:T(8,128)S(1)}, f32[32,512]{1,0:T(8,128)S(1)}, u32[]{:S(2)}, u32[]{:S(2)}) collective-permute-start(f32[32,512]{1,0:T(8,128)S(1)} %get-tuple-element.58), channel_id=1, source_target_pairs={{1,2},{2,1},{3,0},{0,3},{5,6},{6,5},{7,4},{4,7},{9,10},{10,9},{11,... | collective-permute-start | bytes 196616 | tf_op jit(solution)/shard_map/ppermute | solution.py:388
  31.9 2.8 %collective-permute-start.7 = (f32[32,512]{1,0:T(8,128)S(1)}, f32[32,512]{1,0:T(8,128)S(1)}, u32[]{:S(2)}, u32[]{:S(2)}) collective-permute-start(f32[32,512]{1,0:T(8,128)S(1)} %get-tuple-element.59), channel_id=1, source_target_pairs={{0,1},{1,0},{2,3},{3,2},{4,5},{5,4},{6,7},{7,6},{8,9},{9,8},{10,11... | collective-permute-start | bytes 196616 | tf_op jit(solution)/shard_map/ppermute | solution.py:393

commit v8 on v7

--- a/solution.py
+++ b/solution.py
@@ -216,7 +216,7 @@
         out[pl.ds(offset + row, 8), :] = total
         return carry
 
-    lax.fori_loop(0, nodes // 2, step, 0, unroll=GROUP)
+    lax.fori_loop(0, nodes // 2, step, 0, unroll=2 * GROUP)
 
 
 def listed_pairs(order, slots, field, weight, base, out, first, until):

time: 35.8 us -> 35.8 us (level)
  no operation moved by 1% of the time
where the time goes in v8:
time: 35.8 us; the launch traced here: 35.6 us
  Pallas kernels  19.5 us (54%)
  starting transfers between devices  15.3 us (43%)
  waiting for transfers between devices  0.63 us (2%)
    ppermute x3, starting transfers between devices, swap_far_parts(): return lax.ppermute(array, ('dom', 'dir'), pairs)  9.35 us
    ppermute x1, starting transfers between devices, swap_far_sectors(): return lax.ppermute(array, 'dir', pairs)  5.95 us
    pallas_call x1, Pallas kernels, shards(): pl.pallas_call(second_body, out_shape=(fields, jax.ShapeDtypeStruct((colu...  4.97 us
    pallas_call x1, Pallas kernels, shards(): pl.pallas_call(weights_body, out_shape=(weights, bases, jax.ShapeDtypeStr...  4.36 us
    pallas_call x1, Pallas kernels, shards(): pl.pallas_call(first_body, out_shape=(fields, fields), in_specs=[SMEM, SM...  3.79 us
    pallas_call x1, Pallas kernels, shards(): pl.pallas_call(inner_body, out_shape=(plane_shape, jax.ShapeDtypeStruct((...  2.79 us
    pallas_call x1, Pallas kernels, shards(): pl.pallas_call(rows_body, out_shape=(fields, shares, shares, edges, edges...  1.66 us
    pallas_call x1, Pallas kernels, shards(): pl.pallas_call(edge_body, out_shape=plane_shape, in_specs=[VMEM] * 6 + [A...  0.82 us
  transfers between devices with their start and end apart: 8, of which 1 were waited for; matrix products, arithmetic and copies ran while one was open for 0% of the time, Pallas kernels for 45%

profile of v8, /device:TPU:129, one launch (start us, length us, event | category | flops | bytes accessed | tf_op | source)
XLA Modules:
  0.0 35.6 jit_solution(8122613491437760909)
XLA Ops:
  0.0 1.7 %rows.1 = (f32[2320,128]{1,0:T(8,128)S(1)}, f32[128,128]{1,0:T(8,128)S(1)}, f32[128,128]{1,0:T(8,128)S(1)}, f32[6,512]{1,0:T(8,128)S(1)}, f32[6,512]{1,0:T(8,128)S(1)}, /*index=5*/s32[32,128]{1,0:T(8,128)S(1)}) custom-call(s32[2,32]{1,0:T(2,128)} %send_hbm.3, f32[512,512]{1,0:T(8,128)} %bitcast.5, f32[6,512]{1,0:T(8,128)} %angle_hbm.1, f32[6,512]{1,0:T(8,128)} %speed_hbm.1, ...), custom_call_target="tpu_custom_call" | custom-call | tf_op jit(solution)/shard_map/rows/pallas_call | solution.py:410
  1.7 3.3 %collective-permute-start = (f32[128,128]{1,0:T(8,128)S(1)}, f32[128,128]{1,0:T(8,128)S(1)}, u32[]{:S(2)}, u32[]{:S(2)}) collective-permute-start(f32[128,128]{1,0:T(8,128)S(1)} %get-tuple-element.40), channel_id=1, source_target_pairs={{4,8},{8,4},{12,16},{16,12},{20,24},{24,20},{28,32},{32,28},{36,40... | collective-permute-start | bytes 196616 | tf_op jit(solution)/shard_map/ppermute | solution.py:382
  5.0 0.0 collective-permute-start.1
  5.0 4.4 %weights.1 = (f32[12304,128]{1,0:T(8,128)S(1)}, f32[2064,128]{1,0:T(8,128)S(1)}, f32[1536,128]{1,0:T(8,128)S(1)}, f32[256,128]{1,0:T(8,128)S(1)}, f32[96,512]{1,...) custom-call(s32[2,32]{1,0:T(2,128)} %send_hbm.3, ...), custom_call_target="tpu_custom_call" | custom-call | flops 1073741824 | bytes 8388608 | tf_op jit(solution)/shard_map/weights/pallas_call | solution.py:426
  9.3 0.0 collective-permute-done.from_far
  9.3 0.0 collective-permute-done.1.from_near
  9.4 0.3 shared.2
  9.7 3.0 %collective-permute-start.2 = (f32[128,128]{1,0:T(8,128)S(1)}, f32[128,128]{1,0:T(8,128)S(1)}, u32[]{:S(2)}, u32[]{:S(2)}) collective-permute-start(f32[128,128]{1,0:T(8,128)S(1)} %get-tuple-element.48), channel_id=1, source_target_pairs={{4,8},{8,4},{12,16},{16,12},{20,24},{24,20},{28,32},{32,28},{36,40... | collective-permute-start | bytes 196616 | tf_op jit(solution)/shard_map/ppermute | solution.py:382
  12.7 0.0 collective-permute-start.3
  12.7 3.8 %first_sweep.1 = (f32[2320,128]{1,0:T(8,128)S(1)}, f32[2320,128]{1,0:T(8,128)S(1)}) custom-call(s32[264]{0:T(512)S(4)} %get-tuple-element.38.order, s32[4096]{0:T(1024)S(4)} %get-tuple-element.39.slots, f32[2320,128]{1,0:T(8,128)S(1)} %get-tuple-element.44.field, f32[12304,128]{1,0:T(8,128)S(1)} %get-tuple-element.45.weight, ...), custom_call_target="tpu_custom_call" | custom-call | flops 1073741824 | bytes 8388608 | tf_op jit(solution)/shard_map/first_sweep/pallas_call | solution.py:463
  16.5 0.6 %collective-permute-done.2.from_far = f32[128,128]{1,0:T(8,128)S(1)} collective-permute-done((f32[128,128]{1,0:T(8,128)S(1)}, f32[128,128]{1,0:T(8,128)S(1)}, u32[]{:S(2)}, u32[]{:S(2)}) %collective-permute-start.2) | collective-permute-done | bytes 65568 | tf_op jit(solution)/shard_map/ppermute | solution.py:382
  17.1 0.0 collective-permute-done.3.from_near
  17.1 0.3 shared.3
  17.5 3.0 %collective-permute-start.4 = (f32[128,128]{1,0:T(8,128)S(1)}, f32[128,128]{1,0:T(8,128)S(1)}, u32[]{:S(2)}, u32[]{:S(2)}) collective-permute-start(f32[128,128]{1,0:T(8,128)S(1)} %get-tuple-element.50), channel_id=1, source_target_pairs={{4,8},{8,4},{12,16},{16,12},{20,24},{24,20},{28,32},{32,28},{36,40... | collective-permute-start | bytes 196616 | tf_op jit(solution)/shard_map/ppermute | solution.py:382
  20.5 0.0 collective-permute-start.5
  20.5 5.0 %second_sweep.1 = (f32[2320,128]{1,0:T(8,128)S(1)}, f32[512,512]{1,0:T(8,128)S(1)}) custom-call(s32[264]{0:T(512)S(4)} %get-tuple-element.38.order, s32[4096]{0:T(1024)S(4)} %get-tuple-element.39.slots, f32[2320,128]{1,0:T(8,128)S(1)} %get-tuple-element.54.field, f32[12304,128]{1,0:T(8,128)S(1)} %get-tuple-element.45.weight, ...), custom_call_target="tpu_custom_call", output_to_operand_aliasing={{0}: (5, {})} | custom-call | flops 2147483648 | bytes 16777216 | tf_op jit(solution)/shard_map/second_sweep/pallas_call | solution.py:473
  25.5 0.0 collective-permute-done.4.from_far
  25.5 0.0 collective-permute-done.5.from_near
  25.5 0.0 copy-start
  25.5 0.0 copy-start.1
  25.5 0.0 copy-start.2
  25.5 0.4 %last_sweep_edges.1 = (f32[32,512]{1,0:T(8,128)S(1)}, f32[32,512]{1,0:T(8,128)S(1)}) custom-call(f32[128,128]{1,0:T(8,128)S(1)} %collective-permute-done.4.from_far, f32[128,128]{1,0:T(8,128)S(1)} %collective-permute-done.5.from_near, bf16[1152,512]{1,0:T(8,128)(2,1)S(1)} %get-tuple-element.52.pick, f32[96,512]{1,0:T(8,128)S(1)} %get-tuple-element.53.plane_weight, ...), custom_call_target="tpu_custom_call" | custom-call | tf_op jit(solution)/shard_map/last_sweep_edges/pallas_call | solution.py:487
  26.0 5.9 %collective-permute-start.6 = (f32[32,512]{1,0:T(8,128)S(1)}, f32[32,512]{1,0:T(8,128)S(1)}, u32[]{:S(2)}, u32[]{:S(2)}) collective-permute-start(f32[32,512]{1,0:T(8,128)S(1)} %get-tuple-element.58), channel_id=1, source_target_pairs={{1,2},{2,1},{3,0},{0,3},{5,6},{6,5},{7,4},{4,7},{9,10},{10,9},{11,... | collective-permute-start | bytes 196616 | tf_op jit(solution)/shard_map/ppermute | solution.py:388
  31.9 0.0 collective-permute-start.7
  31.9 0.0 copy-done
  31.9 0.0 copy-done.1
  31.9 0.0 copy-done.2
  31.9 2.8 %inner_planes.1 = (f32[512,512]{1,0:T(8,128)}, f32[4,32,512]{2,1,0:T(8,128)S(1)}) custom-call(f32[128,128]{1,0:T(8,128)S(1)} %collective-permute-done.4.from_far, f32[128,128]{1,0:T(8,128)S(1)} %collective-permute-done.5.from_near, bf16[1152,512]{1,0:T(8,128)(2,1)S(1)} %get-tuple-element.52.pick, f32[96,512]{1,0:T(8,128)S(1)} %get-tuple-element.53.plane_weight, ...), custom_call_target="tpu_custom_call" | custom-call | flops 268435456 | bytes 2097152 | tf_op jit(solution)/shard_map/inner_planes/pallas_call | solution.py:497
  34.7 0.0 collective-permute-done.6.from_far
  34.8 0.0 collective-permute-done.7.from_near
  34.8 0.8 %edge_planes.1 = f32[512,512]{1,0:T(8,128)} custom-call(f32[4,32,512]{2,1,0:T(8,128)S(1)} %get-tuple-element.57.ends, f32[32,512]{1,0:T(8,128)S(1)} %collective-permute-done.6.from_far, f32[32,512]{1,0:T(8,128)S(1)} %collective-permute-done.7.from_near, f32[32,512]{1,0:T(8,128)S(1)} %copy-done, ...), custom_call_target="tpu_custom_call", output_to_operand_aliasing={{}: (6, {})} | custom-call | tf_op jit(solution)/shard_map/edge_planes/pallas_call | solution.py:511
Async XLA Ops:
  1.7 7.7 %collective-permute-start = (f32[128,128]{1,0:T(8,128)S(1)}, f32[128,128]{1,0:T(8,128)S(1)}, u32[]{:S(2)}, u32[]{:S(2)}) collective-permute-start(f32[128,128]{1,0:T(8,128)S(1)} %get-tuple-element.40), channel_id=1, source_target_pairs={{4,8},{8,4},{12,16},{16,12},{20,24},{24,20},{28,32},{32,28},{36,40... | collective-permute-start | bytes 196616 | tf_op jit(solution)/shard_map/ppermute | solution.py:382
  5.0 4.4 %collective-permute-start.1 = (f32[128,128]{1,0:T(8,128)S(1)}, f32[128,128]{1,0:T(8,128)S(1)}, u32[]{:S(2)}, u32[]{:S(2)}) collective-permute-start(f32[128,128]{1,0:T(8,128)S(1)} %get-tuple-element.41), channel_id=1, source_target_pairs={{0,4},{4,0},{8,12},{12,8},{16,20},{20,16},{24,28},{28,24},{32,36},... | collective-permute-start | bytes 196616 | tf_op jit(solution)/shard_map/ppermute | solution.py:393
  9.7 7.4 %collective-permute-start.2 = (f32[128,128]{1,0:T(8,128)S(1)}, f32[128,128]{1,0:T(8,128)S(1)}, u32[]{:S(2)}, u32[]{:S(2)}) collective-permute-start(f32[128,128]{1,0:T(8,128)S(1)} %get-tuple-element.48), channel_id=1, source_target_pairs={{4,8},{8,4},{12,16},{16,12},{20,24},{24,20},{28,32},{32,28},{36,40... | collective-permute-start | bytes 196616 | tf_op jit(solution)/shard_map/ppermute | solution.py:382
  12.7 4.4 %collective-permute-start.3 = (f32[128,128]{1,0:T(8,128)S(1)}, f32[128,128]{1,0:T(8,128)S(1)}, u32[]{:S(2)}, u32[]{:S(2)}) collective-permute-start(f32[128,128]{1,0:T(8,128)S(1)} %get-tuple-element.49), channel_id=1, source_target_pairs={{0,4},{4,0},{8,12},{12,8},{16,20},{20,16},{24,28},{28,24},{32,36},... | collective-permute-start | bytes 196616 | tf_op jit(solution)/shard_map/ppermute | solution.py:393
  17.5 8.0 %collective-permute-start.4 = (f32[128,128]{1,0:T(8,128)S(1)}, f32[128,128]{1,0:T(8,128)S(1)}, u32[]{:S(2)}, u32[]{:S(2)}) collective-permute-start(f32[128,128]{1,0:T(8,128)S(1)} %get-tuple-element.50), channel_id=1, source_target_pairs={{4,8},{8,4},{12,16},{16,12},{20,24},{24,20},{28,32},{32,28},{36,40... | collective-permute-start | bytes 196616 | tf_op jit(solution)/shard_map/ppermute | solution.py:382
  20.5 5.0 %collective-permute-start.5 = (f32[128,128]{1,0:T(8,128)S(1)}, f32[128,128]{1,0:T(8,128)S(1)}, u32[]{:S(2)}, u32[]{:S(2)}) collective-permute-start(f32[128,128]{1,0:T(8,128)S(1)} %get-tuple-element.51), channel_id=1, source_target_pairs={{0,4},{4,0},{8,12},{12,8},{16,20},{20,16},{24,28},{28,24},{32,36},... | collective-permute-start | bytes 196616 | tf_op jit(solution)/shard_map/ppermute | solution.py:393
  25.5 6.4 %copy-start = (f32[32,512]{1,0:T(8,128)S(1)}, f32[32,512]{1,0:T(8,128)}, u32[]{:S(2)}) copy-start(f32[32,512]{1,0:T(8,128)} %rate.3) | copy-start | bytes 196612
  25.5 6.4 %copy-start.1 = (f32[32,512]{1,0:T(8,128)S(1)}, f32[32,512]{1,0:T(8,128)}, u32[]{:S(2)}) copy-start(f32[32,512]{1,0:T(8,128)} %shift.3) | copy-start | bytes 196612
  25.5 6.4 %copy-start.2 = (f32[512]{0:T(512)S(1)}, f32[512]{0:T(512)}, u32[]{:S(2)}) copy-start(f32[512]{0:T(512)} %param.14) | copy-start | bytes 6148
  26.0 8.8 %collective-permute-start.6 = (f32[32,512]{1,0:T(8,128)S(1)}, f32[32,512]{1,0:T(8,128)S(1)}, u32[]{:S(2)}, u32[]{:S(2)}) collective-permute-start(f32[32,512]{1,0:T(8,128)S(1)} %get-tuple-element.58), channel_id=1, source_target_pairs={{1,2},{2,1},{3,0},{0,3},{5,6},{6,5},{7,4},{4,7},{9,10},{10,9},{11,... | collective-permute-start | bytes 196616 | tf_op jit(solution)/shard_map/ppermute | solution.py:388
  31.9 2.8 %collective-permute-start.7 = (f32[32,512]{1,0:T(8,128)S(1)}, f32[32,512]{1,0:T(8,128)S(1)}, u32[]{:S(2)}, u32[]{:S(2)}) collective-permute-start(f32[32,512]{1,0:T(8,128)S(1)} %get-tuple-element.59), channel_id=1, source_target_pairs={{0,1},{1,0},{2,3},{3,2},{4,5},{5,4},{6,7},{7,6},{8,9},{9,8},{10,11... | collective-permute-start | bytes 196616 | tf_op jit(solution)/shard_map/ppermute | solution.py:393
